TPU v7x, 256 devices: a whole 4x4x8 slice. The times are simulated.
256 devices in a mesh: node: 16 (over x, y), tile: 16 (over z, core).
Axes of the slice: x: 4, y: 4, z: 8, core: 2. Of those that a mesh axis runs over, the one named last changes fastest.
Arguments:
- schur: float32 [16, 1536, 24576], P(None, 'tile', 'node'), may hold values from -0.0390625 to 0.0390625
- samples: float32 [16, 1536, 512], P(None, 'tile'), may hold values from -6 to 6
Outputs:
- leaf_basis: float32 [16, 1536, 512], P('node', 'tile')
- level_one: float32 [16, 512, 512], P('node', 'tile')
- level_two: float32 [16, 512, 512], P('node', 'tile')
All inputs are finite; a program needn't handle non-finite values.
Results may differ from a plain program's by a relative error of at most 0.00011.
Values sent between devices are 32-bit elements; how exact they have to be, the bound alone decides.
A program may use at most 128 MiB of HBM per device.

v0:
```python
import math

import jax
import jax.numpy as jnp
from jax import lax
from jax.sharding import PartitionSpec as P

HIGH = lax.Precision.HIGHEST


def from_partner(block, axis, bit):
    count = lax.axis_size(axis)
    route = []
    for low in range(count):
        high = low | 1 << bit
        if high != low and high < count:
            route += [(low, high), (high, low)]
    return lax.ppermute(block, axis, route)


def product(left, right):
    return jnp.dot(left, right, precision=HIGH, preferred_element_type=jnp.float32)


def transposed(left, right):
    return lax.dot_general(
        left, right, (((0,), (0,)), ((), ())), precision=HIGH, preferred_element_type=jnp.float32
    )


def solve_right(factor, rows):
    return jax.scipy.linalg.solve_triangular(factor, rows.T, lower=True).T


def on_device(schur, samples):
    leaves, slice_cols, leaf_rows = schur.shape
    rank_size = samples.shape[2]
    node = lax.axis_index("node")
    tile = lax.axis_index("tile")
    tile_count = lax.axis_size("tile")
    owned = lax.dynamic_index_in_dim(samples, node, 0, keepdims=False)
    keep = (jnp.arange(leaves, dtype=jnp.int32) != node)[:, None, None]
    masked = jnp.where(keep, samples, 0.0).reshape(leaves * slice_cols, rank_size)
    stacked = schur.reshape(leaves * slice_cols, leaf_rows)
    sample_rows = lax.psum_scatter(
        transposed(stacked, masked), "tile", scatter_dimension=0, tiled=True
    )
    gram_part = transposed(sample_rows, sample_rows)
    gram = lax.psum(gram_part, "tile")
    factor = jnp.linalg.cholesky(gram)
    basis_rows = solve_right(factor, sample_rows)
    reduced = lax.psum(transposed(basis_rows, owned), "tile")

    def coupling(targets, panels):
        pieces = [lax.dynamic_index_in_dim(schur, target, 0, keepdims=False) for target in targets]
        total = None
        for piece, panel in zip(pieces, panels):
            term = transposed(piece, panel)
            total = term if total is None else total + term
        summed_rows = lax.psum_scatter(total, "tile", scatter_dimension=0, tiled=True)
        return lax.psum(transposed(basis_rows, summed_rows), "tile")

    out_rows = rank_size // tile_count
    panel_one = product(basis_rows, reduced)
    sibling_rows = from_partner(panel_one, "node", 0)
    near = coupling([jnp.bitwise_xor(node, 1)], [sibling_rows])
    parent_sample = factor.T - near
    other_sample, other_reduced = from_partner((parent_sample, reduced), "node", 0)
    parent_factor = jnp.linalg.cholesky(
        transposed(parent_sample, parent_sample) + transposed(other_sample, other_sample)
    )
    transfer_own = solve_right(parent_factor, parent_sample)
    transfer_other = solve_right(parent_factor, other_sample)
    parent_reduced = transposed(transfer_own, reduced) + transposed(transfer_other, other_reduced)
    panel_two = product(basis_rows, product(transfer_own, parent_reduced))
    cousin_rows = from_partner(panel_two, "node", 1)
    further_rows = from_partner(cousin_rows, "node", 0)
    far_sum = coupling(
        [jnp.bitwise_xor(node, 2), jnp.bitwise_xor(node, 3)], [cousin_rows, further_rows]
    )
    far_share = transposed(transfer_own, far_sum)
    partner_share = from_partner(far_share, "node", 0)
    grand_sample = parent_factor.T - (far_share + partner_share)
    cousin_grand = from_partner(grand_sample, "node", 1)
    grand_factor = jnp.linalg.cholesky(
        transposed(grand_sample, grand_sample) + transposed(cousin_grand, cousin_grand)
    )
    grand_transfer = solve_right(grand_factor, grand_sample)
    leaf_out = (basis_rows * math.sqrt(leaf_rows))[None]
    one_rows = lax.dynamic_slice_in_dim(transfer_own, tile * out_rows, out_rows, 0)
    level_one = (one_rows * math.sqrt(2 * rank_size))[None]
    two_rows = product(one_rows, grand_transfer)
    level_two = (two_rows * (2.0 * math.sqrt(rank_size)))[None]
    return (leaf_out, level_one, level_two)


def solution(mesh):
    placed = (P(None, "tile", "node"), P(None, "tile", None))
    return jax.shard_map(
        on_device,
        mesh=mesh,
        in_specs=placed,
        out_specs=(P("node", "tile", None), P("node", "tile", None), P("node", "tile", None)),
        check_vma=False,
    )
```

profile of v0, /device:TPU:1, one launch (start us, length us, event | category | flops | bytes accessed | tf_op | source)
XLA Modules:
  0.0 1252.0 jit_solution(2897463930405128078)
XLA Ops:
  7.2 20.2 %convolution_bitcast_fusion = f32[1536,512]{0,1:T(8,128)} fusion(f32[16,96,1536]{2,1,0:T(8,128)} %param.5, f32[16,96,512]{2,1,0:T(8,128)} %param.6, pred[16]{0:T(512)(128)(4,1)S(1)} %iota_compare_fusion.3), kind=kOutput, calls=%fused_computation.7 | convolution fusion | flops 14496301056 | bytes 15728656 | tf_op jit(solution)/shard_map/dot_general | solution.py:26
  31.1 61.9 %reduce-scatter.10.cloned.1.call-done = f32[96,512]{1,0:T(8,128)} async-done(((f32[1536,512]{1,0:T(8,128)}), f32[96,512]{1,0:T(8,128)}) %reduce-scatter.10.cloned.1.call-update) | async-done | bytes 196624
  97.7 111.2 %all-reduce.6.cloned.1.call-done = f32[512,512]{0,1:T(8,128)} async-done(((f32[512,512]{0,1:T(8,128)}), f32[512,512]{0,1:T(8,128)}) %all-reduce.6.cloned.1.call-update) | async-done | bytes 1048592 | tf_op jit(solution)/shard_map/psum | solution.py:49
  212.0 11.7 cholesky.374
  234.3 11.7 cholesky.393
  246.1 9.9 custom-call.37
  256.7 11.7 cholesky.414
  279.6 11.7 cholesky.431
  303.5 39.3 %custom-call.27 = f32[4,128,128]{1,2,0:T(8,128)S(1)} custom-call(f32[4,128,128]{2,1,0:T(8,128)S(1)} %get-tuple-element.20), custom_call_target="InvertDiagBlocksLowerTriangular" | custom-call | tf_op jit(solution)/shard_map/jit(_solve_triangular)/triangular_solve | solution.py:32
  347.9 111.7 %all-reduce.8.cloned.1.call-done = f32[512,512]{1,0:T(8,128)} async-done(((f32[512,512]{1,0:T(8,128)}), f32[512,512]{1,0:T(8,128)}) %all-reduce.8.cloned.1.call-update) | async-done | bytes 1048592 | tf_op jit(solution)/shard_map/psum | solution.py:52
  472.7 58.6 %reduce-scatter.6.cloned.1.call-done = f32[96,512]{1,0:T(8,128)} async-done(((f32[1536,512]{1,0:T(8,128)}), f32[96,512]{1,0:T(8,128)}) %reduce-scatter.6.cloned.1.call-update) | async-done | bytes 196624 | tf_op jit(solution)/shard_map/reduce_scatter | solution.py:60
  534.2 112.8 %all-reduce.10.cloned.1.call-done = f32[512,512]{0,1:T(8,128)} async-done(((f32[512,512]{0,1:T(8,128)}), f32[512,512]{0,1:T(8,128)}) %all-reduce.10.cloned.1.call-update) | async-done | bytes 1048592 | tf_op jit(solution)/shard_map/psum | solution.py:61
  652.3 20.1 %collective-permute-done.1 = f32[512,512]{0,1:T(8,128)S(1)} collective-permute-done((f32[512,512]{0,1:T(8,128)S(1)}, f32[512,512]{0,1:T(8,128)S(1)}, u32[]{:S(2)}, u32[]{:S(2)}) %collective-permute-start.1) | collective-permute-done | bytes 1048608 | tf_op jit(solution)/shard_map/ppermute | solution.py:18
  678.0 11.7 cholesky.446
  689.9 9.8 custom-call.39
  702.9 13.3 %cholesky.465 = f32[128,128]{1,0:T(8,128)} custom-call(f32[128,128]{1,0:T(8,128)} %cholesky.603), custom_call_target="Cholesky" | custom-call | tf_op jit(solution)/shard_map/jit(cholesky)/cholesky | solution.py:69
  719.0 11.3 custom-call.40
  732.7 12.3 cholesky.486
  746.5 10.4 custom-call.41
  759.3 11.7 cholesky.503
  776.0 14.0 %while.8 = (s32[]{:T(128)}, f32[512,512]{1,0:T(8,128)}, s32[4,2]{0,1:T(2,128)S(1)}, f32[4,128,128]{2,1,0:T(8,128)}, s32[]{:T(128)}) while((s32[]{:T(128)}, f32[512,512]{1,0:T(8,128)}, s32[4,2]{0,1:T(2,128)S(1)}, f32[4,128,128]{2,1,0:T(8,128)}, s32[]{:T(128)}) %tuple.104), condition=%wide.while_cond, body=%wide.while_body.sunk | while | flops 2 | bytes 132705 | solution.py:32
  790.0 41.1 %custom-call.42 = f32[4,128,128]{1,2,0:T(8,128)} custom-call(f32[4,128,128]{2,1,0:T(8,128)} %get-tuple-element.33), custom_call_target="InvertDiagBlocksLowerTriangular" | custom-call | tf_op jit(solution)/shard_map/jit(_solve_triangular)/triangular_solve | solution.py:32
  867.8 62.0 %reduce-scatter.8.cloned.1.call-done = f32[96,512]{1,0:T(8,128)} async-done(((f32[1536,512]{1,0:T(8,128)}), f32[96,512]{1,0:T(8,128)}) %reduce-scatter.8.cloned.1.call-update) | async-done | bytes 196624 | tf_op jit(solution)/shard_map/reduce_scatter | solution.py:60
  932.7 113.0 %all-reduce.12.cloned.1.call-done = f32[512,512]{1,0:T(8,128)} async-done(((f32[512,512]{1,0:T(8,128)}), f32[512,512]{1,0:T(8,128)}) %all-reduce.12.cloned.1.call-update) | async-done | bytes 1048592 | tf_op jit(solution)/shard_map/psum | solution.py:61
  1050.2 22.6 %collective-permute-done.5 = f32[512,512]{0,1:T(8,128)S(1)} collective-permute-done((f32[512,512]{0,1:T(8,128)S(1)}, f32[512,512]{0,1:T(8,128)S(1)}, u32[]{:S(2)}, u32[]{:S(2)}) %collective-permute-start.5) | collective-permute-done | bytes 1048608 | tf_op jit(solution)/shard_map/ppermute | solution.py:18
  1078.8 19.0 %collective-permute-done.6 = f32[512,512]{0,1:T(8,128)S(1)} collective-permute-done((f32[512,512]{0,1:T(8,128)S(1)}, f32[512,512]{0,1:T(8,128)S(1)}, u32[]{:S(2)}, u32[]{:S(2)}) %collective-permute-start.6) | collective-permute-done | bytes 1048608 | tf_op jit(solution)/shard_map/ppermute | solution.py:18
  1103.2 11.7 cholesky.518
  1115.1 9.8 custom-call.44
  1127.4 12.1 cholesky.537
  1152.2 11.7 cholesky.558
  1176.0 11.7 cholesky.575
  1199.7 39.3 %custom-call.47 = f32[4,128,128]{1,2,0:T(8,128)S(1)} custom-call(f32[4,128,128]{2,1,0:T(8,128)S(1)} %get-tuple-element.35), custom_call_target="InvertDiagBlocksLowerTriangular" | custom-call | tf_op jit(solution)/shard_map/jit(_solve_triangular)/triangular_solve | solution.py:32
  (203 shorter events, 218.2 us)
Async XLA Ops:
  7.2 85.8 %reduce-scatter.10.cloned.1.call-start = ((), (), s32[]{:S(2)}) async-start(), calls=%async_computation.9 | async-start | bytes 3342336
  31.0 177.9 %all-reduce.6.cloned.1.call-start = ((), (), s32[]{:S(2)}) async-start(), calls=%async_computation.3 | async-start | bytes 2097152 | tf_op jit(solution)/shard_map/psum | solution.py:49
  96.1 363.5 %all-reduce.8.cloned.1.call-start = ((), (), s32[]{:S(2)}) async-start(), calls=%async_computation.4 | async-start | bytes 2097152 | tf_op jit(solution)/shard_map/psum | solution.py:52
  347.8 183.4 %reduce-scatter.6.cloned.1.call-start = ((), (), s32[]{:S(2)}) async-start(), calls=%async_computation.5 | async-start | bytes 3342336 | tf_op jit(solution)/shard_map/reduce_scatter | solution.py:60
  461.5 5.7 collective-permute-start
  472.6 174.4 %all-reduce.10.cloned.1.call-start = ((), (), s32[]{:S(2)}) async-start(), calls=%async_computation.6 | async-start | bytes 2097152 | tf_op jit(solution)/shard_map/psum | solution.py:61
  534.2 395.6 %reduce-scatter.8.cloned.1.call-start = ((), (), s32[]{:S(2)}) async-start(), calls=%async_computation.7 | async-start | bytes 3342336 | tf_op jit(solution)/shard_map/reduce_scatter | solution.py:60
  648.5 23.9 %collective-permute-start.1 = (f32[512,512]{0,1:T(8,128)S(1)}, f32[512,512]{0,1:T(8,128)S(1)}, u32[]{:S(2)}, u32[]{:S(2)}) collective-permute-start(f32[512,512]{0,1:T(8,128)S(1)} %bitcast_subtract_fusion.1), channel_id=1, source_target_pairs={{0,16},{16,0},{32,48},{48,32},{64,80},{80,64},{96,112},{112,96},{1... | collective-permute-start | bytes 3145736 | tf_op jit(solution)/shard_map/ppermute | solution.py:18
  649.8 194.9 %collective-permute-start.2 = (f32[512,512]{1,0:T(8,128)}, f32[512,512]{1,0:T(8,128)}, u32[]{:S(2)}, u32[]{:S(2)}) collective-permute-start(f32[512,512]{1,0:T(8,128)} %all-reduce.8.cloned.1.call-done), channel_id=1, source_target_pairs={{0,16},{16,0},{32,48},{48,32},{64,80},{80,64},{96,112},{112,96},{1... | collective-permute-start | bytes 3145736 | tf_op jit(solution)/shard_map/ppermute | solution.py:18
  672.4 163.9 %copy-start = (f32[512,512]{0,1:T(8,128)}, f32[512,512]{0,1:T(8,128)S(1)}, u32[]{:S(2)}) copy-start(f32[512,512]{0,1:T(8,128)S(1)} %collective-permute-done.1) | copy-start | bytes 3145732
  677.0 1.0 copy-start.3
  831.1 6.5 copy-start.6
  831.1 6.9 copy-start.1
  838.4 4.4 copy-start.2
  850.4 6.1 collective-permute-start.3
  856.5 5.7 collective-permute-start.4
  867.7 178.0 %all-reduce.12.cloned.1.call-start = ((), (), s32[]{:S(2)}) async-start(), calls=%async_computation.8 | async-start | bytes 2097152 | tf_op jit(solution)/shard_map/psum | solution.py:61
  1048.9 23.9 %collective-permute-start.5 = (f32[512,512]{0,1:T(8,128)S(1)}, f32[512,512]{0,1:T(8,128)S(1)}, u32[]{:S(2)}, u32[]{:S(2)}) collective-permute-start(f32[512,512]{0,1:T(8,128)S(1)} %fusion.163), channel_id=1, source_target_pairs={{0,16},{16,0},{32,48},{48,32},{64,80},{80,64},{96,112},{112,96},{1... | collective-permute-start | bytes 3145736 | tf_op jit(solution)/shard_map/ppermute | solution.py:18
  1073.1 24.7 %collective-permute-start.6 = (f32[512,512]{0,1:T(8,128)S(1)}, f32[512,512]{0,1:T(8,128)S(1)}, u32[]{:S(2)}, u32[]{:S(2)}) collective-permute-start(f32[512,512]{0,1:T(8,128)S(1)} %bitcast_subtract_fusion), channel_id=1, source_target_pairs={{0,32},{32,0},{16,48},{48,16},{64,96},{96,64},{80,112},{112,80},{1... | collective-permute-start | bytes 3145736 | tf_op jit(solution)/shard_map/ppermute | solution.py:18
  1076.9 1.0 copy-start.5
  1102.1 1.0 copy-start.4
Sparse Core Ops, SparseCore 0:
  31.2 61.8 reduce-scatter.9
  96.2 112.6 all-reduce.5
  347.9 111.5 all-reduce.7
  472.7 58.4 reduce-scatter.5
  534.3 112.6 all-reduce.9
  867.8 61.8 reduce-scatter.7
  932.9 112.8 all-reduce.11
where the time goes:
time: 1260 us; the launch traced here: 1250 us
  waiting for transfers between devices  701 us (56%)
  other arithmetic  371 us (29%)
  matrix products  101 us (8%)
  local copies, waits for them, and re-layouts  43.6 us (3%)
  between operations  22.8 us (2%)
    psum x2, waiting for transfers between devices, coupling(): return lax.psum(transposed(basis_rows, summed_rows), 'tile')  226 us
    another operation x8, other arithmetic, solve_right(): return jax.scipy.linalg.solve_triangular(factor, rows.T, lower=True).T  121 us
    reduce_scatter x2, waiting for transfers between devices, coupling(): lax.psum_scatter(total, 'tile', scatter_dimension=0, tiled=True)  121 us
    psum x1, waiting for transfers between devices, on_device(): reduced = lax.psum(transposed(basis_rows, owned), 'tile')  112 us
    psum x1, waiting for transfers between devices, on_device(): gram = lax.psum(gram_part, 'tile')  111 us
    another operation x15, other arithmetic, on_device(): jnp.linalg.cholesky(transposed(parent_sample, parent_sample) + transposed...  85.7 us
    another operation x15, other arithmetic, on_device(): jnp.linalg.cholesky(transposed(grand_sample, grand_sample) + transposed(c...  79.5 us
    another operation x14, other arithmetic, on_device(): factor = jnp.linalg.cholesky(gram)  78.5 us
  transfers between devices with their start and end apart: 14, of which 13 were waited for; matrix products, arithmetic and copies ran while one was open for 14% of the time, Pallas kernels for 0%

commit v1 on v0

v1 whole, which is shorter than its diff:
```python
import math

import jax
import jax.numpy as jnp
from jax import lax
from jax.sharding import PartitionSpec as P

HIGH = lax.Precision.HIGHEST


def swap(block, axis, mask):
    count = lax.axis_size(axis)
    return lax.ppermute(block, axis, [(low, low ^ mask) for low in range(count)])


def product(left, right):
    return jnp.dot(left, right, precision=HIGH, preferred_element_type=jnp.float32)


def transposed(left, right):
    return lax.dot_general(
        left, right, (((0,), (0,)), ((), ())), precision=HIGH, preferred_element_type=jnp.float32
    )


def inverse_lower(factor):
    eye = jnp.eye(factor.shape[0], dtype=factor.dtype)
    return jax.scipy.linalg.solve_triangular(factor, eye, lower=True)


def tile_bits():
    return [bit for bit in range(lax.axis_size("tile").bit_length() - 1)]


def halve(block):
    tile = lax.axis_index("tile")
    for bit in tile_bits():
        side = (tile >> bit) & 1
        half = block.shape[0] // 2
        keep = lax.dynamic_slice_in_dim(block, side * half, half, 0)
        send = lax.dynamic_slice_in_dim(block, (1 - side) * half, half, 0)
        block = keep + swap(send, "tile", 1 << bit)
    return block


def double(block, dim):
    tile = lax.axis_index("tile")
    for bit in reversed(tile_bits()):
        side = (tile >> bit) & 1
        other = swap(block, "tile", 1 << bit)
        block = jnp.where(
            side == 0,
            jnp.concatenate([block, other], axis=dim),
            jnp.concatenate([other, block], axis=dim),
        )
    return block


def chunk_rows(block, count):
    tile = lax.axis_index("tile")
    start = 0
    size = block.shape[0]
    for bit in tile_bits():
        size //= 2
        start = start + ((tile >> bit) & 1) * size
    return lax.dynamic_slice_in_dim(block, start, count, 0)


def on_device(schur, samples):
    leaves, slice_cols, leaf_rows = schur.shape
    rank_size = samples.shape[2]
    node = lax.axis_index("node")
    tile = lax.axis_index("tile")
    tile_count = lax.axis_size("tile")
    out_rows = rank_size // tile_count
    owned = lax.dynamic_index_in_dim(samples, node, 0, keepdims=False)
    keep = (jnp.arange(leaves, dtype=jnp.int32) != node)[:, None, None]
    masked = jnp.where(keep, samples, 0.0).reshape(leaves * slice_cols, rank_size)
    stacked = schur.reshape(leaves * slice_cols, leaf_rows)
    sample_rows = lax.psum_scatter(
        transposed(stacked, masked), "tile", scatter_dimension=0, tiled=True
    )
    both = lax.all_gather(
        jnp.concatenate([sample_rows, owned], axis=1), "tile", axis=0, tiled=True
    )
    local = both[:, :rank_size]
    omega = both[:, rank_size:]
    factor = jnp.linalg.cholesky(transposed(local, local))
    basis = product(local, inverse_lower(factor).T)
    reduced = transposed(basis, omega)
    basis_rows = lax.dynamic_slice_in_dim(basis, tile * slice_cols, slice_cols, 0)

    def meet(target):
        piece = lax.dynamic_index_in_dim(schur, target, 0, keepdims=False)
        return product(piece, basis)

    panel_one = product(basis_rows, reduced)
    sibling_rows = swap(panel_one, "node", 1)
    other_reduced = swap(reduced, "node", 1)
    near_meet = meet(jnp.bitwise_xor(node, 1))
    cousin_meet = meet(jnp.bitwise_xor(node, 2))
    further_meet = meet(jnp.bitwise_xor(node, 3))

    near_part = halve(transposed(near_meet, sibling_rows))
    sample_part = chunk_rows(factor.T, near_part.shape[0]) - near_part
    other_part = swap(sample_part, "node", 1)
    pair = double(jnp.stack([sample_part, other_part]), 1)
    parent_sample, other_sample = pair[0], pair[1]
    parent_factor = jnp.linalg.cholesky(
        transposed(parent_sample, parent_sample) + transposed(other_sample, other_sample)
    )
    parent_inverse = inverse_lower(parent_factor).T
    transfer_own = product(parent_sample, parent_inverse)
    transfer_other = product(other_sample, parent_inverse)
    parent_reduced = transposed(transfer_own, reduced) + transposed(transfer_other, other_reduced)
    panel_two = product(basis_rows, product(transfer_own, parent_reduced))
    cousin_rows = swap(panel_two, "node", 2)
    further_rows = swap(panel_two, "node", 3)
    far_sum = transposed(cousin_meet, cousin_rows) + transposed(further_meet, further_rows)
    far_part = halve(transposed(transfer_own, far_sum))
    far_pair = far_part + swap(far_part, "node", 1)
    grand_part = chunk_rows(parent_factor.T, far_pair.shape[0]) - far_pair
    cousin_part = swap(grand_part, "node", 2)
    grand_pair = double(jnp.stack([grand_part, cousin_part]), 1)
    grand_sample, cousin_grand = grand_pair[0], grand_pair[1]
    grand_factor = jnp.linalg.cholesky(
        transposed(grand_sample, grand_sample) + transposed(cousin_grand, cousin_grand)
    )
    grand_transfer = product(grand_sample, inverse_lower(grand_factor).T)
    leaf_out = (basis_rows * math.sqrt(leaf_rows))[None]
    one_rows = lax.dynamic_slice_in_dim(transfer_own, tile * out_rows, out_rows, 0)
    level_one = (one_rows * math.sqrt(2 * rank_size))[None]
    two_rows = product(one_rows, grand_transfer)
    level_two = (two_rows * (2.0 * math.sqrt(rank_size)))[None]
    return (leaf_out, level_one, level_two)


def solution(mesh):
    placed = (P(None, "tile", "node"), P(None, "tile", None))
    return jax.shard_map(
        on_device,
        mesh=mesh,
        in_specs=placed,
        out_specs=(P("node", "tile", None), P("node", "tile", None), P("node", "tile", None)),
        check_vma=False,
    )
```

time: 1260 us -> 906 us (0.72)
  waiting for transfers between devices: 701 us -> 276 us
  other arithmetic: 371 us -> 396 us
  local copies, waits for them, and re-layouts: 43.6 us -> 60.8 us
  matrix products: 101 us -> 118 us
  starting transfers between devices: 12.5 us -> 26.4 us
    psum x4 -> x0, waiting for transfers between devices: 449 us -> none  [the longest x2 226 us: coupling(): return lax.psum(transposed(basis_rows, summed_rows), 'tile')]
    reduce_scatter x2 -> x0, waiting for transfers between devices: 121 us -> none  [coupling(): lax.psum_scatter(total, 'tile', scatter_dimension=0, tiled=True)]
    ppermute x7 -> x23, waiting for transfers between devices: 70 us -> 167 us  [swap(): lax.ppermute(block, axis, [(low, low ^ mask) for low in range(count)])]
    all_gather x0 -> x1, waiting for transfers between devices: none -> 48 us  [on_device(): lax.all_gather(jnp.concatenate([sample_rows, owned], axis=1), 'tile', axi...]
    dot_general x4 -> x11, matrix products: 7.37 us -> 27.6 us  [product(): jnp.dot(left, right, precision=HIGH, preferred_element_type=jnp.float32)]
    ppermute x7 -> x23, starting transfers between devices: 11.8 us -> 26.1 us  [swap(): lax.ppermute(block, axis, [(low, low ^ mask) for low in range(count)])]
    dot_general x15 -> x13, matrix products: 62.2 us -> 50.4 us  [transposed(): lax.dot_general(left, right, (((0,), (0,)), ((), ())), precision=HIGH, pr...]
    another operation x41 -> x50, local copies, waits for them, and re-layouts: 30.4 us -> 37.2 us  [the longest x40 34.6 us: inverse_lower(): return jax.scipy.linalg.solve_triangular(factor, eye, lower=True)]
  transfers between devices with their start and end apart: 14 -> 25, of which waited for: 13 -> 23; matrix products, arithmetic and copies ran while one was open for 14% -> 22% of each run, Pallas kernels for 0% -> 0%
where the time goes in v1:
time: 906 us; the launch traced here: 901 us
  other arithmetic  396 us (44%)
  waiting for transfers between devices  276 us (30%)
  matrix products  118 us (13%)
  local copies, waits for them, and re-layouts  60.8 us (7%)
  starting transfers between devices  26.4 us (3%)
  between operations  23.1 us (3%)
    ppermute x23, waiting for transfers between devices, swap(): lax.ppermute(block, axis, [(low, low ^ mask) for low in range(count)])  167 us
    another operation x7, other arithmetic, inverse_lower(): return jax.scipy.linalg.solve_triangular(factor, eye, lower=True)  127 us
    another operation x15, other arithmetic, on_device(): jnp.linalg.cholesky(transposed(parent_sample, parent_sample) + transposed...  83.9 us
    another operation x15, other arithmetic, on_device(): jnp.linalg.cholesky(transposed(grand_sample, grand_sample) + transposed(c...  81.2 us
    another operation x14, other arithmetic, on_device(): factor = jnp.linalg.cholesky(transposed(local, local))  79 us
    unnamed x3, waiting for transfers between devices  60.7 us
    dot_general x13, matrix products, transposed(): lax.dot_general(left, right, (((0,), (0,)), ((), ())), precision=HIGH, pr...  50.4 us
    all_gather x1, waiting for transfers between devices, on_device(): lax.all_gather(jnp.concatenate([sample_rows, owned], axis=1), 'tile', axi...  48 us
  transfers between devices with their start and end apart: 25, of which 23 were waited for; matrix products, arithmetic and copies ran while one was open for 22% of the time, Pallas kernels for 0%

profile of v1, /device:TPU:1, one launch (start us, length us, event | category | flops | bytes accessed | tf_op | source)
XLA Modules:
  0.0 900.6 jit_solution(1732461360240981253)
XLA Ops:
  7.2 18.4 %convolution_bitcast_fusion = f32[1536,512]{0,1:T(8,128)S(1)} fusion(f32[16,96,1536]{2,1,0:T(8,128)} %param.5, f32[16,96,512]{2,1,0:T(8,128)} %param.6, pred[16]{0:T(512)(128)(4,1)S(1)} %iota_compare_fusion.4), kind=kOutput, calls=%fused_computation.6 | convolution fusion | flops 14496301056 | bytes 15728656 | tf_op jit(solution)/shard_map/dot_general | solution.py:21
  29.4 60.6 %reduce-scatter.4.cloned.1.call-done = f32[96,512]{1,0:T(8,128)} async-done(((f32[1536,512]{1,0:T(8,128)}), f32[96,512]{1,0:T(8,128)}) %reduce-scatter.4.cloned.1.call-update) | async-done | bytes 196624
  92.2 48.0 %all-gather.2.cloned.1.call-done = f32[1536,1024]{1,0:T(8,128)} async-done(((f32[96,1024]{1,0:T(8,128)}), f32[1536,1024]{1,0:T(8,128)}) %all-gather.2.cloned.1.call-update) | async-done | bytes 6291472 | tf_op jit(solution)/shard_map/all_gather | solution.py:83
  149.7 11.7 %cholesky.374 = f32[128,128]{1,0:T(8,128)S(1)} custom-call(f32[128,128]{1,0:T(8,128)S(1)} %cholesky.586), custom_call_target="Cholesky" | custom-call | tf_op jit(solution)/shard_map/jit(cholesky)/cholesky | solution.py:88
  161.5 10.0 %custom-call.31 = f32[1,128,128]{1,2,0:T(8,128)S(1)} custom-call(f32[1,128,128]{2,1,0:T(8,128)S(1)} %get-tuple-element.91), custom_call_target="InvertDiagBlocksLowerTriangular" | custom-call | tf_op jit(solution)/shard_map/jit(cholesky)/cholesky | solution.py:88
  174.5 11.7 %cholesky.393 = f32[128,128]{1,0:T(8,128)S(1)} custom-call(f32[128,128]{1,0:T(8,128)S(1)} %cholesky.590), custom_call_target="Cholesky" | custom-call | tf_op jit(solution)/shard_map/jit(cholesky)/cholesky | solution.py:88
  197.7 11.7 %cholesky.414 = f32[128,128]{1,0:T(8,128)S(1)} custom-call(f32[128,128]{1,0:T(8,128)S(1)} %cholesky.595), custom_call_target="Cholesky" | custom-call | tf_op jit(solution)/shard_map/jit(cholesky)/cholesky | solution.py:88
  210.1 10.2 %custom-call.33 = f32[1,128,128]{1,2,0:T(8,128)S(1)} custom-call(f32[1,128,128]{2,1,0:T(8,128)S(1)} %get-tuple-element.85), custom_call_target="InvertDiagBlocksLowerTriangular" | custom-call | tf_op jit(solution)/shard_map/jit(cholesky)/cholesky | solution.py:88
  221.7 11.7 %cholesky.431 = f32[128,128]{1,0:T(8,128)S(1)} custom-call(f32[128,128]{1,0:T(8,128)S(1)} %convolution_subtract_fusion.17), custom_call_target="Cholesky" | custom-call | tf_op jit(solution)/shard_map/jit(cholesky)/cholesky | solution.py:88
  246.7 39.5 %custom-call.34 = f32[4,128,128]{1,2,0:T(8,128)S(1)} custom-call(f32[4,128,128]{2,1,0:T(8,128)S(1)} %get-tuple-element.25), custom_call_target="InvertDiagBlocksLowerTriangular" | custom-call | tf_op jit(solution)/shard_map/jit(_solve_triangular)/triangular_solve | solution.py:28
  327.8 12.6 %collective-permute-done.3 = f32[64,512]{0,1:T(8,128)} collective-permute-done((f32[64,512]{0,1:T(8,128)S(1)}, f32[64,512]{0,1:T(8,128)}, u32[]{:S(2)}, u32[]{:S(2)}) %collective-permute-start.3) | collective-permute-done | bytes 131104 | tf_op jit(solution)/shard_map/ppermute | solution.py:13
  344.9 14.9 %collective-permute-done.4 = f32[32,512]{0,1:T(8,128)} collective-permute-done((f32[32,512]{0,1:T(8,128)}, f32[32,512]{0,1:T(8,128)}, u32[]{:S(2)}, u32[]{:S(2)}) %collective-permute-start.4) | collective-permute-done | bytes 65568 | tf_op jit(solution)/shard_map/ppermute | solution.py:13
  378.5 14.7 %collective-permute-done.7 = f32[2,64,512]{2,1,0:T(8,128)} collective-permute-done((f32[2,64,512]{2,1,0:T(8,128)S(1)}, f32[2,64,512]{2,1,0:T(8,128)}, u32[]{:S(2)}, u32[]{:S(2)}) %collective-permute-start.7) | collective-permute-done | bytes 262176 | tf_op jit(solution)/shard_map/ppermute | solution.py:13
  395.1 13.3 %collective-permute-done.8 = f32[2,128,512]{2,1,0:T(8,128)} collective-permute-done((f32[2,128,512]{2,1,0:T(8,128)}, f32[2,128,512]{2,1,0:T(8,128)}, u32[]{:S(2)}, u32[]{:S(2)}) %collective-permute-start.8) | collective-permute-done | bytes 524320 | tf_op jit(solution)/shard_map/ppermute | solution.py:13
  430.1 11.7 %cholesky.446 = f32[128,128]{1,0:T(8,128)S(1)} custom-call(f32[128,128]{1,0:T(8,128)S(1)} %cholesky.599), custom_call_target="Cholesky" | custom-call | tf_op jit(solution)/shard_map/jit(cholesky)/cholesky | solution.py:109
  442.4 10.6 %custom-call.35 = f32[1,128,128]{1,2,0:T(8,128)} custom-call(f32[1,128,128]{2,1,0:T(8,128)S(1)} %get-tuple-element.81), custom_call_target="InvertDiagBlocksLowerTriangular" | custom-call | tf_op jit(solution)/shard_map/jit(cholesky)/cholesky | solution.py:109
  458.6 11.7 %cholesky.465 = f32[128,128]{1,0:T(8,128)S(1)} custom-call(f32[128,128]{1,0:T(8,128)S(1)} %cholesky.603), custom_call_target="Cholesky" | custom-call | tf_op jit(solution)/shard_map/jit(cholesky)/cholesky | solution.py:109
  487.0 12.3 %cholesky.486 = f32[128,128]{1,0:T(8,128)} custom-call(f32[128,128]{1,0:T(8,128)S(1)} %cholesky.608), custom_call_target="Cholesky" | custom-call | tf_op jit(solution)/shard_map/jit(cholesky)/cholesky | solution.py:109
  501.5 10.6 %custom-call.37 = f32[1,128,128]{1,2,0:T(8,128)} custom-call(f32[1,128,128]{2,1,0:T(8,128)S(1)} %get-tuple-element.75), custom_call_target="InvertDiagBlocksLowerTriangular" | custom-call | tf_op jit(solution)/shard_map/jit(cholesky)/cholesky | solution.py:109
  515.2 11.7 %cholesky.503 = f32[128,128]{1,0:T(8,128)S(1)} custom-call(f32[128,128]{1,0:T(8,128)S(1)} %convolution_subtract_fusion.16), custom_call_target="Cholesky" | custom-call | tf_op jit(solution)/shard_map/jit(cholesky)/cholesky | solution.py:109
  534.4 14.0 %while.7 = (s32[]{:T(128)}, f32[512,512]{1,0:T(8,128)}, s32[4,2]{0,1:T(2,128)S(1)}, f32[4,128,128]{2,1,0:T(8,128)}, s32[]{:T(128)}) while((s32[]{:T(128)}, f32[512,512]{1,0:T(8,128)}, s32[4,2]{0,1:T(2,128)S(1)}, f32[4,128,128]{2,1,0:T(8,128)}, s32[]{:T(128)}) %tuple.89), condition=%wide.while_cond.clone, body=%wide.while_body.clone.sunk | while | flops 2 | bytes 132705 | solution.py:28
  548.3 41.1 %custom-call.38 = f32[4,128,128]{1,2,0:T(8,128)} custom-call(f32[4,128,128]{2,1,0:T(8,128)} %get-tuple-element.26), custom_call_target="InvertDiagBlocksLowerTriangular" | custom-call | tf_op jit(solution)/shard_map/jit(_solve_triangular)/triangular_solve | solution.py:28
  635.8 14.5 %collective-permute-done.15 = f32[64,512]{0,1:T(8,128)S(1)} collective-permute-done((f32[64,512]{0,1:T(8,128)S(1)}, f32[64,512]{0,1:T(8,128)S(1)}, u32[]{:S(2)}, u32[]{:S(2)}) %collective-permute-start.15) | collective-permute-done | bytes 131104 | tf_op jit(solution)/shard_map/ppermute | solution.py:13
  652.3 14.7 %collective-permute-done.16 = f32[32,512]{0,1:T(8,128)S(1)} collective-permute-done((f32[32,512]{0,1:T(8,128)S(1)}, f32[32,512]{0,1:T(8,128)S(1)}, u32[]{:S(2)}, u32[]{:S(2)}) %collective-permute-start.16) | collective-permute-done | bytes 65568 | tf_op jit(solution)/shard_map/ppermute | solution.py:13
  693.2 13.6 %collective-permute-done.20 = f32[2,64,512]{2,1,0:T(8,128)S(1)} collective-permute-done((f32[2,64,512]{2,1,0:T(8,128)S(1)}, f32[2,64,512]{2,1,0:T(8,128)S(1)}, u32[]{:S(2)}, u32[]{:S(2)}) %collective-permute-start.20) | collective-permute-done | bytes 262176 | tf_op jit(solution)/shard_map/ppermute | solution.py:13
  707.0 12.1 %collective-permute-done.21 = f32[2,128,512]{2,1,0:T(8,128)S(1)} collective-permute-done((f32[2,128,512]{2,1,0:T(8,128)S(1)}, f32[2,128,512]{2,1,0:T(8,128)S(1)}, u32[]{:S(2)}, u32[]{:S(2)}) %collective-permute-start.21) | collective-permute-done | bytes 524320 | tf_op jit(solution)/shard_map/ppermute | solution.py:13
  735.5 11.7 %cholesky.518 = f32[128,128]{1,0:T(8,128)S(1)} custom-call(f32[128,128]{1,0:T(8,128)S(1)} %cholesky.612), custom_call_target="Cholesky" | custom-call | tf_op jit(solution)/shard_map/jit(cholesky)/cholesky | solution.py:126
  761.4 11.9 %cholesky.537 = f32[128,128]{1,0:T(8,128)S(1)} custom-call(f32[128,128]{1,0:T(8,128)S(1)} %cholesky.616), custom_call_target="Cholesky" | custom-call | tf_op jit(solution)/shard_map/jit(cholesky)/cholesky | solution.py:126
  787.5 11.7 %cholesky.558 = f32[128,128]{1,0:T(8,128)S(1)} custom-call(f32[128,128]{1,0:T(8,128)S(1)} %cholesky.621), custom_call_target="Cholesky" | custom-call | tf_op jit(solution)/shard_map/jit(cholesky)/cholesky | solution.py:126
  812.8 11.7 %cholesky.575 = f32[128,128]{1,0:T(8,128)S(1)} custom-call(f32[128,128]{1,0:T(8,128)S(1)} %convolution_subtract_fusion.15), custom_call_target="Cholesky" | custom-call | tf_op jit(solution)/shard_map/jit(cholesky)/cholesky | solution.py:126
  830.7 12.0 %while.8 = (s32[]{:T(128)}, f32[512,512]{1,0:T(8,128)}, s32[4,2]{0,1:T(2,128)S(1)}, f32[4,128,128]{2,1,0:T(8,128)S(1)}, s32[]{:T(128)}) while((s32[]{:T(128)}, f32[512,512]{1,0:T(8,128)}, s32[4,2]{0,1:T(2,128)S(1)}, f32[4,128,128]{2,1,0:T(8,128)S(1)}, s32[]{:T(128)}) %tuple.90), condition=%wide.while_cond.clone.1, body=%wide.while_body.clone.1.sunk | while | flops 2 | bytes 131181 | solution.py:28
  843.5 40.1 %custom-call.42 = f32[4,128,128]{1,2,0:T(8,128)S(1)} custom-call(f32[4,128,128]{2,1,0:T(8,128)} %copy-done.16), custom_call_target="InvertDiagBlocksLowerTriangular" | custom-call | tf_op jit(solution)/shard_map/jit(_solve_triangular)/triangular_solve | solution.py:28
  (279 shorter events, 344.6 us)
Async XLA Ops:
  7.2 82.9 %reduce-scatter.4.cloned.1.call-start = ((), (), s32[]{:S(2)}) async-start(), calls=%async_computation.2 | async-start | bytes 3342336
  28.1 112.1 %all-gather.2.cloned.1.call-start = ((), (), s32[]{:S(2)}) async-start(), calls=%async_computation.1 | async-start | bytes 6684672 | tf_op jit(solution)/shard_map/all_gather | solution.py:83
  92.2 196.1 %copy-start.3 = (f32[512,512]{1,0:T(8,128)}, f32[512,512]{1,0:T(8,128)S(1)}, u32[]{:S(2)}) copy-start(f32[512,512]{1,0:T(8,128)S(1)} %fusion.32) | copy-start | bytes 3145732
  288.9 7.7 slice-start
  289.4 7.3 slice-start.1
  302.1 8.1 copy-start.5
  302.9 6.3 collective-permute-start
  311.4 2.9 collective-permute-start.1
  316.5 7.7 collective-permute-start.2
  326.1 14.3 %collective-permute-start.3 = (f32[64,512]{0,1:T(8,128)S(1)}, f32[64,512]{0,1:T(8,128)}, u32[]{:S(2)}, u32[]{:S(2)}) collective-permute-start(f32[64,512]{0,1:T(8,128)S(1)} %constant_dynamic-slice_fusion.8), channel_id=1, source_target_pairs={{0,4},{1,5},{2,6},{3,7},{4,0},{5,1},{6,2},{7,3},{8,12},{9,13},{10,... | collective-permute-start | bytes 393224 | tf_op jit(solution)/shard_map/ppermute | solution.py:13
  342.3 17.4 %collective-permute-start.4 = (f32[32,512]{0,1:T(8,128)}, f32[32,512]{0,1:T(8,128)}, u32[]{:S(2)}, u32[]{:S(2)}) collective-permute-start(f32[32,512]{0,1:T(8,128)} %constant_dynamic-slice_fusion.7), channel_id=1, source_target_pairs={{0,8},{1,9},{2,10},{3,11},{4,12},{5,13},{6,14},{7,15},{8,0},{9,1},... | collective-permute-start | bytes 196616 | tf_op jit(solution)/shard_map/ppermute | solution.py:13
  361.7 7.6 collective-permute-start.5
  369.4 7.9 collective-permute-start.6
  378.4 14.8 %collective-permute-start.7 = (f32[2,64,512]{2,1,0:T(8,128)S(1)}, f32[2,64,512]{2,1,0:T(8,128)}, u32[]{:S(2)}, u32[]{:S(2)}) collective-permute-start(f32[2,64,512]{2,1,0:T(8,128)S(1)} %maximum_select_fusion.6), channel_id=1, source_target_pairs={{0,4},{1,5},{2,6},{3,7},{4,0},{5,1},{6,2},{7,3},{8,12},{9,13},{10,... | collective-permute-start | bytes 786440 | tf_op jit(solution)/shard_map/ppermute | solution.py:13
  395.1 13.3 %collective-permute-start.8 = (f32[2,128,512]{2,1,0:T(8,128)}, f32[2,128,512]{2,1,0:T(8,128)}, u32[]{:S(2)}, u32[]{:S(2)}) collective-permute-start(f32[2,128,512]{2,1,0:T(8,128)} %maximum_select_fusion.4), channel_id=1, source_target_pairs={{0,2},{1,3},{2,0},{3,1},{4,6},{5,7},{6,4},{7,5},{8,10},{9,11},{10,... | collective-permute-start | bytes 1572872 | tf_op jit(solution)/shard_map/ppermute | solution.py:13
  411.2 6.0 collective-permute-start.9
  412.6 190.8 %collective-permute-start.10 = (f32[512,512]{1,0:T(8,128)}, f32[512,512]{1,0:T(8,128)}, u32[]{:S(2)}, u32[]{:S(2)}) collective-permute-start(f32[512,512]{1,0:T(8,128)} %copy-done.5), channel_id=1, source_target_pairs={{0,16},{16,0},{32,48},{48,32},{64,80},{80,64},{96,112},{112,96},{1... | collective-permute-start | bytes 3145736 | tf_op jit(solution)/shard_map/ppermute | solution.py:13
  589.4 8.2 copy-start.1
  601.4 21.3 %copy-start.2 = (f32[512,512]{1,0:T(8,128)}, f32[512,512]{1,0:T(8,128)S(1)}, u32[]{:S(2)}) copy-start(f32[512,512]{1,0:T(8,128)S(1)} %fusion.33) | copy-start | bytes 3145732
  609.3 7.5 collective-permute-start.12
  614.2 7.5 collective-permute-start.11
  624.7 3.0 collective-permute-start.13
  627.9 7.6 collective-permute-start.14
  635.7 14.6 %collective-permute-start.15 = (f32[64,512]{0,1:T(8,128)S(1)}, f32[64,512]{0,1:T(8,128)S(1)}, u32[]{:S(2)}, u32[]{:S(2)}) collective-permute-start(f32[64,512]{0,1:T(8,128)S(1)} %constant_dynamic-slice_fusion.4), channel_id=1, source_target_pairs={{0,4},{1,5},{2,6},{3,7},{4,0},{5,1},{6,2},{7,3},{8,12},{9,13},{10,... | collective-permute-start | bytes 393224 | tf_op jit(solution)/shard_map/ppermute | solution.py:13
  650.5 16.4 %collective-permute-start.16 = (f32[32,512]{0,1:T(8,128)S(1)}, f32[32,512]{0,1:T(8,128)S(1)}, u32[]{:S(2)}, u32[]{:S(2)}) collective-permute-start(f32[32,512]{0,1:T(8,128)S(1)} %constant_dynamic-slice_fusion.3), channel_id=1, source_target_pairs={{0,8},{1,9},{2,10},{3,11},{4,12},{5,13},{6,14},{7,15},{8,0},{9,1},... | collective-permute-start | bytes 196616 | tf_op jit(solution)/shard_map/ppermute | solution.py:13
  667.1 7.5 collective-permute-start.17
  675.6 8.2 collective-permute-start.18
  684.9 7.8 collective-permute-start.19
  692.7 14.1 %collective-permute-start.20 = (f32[2,64,512]{2,1,0:T(8,128)S(1)}, f32[2,64,512]{2,1,0:T(8,128)S(1)}, u32[]{:S(2)}, u32[]{:S(2)}) collective-permute-start(f32[2,64,512]{2,1,0:T(8,128)S(1)} %maximum_select_fusion.7), channel_id=1, source_target_pairs={{0,4},{1,5},{2,6},{3,7},{4,0},{5,1},{6,2},{7,3},{8,12},{9,13},{10,... | collective-permute-start | bytes 786440 | tf_op jit(solution)/shard_map/ppermute | solution.py:13
  706.9 12.2 %collective-permute-start.21 = (f32[2,128,512]{2,1,0:T(8,128)S(1)}, f32[2,128,512]{2,1,0:T(8,128)S(1)}, u32[]{:S(2)}, u32[]{:S(2)}) collective-permute-start(f32[2,128,512]{2,1,0:T(8,128)S(1)} %maximum_select_fusion.5), channel_id=1, source_target_pairs={{0,2},{1,3},{2,0},{3,1},{4,6},{5,7},{6,4},{7,5},{8,10},{9,11},{10,... | collective-permute-start | bytes 1572872 | tf_op jit(solution)/shard_map/ppermute | solution.py:13
  720.2 4.9 collective-permute-start.22
  760.1 123.5 %copy-start.4 = (f32[512,512]{1,0:T(8,128)S(1)}, f32[512,512]{1,0:T(8,128)}, u32[]{:S(2)}) copy-start(f32[512,512]{1,0:T(8,128)} %copy-done.3) | copy-start | bytes 3145732
  (12 other events, 20.4 us)
Sparse Core Ops, SparseCore 0:
  28.2 61.7 reduce-scatter.3
  92.2 47.9 all-gather.1

commit v2 on v1

--- a/solution.py
+++ b/solution.py
@@ -1,8 +1,11 @@
+import functools
 import math
 
 import jax
 import jax.numpy as jnp
 from jax import lax
+from jax.experimental import pallas as pl
+from jax.experimental.pallas import tpu as pltpu
 from jax.sharding import PartitionSpec as P
 
 HIGH = lax.Precision.HIGHEST
@@ -28,42 +31,105 @@
     return jax.scipy.linalg.solve_triangular(factor, eye, lower=True)
 
 
-def tile_bits():
-    return [bit for bit in range(lax.axis_size("tile").bit_length() - 1)]
-
-
-def halve(block):
-    tile = lax.axis_index("tile")
-    for bit in tile_bits():
-        side = (tile >> bit) & 1
-        half = block.shape[0] // 2
-        keep = lax.dynamic_slice_in_dim(block, side * half, half, 0)
-        send = lax.dynamic_slice_in_dim(block, (1 - side) * half, half, 0)
-        block = keep + swap(send, "tile", 1 << bit)
-    return block
-
-
-def double(block, dim):
-    tile = lax.axis_index("tile")
-    for bit in reversed(tile_bits()):
-        side = (tile >> bit) & 1
-        other = swap(block, "tile", 1 << bit)
-        block = jnp.where(
-            side == 0,
-            jnp.concatenate([block, other], axis=dim),
-            jnp.concatenate([other, block], axis=dim),
+MESH = pl.DeviceIdType.MESH
+VMEM = pltpu.VMEM
+
+
+def greet(count):
+    me = lax.axis_index("tile")
+    barrier = pltpu.get_barrier_semaphore()
+    for step in range(1, count):
+        pl.semaphore_signal(
+            barrier, inc=1, device_id={"tile": lax.rem(me + step, count)}, device_id_type=MESH
         )
-    return block
-
-
-def chunk_rows(block, count):
-    tile = lax.axis_index("tile")
-    start = 0
-    size = block.shape[0]
-    for bit in tile_bits():
-        size //= 2
-        start = start + ((tile >> bit) & 1) * size
-    return lax.dynamic_slice_in_dim(block, start, count, 0)
+    pl.semaphore_wait(barrier, count - 1)
+    return me
+
+
+def scatter_kernel(count, block_ref, out_ref, held, send_sem, recv_sem):
+    me = greet(count)
+    rows = out_ref.shape[0]
+    copies = []
+    for step in range(1, count):
+        target = lax.rem(me + step, count)
+        copy = pltpu.make_async_remote_copy(
+            src_ref=block_ref.at[pl.ds(pl.multiple_of(target * rows, 8), rows)],
+            dst_ref=held.at[step],
+            send_sem=send_sem.at[step],
+            recv_sem=recv_sem.at[step],
+            device_id={"tile": target},
+            device_id_type=MESH,
+        )
+        copy.start()
+        copies.append(copy)
+    total = block_ref[pl.ds(pl.multiple_of(me * rows, 8), rows), :]
+    for step, copy in zip(range(1, count), copies):
+        copy.wait()
+        total = total + held[step]
+    out_ref[...] = total
+
+
+def gather_kernel(count, block_ref, out_ref, held, send_sem, recv_sem):
+    me = greet(count)
+    rows = block_ref.shape[0]
+    copies = []
+    for step in range(1, count):
+        target = lax.rem(me + step, count)
+        copy = pltpu.make_async_remote_copy(
+            src_ref=block_ref,
+            dst_ref=held.at[pl.ds(pl.multiple_of(me * rows, 8), rows)],
+            send_sem=send_sem.at[step],
+            recv_sem=recv_sem.at[step],
+            device_id={"tile": target},
+            device_id_type=MESH,
+        )
+        copy.start()
+        copies.append(copy)
+    out_ref[pl.ds(pl.multiple_of(me * rows, 8), rows), :] = block_ref[...]
+    for step, copy in zip(range(1, count), copies):
+        copy.wait()
+        source = lax.rem(me + count - step, count)
+        out_ref[pl.ds(pl.multiple_of(source * rows, 8), rows), :] = held[
+            pl.ds(pl.multiple_of(source * rows, 8), rows), :
+        ]
+
+
+def tile_scatter(block, ident):
+    count = lax.axis_size("tile")
+    rows = block.shape[0] // count
+    return pl.pallas_call(
+        functools.partial(scatter_kernel, count),
+        out_shape=jax.ShapeDtypeStruct((rows, block.shape[1]), block.dtype),
+        in_specs=[pl.BlockSpec(memory_space=VMEM)],
+        out_specs=pl.BlockSpec(memory_space=VMEM),
+        scratch_shapes=[
+            VMEM((count, rows, block.shape[1]), block.dtype),
+            pltpu.SemaphoreType.DMA((count,)),
+            pltpu.SemaphoreType.DMA((count,)),
+        ],
+        compiler_params=pltpu.CompilerParams(
+            collective_id=ident, has_side_effects=True
+        ),
+    )(block)
+
+
+def tile_gather(block, ident):
+    count = lax.axis_size("tile")
+    shape = (block.shape[0] * count, block.shape[1])
+    return pl.pallas_call(
+        functools.partial(gather_kernel, count),
+        out_shape=jax.ShapeDtypeStruct(shape, block.dtype),
+        in_specs=[pl.BlockSpec(memory_space=VMEM)],
+        out_specs=pl.BlockSpec(memory_space=VMEM),
+        scratch_shapes=[
+            VMEM(shape, block.dtype),
+            pltpu.SemaphoreType.DMA((count,)),
+            pltpu.SemaphoreType.DMA((count,)),
+        ],
+        compiler_params=pltpu.CompilerParams(
+            collective_id=ident, has_side_effects=True
+        ),
+    )(block)
 
 
 def on_device(schur, samples):
@@ -77,12 +143,8 @@
     keep = (jnp.arange(leaves, dtype=jnp.int32) != node)[:, None, None]
     masked = jnp.where(keep, samples, 0.0).reshape(leaves * slice_cols, rank_size)
     stacked = schur.reshape(leaves * slice_cols, leaf_rows)
-    sample_rows = lax.psum_scatter(
-        transposed(stacked, masked), "tile", scatter_dimension=0, tiled=True
-    )
-    both = lax.all_gather(
-        jnp.concatenate([sample_rows, owned], axis=1), "tile", axis=0, tiled=True
-    )
+    sample_rows = tile_scatter(transposed(stacked, masked), 1)
+    both = tile_gather(jnp.concatenate([sample_rows, owned], axis=1), 2)
     local = both[:, :rank_size]
     omega = both[:, rank_size:]
     factor = jnp.linalg.cholesky(transposed(local, local))
@@ -101,11 +163,12 @@
     cousin_meet = meet(jnp.bitwise_xor(node, 2))
     further_meet = meet(jnp.bitwise_xor(node, 3))
 
-    near_part = halve(transposed(near_meet, sibling_rows))
-    sample_part = chunk_rows(factor.T, near_part.shape[0]) - near_part
+    near_part = tile_scatter(transposed(near_meet, sibling_rows), 3)
+    chunk = near_part.shape[0]
+    sample_part = lax.dynamic_slice_in_dim(factor.T, tile * chunk, chunk, 0) - near_part
     other_part = swap(sample_part, "node", 1)
-    pair = double(jnp.stack([sample_part, other_part]), 1)
-    parent_sample, other_sample = pair[0], pair[1]
+    pair = tile_gather(jnp.concatenate([sample_part, other_part], axis=1), 4)
+    parent_sample, other_sample = pair[:, :rank_size], pair[:, rank_size:]
     parent_factor = jnp.linalg.cholesky(
         transposed(parent_sample, parent_sample) + transposed(other_sample, other_sample)
     )
@@ -117,12 +180,12 @@
     cousin_rows = swap(panel_two, "node", 2)
     further_rows = swap(panel_two, "node", 3)
     far_sum = transposed(cousin_meet, cousin_rows) + transposed(further_meet, further_rows)
-    far_part = halve(transposed(transfer_own, far_sum))
+    far_part = tile_scatter(transposed(transfer_own, far_sum), 5)
     far_pair = far_part + swap(far_part, "node", 1)
-    grand_part = chunk_rows(parent_factor.T, far_pair.shape[0]) - far_pair
+    grand_part = lax.dynamic_slice_in_dim(parent_factor.T, tile * chunk, chunk, 0) - far_pair
     cousin_part = swap(grand_part, "node", 2)
-    grand_pair = double(jnp.stack([grand_part, cousin_part]), 1)
-    grand_sample, cousin_grand = grand_pair[0], grand_pair[1]
+    grand_pair = tile_gather(jnp.concatenate([grand_part, cousin_part], axis=1), 6)
+    grand_sample, cousin_grand = grand_pair[:, :rank_size], grand_pair[:, rank_size:]
     grand_factor = jnp.linalg.cholesky(
         transposed(grand_sample, grand_sample) + transposed(cousin_grand, cousin_grand)
     )

time: 906 us -> 1000 us (1.10)
  Pallas kernels: 0 us -> 393 us
  waiting for transfers between devices: 276 us -> 34.2 us
  other arithmetic: 396 us -> 376 us
  starting transfers between devices: 26.4 us -> 8 us
  between operations: 23.1 us -> 9.46 us
  local copies, waits for them, and re-layouts: 60.8 us -> 50.6 us
    pallas_call x0 -> x6, Pallas kernels: none -> 393 us  [the longest x3 252 us: tile_gather(): pl.pallas_call(functools.partial(gather_kernel, count), out_shape=jax.Sha...]
    ppermute x23 -> x7, waiting for transfers between devices: 167 us -> 34.2 us  [swap(): lax.ppermute(block, axis, [(low, low ^ mask) for low in range(count)])]
    unnamed x3 -> x0, waiting for transfers between devices: 60.7 us -> none
    all_gather x1 -> x0, waiting for transfers between devices: 48 us -> none  [on_device(): lax.all_gather(jnp.concatenate([sample_rows, owned], axis=1), 'tile', axi...]
    ppermute x23 -> x7, starting transfers between devices: 26.1 us -> 8 us  [swap(): lax.ppermute(block, axis, [(low, low ^ mask) for low in range(count)])]
    dot_general x13, matrix products: 50.4 us -> 64.1 us  [transposed(): lax.dot_general(left, right, (((0,), (0,)), ((), ())), precision=HIGH, pr...]
    select_n x8 -> x0, other arithmetic: 12.5 us -> none  [double(): jnp.where(side == 0, jnp.concatenate([block, other], axis=dim), jnp.conca...]
    another operation x40 -> x56, local copies, waits for them, and re-layouts: 34.6 us -> 38.6 us  [inverse_lower(): return jax.scipy.linalg.solve_triangular(factor, eye, lower=True)]
  transfers between devices with their start and end apart: 25 -> 7, of which waited for: 23 -> 5; matrix products, arithmetic and copies ran while one was open for 22% -> 20% of each run, Pallas kernels for 0% -> 8%
where the time goes in v2:
time: 1000 us; the launch traced here: 996 us
  Pallas kernels  393 us (39%)
  other arithmetic  376 us (38%)
  matrix products  124 us (12%)
  local copies, waits for them, and re-layouts  50.6 us (5%)
  waiting for transfers between devices  34.2 us (3%)
    pallas_call x3, Pallas kernels, tile_gather(): pl.pallas_call(functools.partial(gather_kernel, count), out_shape=jax.Sha...  252 us
    pallas_call x3, Pallas kernels, tile_scatter(): pl.pallas_call(functools.partial(scatter_kernel, count), out_shape=jax.Sh...  141 us
    another operation x7, other arithmetic, inverse_lower(): return jax.scipy.linalg.solve_triangular(factor, eye, lower=True)  126 us
    another operation x15, other arithmetic, on_device(): jnp.linalg.cholesky(transposed(parent_sample, parent_sample) + transposed...  81.8 us
    another operation x15, other arithmetic, on_device(): jnp.linalg.cholesky(transposed(grand_sample, grand_sample) + transposed(c...  79.7 us
    another operation x14, other arithmetic, on_device(): factor = jnp.linalg.cholesky(transposed(local, local))  79.1 us
    dot_general x13, matrix products, transposed(): lax.dot_general(left, right, (((0,), (0,)), ((), ())), precision=HIGH, pr...  64.1 us
    another operation x56, local copies, waits for them, and re-layouts, inverse_lower(): return jax.scipy.linalg.solve_triangular(factor, eye, lower=True)  38.6 us
  transfers between devices with their start and end apart: 7, of which 5 were waited for; matrix products, arithmetic and copies ran while one was open for 20% of the time, Pallas kernels for 8%

profile of v2, /device:TPU:1, one launch (start us, length us, event | category | flops | bytes accessed | tf_op | source)
XLA Modules:
  0.0 996.0 jit_solution(11251269593545415795)
XLA Ops:
  1.6 21.2 %convolution_bitcast_fusion.block_ref = f32[1536,512]{1,0:T(8,128)} fusion(f32[16,96,1536]{2,1,0:T(8,128)} %param.5, f32[16,96,512]{2,1,0:T(8,128)} %param.6, pred[16]{0:T(512)(128)(4,1)S(1)} %iota_compare_fusion.5), kind=kOutput, calls=%fused_computation.6 | convolution fusion | flops 14496301056 | bytes 15728656 | tf_op jit(solution)/shard_map/dot_general | solution.py:24
  22.8 80.5 %shard_map.49 = f32[96,512]{1,0:T(8,128)} custom-call(f32[1536,512]{1,0:T(8,128)} %convolution_bitcast_fusion.block_ref), custom_call_target="tpu_custom_call" | custom-call | tf_op jit(solution)/shard_map/pallas_call | solution.py:100
  105.1 144.9 %shard_map.50 = f32[1536,1024]{1,0:T(8,128)} custom-call(f32[96,1024]{1,0:T(8,128)} %pad_maximum_fusion.3.block_ref), custom_call_target="tpu_custom_call" | custom-call | tf_op jit(solution)/shard_map/pallas_call | solution.py:119
  258.5 11.7 %cholesky.374 = f32[128,128]{1,0:T(8,128)S(1)} custom-call(f32[128,128]{1,0:T(8,128)S(1)} %cholesky.586), custom_call_target="Cholesky" | custom-call | tf_op jit(solution)/shard_map/jit(cholesky)/cholesky | solution.py:150
  270.3 10.2 %custom-call.31 = f32[1,128,128]{1,2,0:T(8,128)S(1)} custom-call(f32[1,128,128]{2,1,0:T(8,128)S(1)} %get-tuple-element.91), custom_call_target="InvertDiagBlocksLowerTriangular" | custom-call | tf_op jit(solution)/shard_map/jit(cholesky)/cholesky | solution.py:150
  281.6 11.7 %cholesky.393 = f32[128,128]{1,0:T(8,128)S(1)} custom-call(f32[128,128]{1,0:T(8,128)S(1)} %cholesky.590), custom_call_target="Cholesky" | custom-call | tf_op jit(solution)/shard_map/jit(cholesky)/cholesky | solution.py:150
  293.5 9.8 custom-call.32
  304.3 11.9 %cholesky.414 = f32[128,128]{1,0:T(8,128)S(1)} custom-call(f32[128,128]{1,0:T(8,128)S(1)} %cholesky.595), custom_call_target="Cholesky" | custom-call | tf_op jit(solution)/shard_map/jit(cholesky)/cholesky | solution.py:150
  326.9 11.7 %cholesky.431 = f32[128,128]{1,0:T(8,128)S(1)} custom-call(f32[128,128]{1,0:T(8,128)S(1)} %convolution_subtract_fusion.17), custom_call_target="Cholesky" | custom-call | tf_op jit(solution)/shard_map/jit(cholesky)/cholesky | solution.py:150
  353.3 39.7 %custom-call.34 = f32[4,128,128]{1,2,0:T(8,128)S(1)} custom-call(f32[4,128,128]{2,1,0:T(8,128)S(1)} %get-tuple-element.25), custom_call_target="InvertDiagBlocksLowerTriangular" | custom-call | tf_op jit(solution)/shard_map/jit(_solve_triangular)/triangular_solve | solution.py:31
  416.5 22.9 %collective-permute-done = f32[96,512]{1,0:T(8,128)S(1)} collective-permute-done((f32[96,512]{1,0:T(8,128)S(1)}, f32[96,512]{1,0:T(8,128)S(1)}, u32[]{:S(2)}, u32[]{:S(2)}) %collective-permute-start) | collective-permute-done | bytes 196640 | tf_op jit(solution)/shard_map/ppermute | solution.py:16
  441.4 29.9 %shard_map.51 = f32[32,512]{1,0:T(8,128)} custom-call(f32[512,512]{1,0:T(8,128)} %fusion.159.block_ref), custom_call_target="tpu_custom_call" | custom-call | tf_op jit(solution)/shard_map/pallas_call | solution.py:100
  477.4 51.6 %shard_map.52 = f32[512,1024]{1,0:T(8,128)} custom-call(f32[32,1024]{1,0:T(8,128)} %pad_maximum_fusion.4.block_ref), custom_call_target="tpu_custom_call" | custom-call | tf_op jit(solution)/shard_map/pallas_call | solution.py:119
  542.2 11.7 %cholesky.446 = f32[128,128]{1,0:T(8,128)S(1)} custom-call(f32[128,128]{1,0:T(8,128)S(1)} %cholesky.599), custom_call_target="Cholesky" | custom-call | tf_op jit(solution)/shard_map/jit(cholesky)/cholesky | solution.py:172
  554.1 10.2 %custom-call.35 = f32[1,128,128]{1,2,0:T(8,128)S(1)} custom-call(f32[1,128,128]{2,1,0:T(8,128)S(1)} %get-tuple-element.85), custom_call_target="InvertDiagBlocksLowerTriangular" | custom-call | tf_op jit(solution)/shard_map/jit(cholesky)/cholesky | solution.py:172
  569.5 11.7 %cholesky.465 = f32[128,128]{1,0:T(8,128)S(1)} custom-call(f32[128,128]{1,0:T(8,128)S(1)} %cholesky.603), custom_call_target="Cholesky" | custom-call | tf_op jit(solution)/shard_map/jit(cholesky)/cholesky | solution.py:172
  581.4 9.8 custom-call.36
  596.0 12.7 %cholesky.486 = f32[128,128]{1,0:T(8,128)S(1)} custom-call(f32[128,128]{1,0:T(8,128)} %cholesky.608), custom_call_target="Cholesky" | custom-call | tf_op jit(solution)/shard_map/jit(cholesky)/cholesky | solution.py:172
  611.6 10.6 %custom-call.37 = f32[1,128,128]{1,2,0:T(8,128)S(1)} custom-call(f32[1,128,128]{2,1,0:T(8,128)} %get-tuple-element.81), custom_call_target="InvertDiagBlocksLowerTriangular" | custom-call | tf_op jit(solution)/shard_map/jit(cholesky)/cholesky | solution.py:172
  624.7 11.7 %cholesky.503 = f32[128,128]{1,0:T(8,128)S(1)} custom-call(f32[128,128]{1,0:T(8,128)S(1)} %convolution_subtract_fusion.16), custom_call_target="Cholesky" | custom-call | tf_op jit(solution)/shard_map/jit(cholesky)/cholesky | solution.py:172
  645.8 14.4 %while.7 = (s32[]{:T(128)}, f32[512,512]{0,1:T(8,128)}, s32[4,2]{0,1:T(2,128)S(1)}, f32[4,128,128]{2,1,0:T(8,128)}, s32[]{:T(128)}) while((s32[]{:T(128)}, f32[512,512]{0,1:T(8,128)}, s32[4,2]{0,1:T(2,128)S(1)}, f32[4,128,128]{2,1,0:T(8,128)}, s32[]{:T(128)}) %tuple.83), condition=%wide.while_cond.clone, body=%wide.while_body.clone.sunk | while | flops 2 | bytes 393829 | solution.py:31
  660.2 40.9 %custom-call.38 = f32[4,128,128]{1,2,0:T(8,128)} custom-call(f32[4,128,128]{2,1,0:T(8,128)} %get-tuple-element.26), custom_call_target="InvertDiagBlocksLowerTriangular" | custom-call | tf_op jit(solution)/shard_map/jit(_solve_triangular)/triangular_solve | solution.py:31
  740.5 30.7 %shard_map.53 = f32[32,512]{1,0:T(8,128)} custom-call(f32[512,512]{1,0:T(8,128)} %fusion.163.block_ref), custom_call_target="tpu_custom_call" | custom-call | tf_op jit(solution)/shard_map/pallas_call | solution.py:100
  781.9 55.5 %shard_map.54 = f32[512,1024]{1,0:T(8,128)} custom-call(f32[32,1024]{1,0:T(8,128)} %pad_maximum_fusion.5.block_ref), custom_call_target="tpu_custom_call" | custom-call | tf_op jit(solution)/shard_map/pallas_call | solution.py:119
  844.9 11.7 %cholesky.518 = f32[128,128]{1,0:T(8,128)S(1)} custom-call(f32[128,128]{1,0:T(8,128)S(1)} %cholesky.612), custom_call_target="Cholesky" | custom-call | tf_op jit(solution)/shard_map/jit(cholesky)/cholesky | solution.py:189
  856.8 9.8 custom-call.39
  867.3 11.9 %cholesky.537 = f32[128,128]{1,0:T(8,128)S(1)} custom-call(f32[128,128]{1,0:T(8,128)S(1)} %cholesky.616), custom_call_target="Cholesky" | custom-call | tf_op jit(solution)/shard_map/jit(cholesky)/cholesky | solution.py:189
  891.0 11.7 %cholesky.558 = f32[128,128]{1,0:T(8,128)S(1)} custom-call(f32[128,128]{1,0:T(8,128)S(1)} %cholesky.621), custom_call_target="Cholesky" | custom-call | tf_op jit(solution)/shard_map/jit(cholesky)/cholesky | solution.py:189
  903.5 10.2 %custom-call.41 = f32[1,128,128]{1,2,0:T(8,128)S(1)} custom-call(f32[1,128,128]{2,1,0:T(8,128)S(1)} %get-tuple-element.73), custom_call_target="InvertDiagBlocksLowerTriangular" | custom-call | tf_op jit(solution)/shard_map/jit(cholesky)/cholesky | solution.py:189
  914.3 11.7 %cholesky.575 = f32[128,128]{1,0:T(8,128)S(1)} custom-call(f32[128,128]{1,0:T(8,128)S(1)} %convolution_subtract_fusion.15), custom_call_target="Cholesky" | custom-call | tf_op jit(solution)/shard_map/jit(cholesky)/cholesky | solution.py:189
  931.3 14.4 %while.8 = (s32[]{:T(128)}, f32[512,512]{1,0:T(8,128)}, s32[4,2]{0,1:T(2,128)S(1)}, f32[4,128,128]{2,1,0:T(8,128)}, s32[]{:T(128)}) while((s32[]{:T(128)}, f32[512,512]{1,0:T(8,128)}, s32[4,2]{0,1:T(2,128)S(1)}, f32[4,128,128]{2,1,0:T(8,128)}, s32[]{:T(128)}) %tuple.84), condition=%wide.while_cond.clone.1, body=%wide.while_body.clone.1.sunk | while | flops 2 | bytes 132705 | solution.py:31
  945.7 40.3 %custom-call.42 = f32[4,128,128]{1,2,0:T(8,128)S(1)} custom-call(f32[4,128,128]{2,1,0:T(8,128)} %get-tuple-element.27), custom_call_target="InvertDiagBlocksLowerTriangular" | custom-call | tf_op jit(solution)/shard_map/jit(_solve_triangular)/triangular_solve | solution.py:31
  (224 shorter events, 224.1 us)
Async XLA Ops:
  338.9 56.3 %copy-start.2 = (f32[512,512]{1,0:T(8,128)}, f32[512,512]{1,0:T(8,128)S(1)}, u32[]{:S(2)}) copy-start(f32[512,512]{1,0:T(8,128)S(1)} %fusion.33) | copy-start | bytes 3145732
  395.9 7.7 slice-start
  396.3 7.3 slice-start.1
  410.0 306.8 %collective-permute-start.2 = (f32[512,512]{1,0:T(8,128)}, f32[512,512]{1,0:T(8,128)}, u32[]{:S(2)}, u32[]{:S(2)}) collective-permute-start(f32[512,512]{1,0:T(8,128)} %fusion), channel_id=1, source_target_pairs={{0,16},{16,0},{32,48},{48,32},{64,80},{80,64},{96,112},{112,96},{1... | collective-permute-start | bytes 3145736 | tf_op jit(solution)/shard_map/ppermute | solution.py:16
  413.3 26.1 %collective-permute-start = (f32[96,512]{1,0:T(8,128)S(1)}, f32[96,512]{1,0:T(8,128)S(1)}, u32[]{:S(2)}, u32[]{:S(2)}) collective-permute-start(f32[96,512]{1,0:T(8,128)S(1)} %fusion.99), channel_id=1, source_target_pairs={{0,16},{16,0},{32,48},{48,32},{64,80},{80,64},{96,112},{112,96},{1... | collective-permute-start | bytes 589832 | tf_op jit(solution)/shard_map/ppermute | solution.py:16
  472.3 4.4 collective-permute-start.1
  541.2 1.0 copy-start.5
  568.8 0.7 copy-start.6
  701.2 5.8 copy-start.7
  701.2 8.3 copy-start
  713.3 24.3 %copy-start.1 = (f32[512,512]{1,0:T(8,128)}, f32[512,512]{1,0:T(8,128)S(1)}, u32[]{:S(2)}) copy-start(f32[512,512]{1,0:T(8,128)S(1)} %fusion.40) | copy-start | bytes 3145732
  723.0 11.0 %collective-permute-start.4 = (f32[96,512]{1,0:T(8,128)S(1)}, f32[96,512]{1,0:T(8,128)S(1)}, u32[]{:S(2)}, u32[]{:S(2)}) collective-permute-start(f32[96,512]{1,0:T(8,128)S(1)} %fusion.97), channel_id=1, source_target_pairs={{0,48},{16,32},{32,16},{48,0},{64,112},{80,96},{96,80},{112,64},{1... | collective-permute-start | bytes 589832 | tf_op jit(solution)/shard_map/ppermute | solution.py:16
  728.9 7.7 collective-permute-start.3
  771.2 4.2 collective-permute-start.5
  776.3 4.9 collective-permute-start.6
  867.0 119.0 %copy-start.3 = (f32[512,512]{1,0:T(8,128)S(1)}, f32[512,512]{1,0:T(8,128)}, u32[]{:S(2)}) copy-start(f32[512,512]{1,0:T(8,128)} %copy-done.2) | copy-start | bytes 3145732
  945.7 46.1 %copy-start.4 = (f32[512,1024]{1,0:T(8,128)S(1)}, f32[512,1024]{1,0:T(8,128)}, u32[]{:S(2)}) copy-start(f32[512,1024]{1,0:T(8,128)} %shard_map.54) | copy-start | bytes 6291460

commit v3 on v2

--- a/solution.py
+++ b/solution.py
@@ -143,8 +143,12 @@
     keep = (jnp.arange(leaves, dtype=jnp.int32) != node)[:, None, None]
     masked = jnp.where(keep, samples, 0.0).reshape(leaves * slice_cols, rank_size)
     stacked = schur.reshape(leaves * slice_cols, leaf_rows)
-    sample_rows = tile_scatter(transposed(stacked, masked), 1)
-    both = tile_gather(jnp.concatenate([sample_rows, owned], axis=1), 2)
+    sample_rows = lax.psum_scatter(
+        transposed(stacked, masked), "tile", scatter_dimension=0, tiled=True
+    )
+    both = lax.all_gather(
+        jnp.concatenate([sample_rows, owned], axis=1), "tile", axis=0, tiled=True
+    )
     local = both[:, :rank_size]
     omega = both[:, rank_size:]
     factor = jnp.linalg.cholesky(transposed(local, local))

time: 1000 us -> 904 us (0.904)
  Pallas kernels: 393 us -> 170 us
  waiting for transfers between devices: 34.2 us -> 142 us
  between operations: 9.46 us -> 22.9 us
    pallas_call x3 -> x2, Pallas kernels: 252 us -> 109 us  [tile_gather(): pl.pallas_call(functools.partial(gather_kernel, count), out_shape=jax.Sha...]
    pallas_call x3 -> x2, Pallas kernels: 141 us -> 61.1 us  [tile_scatter(): pl.pallas_call(functools.partial(scatter_kernel, count), out_shape=jax.Sh...]
    unnamed x0 -> x3, waiting for transfers between devices: none -> 60.6 us
    all_gather x0 -> x1, waiting for transfers between devices: none -> 47.9 us  [on_device(): lax.all_gather(jnp.concatenate([sample_rows, owned], axis=1), 'tile', axi...]
  transfers between devices with their start and end apart: 7 -> 9, of which waited for: 5 -> 7; matrix products, arithmetic and copies ran while one was open for 20% -> 23% of each run, Pallas kernels for 8% -> 9%
where the time goes in v3:
time: 904 us; the launch traced here: 899 us
  other arithmetic  374 us (41%)
  Pallas kernels  170 us (19%)
  waiting for transfers between devices  142 us (16%)
  matrix products  125 us (14%)
  local copies, waits for them, and re-layouts  56.1 us (6%)
  between operations  22.9 us (3%)
    another operation x7, other arithmetic, inverse_lower(): return jax.scipy.linalg.solve_triangular(factor, eye, lower=True)  126 us
    pallas_call x2, Pallas kernels, tile_gather(): pl.pallas_call(functools.partial(gather_kernel, count), out_shape=jax.Sha...  109 us
    another operation x15, other arithmetic, on_device(): jnp.linalg.cholesky(transposed(parent_sample, parent_sample) + transposed...  81.8 us
    another operation x15, other arithmetic, on_device(): jnp.linalg.cholesky(transposed(grand_sample, grand_sample) + transposed(c...  79.7 us
    another operation x14, other arithmetic, on_device(): factor = jnp.linalg.cholesky(transposed(local, local))  79 us
    dot_general x13, matrix products, transposed(): lax.dot_general(left, right, (((0,), (0,)), ((), ())), precision=HIGH, pr...  61.3 us
    pallas_call x2, Pallas kernels, tile_scatter(): pl.pallas_call(functools.partial(scatter_kernel, count), out_shape=jax.Sh...  61.1 us
    unnamed x3, waiting for transfers between devices  60.6 us
  transfers between devices with their start and end apart: 9, of which 7 were waited for; matrix products, arithmetic and copies ran while one was open for 23% of the time, Pallas kernels for 9%

profile of v3, /device:TPU:1, one launch (start us, length us, event | category | flops | bytes accessed | tf_op | source)
XLA Modules:
  0.0 898.8 jit_solution(15054704045190258612)
XLA Ops:
  7.2 18.4 %convolution_bitcast_fusion = f32[1536,512]{0,1:T(8,128)S(1)} fusion(f32[16,96,1536]{2,1,0:T(8,128)} %param.5, f32[16,96,512]{2,1,0:T(8,128)} %param.6, pred[16]{0:T(512)(128)(4,1)S(1)} %iota_compare_fusion.5), kind=kOutput, calls=%fused_computation.6 | convolution fusion | flops 14496301056 | bytes 15728656 | tf_op jit(solution)/shard_map/dot_general | solution.py:24
  29.5 60.6 %reduce-scatter.4.cloned.1.call-done = f32[96,512]{1,0:T(8,128)} async-done(((f32[1536,512]{1,0:T(8,128)}), f32[96,512]{1,0:T(8,128)}) %reduce-scatter.4.cloned.1.call-update) | async-done | bytes 196624
  92.2 47.9 %all-gather.2.cloned.1.call-done = f32[1536,1024]{1,0:T(8,128)} async-done(((f32[96,1024]{1,0:T(8,128)}), f32[1536,1024]{1,0:T(8,128)}) %all-gather.2.cloned.1.call-update) | async-done | bytes 6291472 | tf_op jit(solution)/shard_map/all_gather | solution.py:149
  149.7 11.7 %cholesky.374 = f32[128,128]{1,0:T(8,128)S(1)} custom-call(f32[128,128]{1,0:T(8,128)S(1)} %cholesky.586), custom_call_target="Cholesky" | custom-call | tf_op jit(solution)/shard_map/jit(cholesky)/cholesky | solution.py:154
  161.6 10.3 %custom-call.31 = f32[1,128,128]{1,2,0:T(8,128)S(1)} custom-call(f32[1,128,128]{2,1,0:T(8,128)S(1)} %get-tuple-element.99), custom_call_target="InvertDiagBlocksLowerTriangular" | custom-call | tf_op jit(solution)/shard_map/jit(cholesky)/cholesky | solution.py:154
  174.7 11.7 %cholesky.393 = f32[128,128]{1,0:T(8,128)S(1)} custom-call(f32[128,128]{1,0:T(8,128)S(1)} %cholesky.590), custom_call_target="Cholesky" | custom-call | tf_op jit(solution)/shard_map/jit(cholesky)/cholesky | solution.py:154
  186.6 9.8 %custom-call.32 = f32[1,128,128]{1,2,0:T(8,128)S(1)} custom-call(f32[1,128,128]{2,1,0:T(8,128)S(1)} %get-tuple-element.97), custom_call_target="InvertDiagBlocksLowerTriangular" | custom-call | tf_op jit(solution)/shard_map/jit(cholesky)/cholesky | solution.py:154
  198.3 11.7 %cholesky.414 = f32[128,128]{1,0:T(8,128)S(1)} custom-call(f32[128,128]{1,0:T(8,128)S(1)} %cholesky.595), custom_call_target="Cholesky" | custom-call | tf_op jit(solution)/shard_map/jit(cholesky)/cholesky | solution.py:154
  210.1 9.9 %custom-call.33 = f32[1,128,128]{1,2,0:T(8,128)S(1)} custom-call(f32[1,128,128]{2,1,0:T(8,128)S(1)} %get-tuple-element.95), custom_call_target="InvertDiagBlocksLowerTriangular" | custom-call | tf_op jit(solution)/shard_map/jit(cholesky)/cholesky | solution.py:154
  221.7 11.7 %cholesky.431 = f32[128,128]{1,0:T(8,128)S(1)} custom-call(f32[128,128]{1,0:T(8,128)S(1)} %convolution_subtract_fusion.17), custom_call_target="Cholesky" | custom-call | tf_op jit(solution)/shard_map/jit(cholesky)/cholesky | solution.py:154
  247.9 39.7 %custom-call.34 = f32[4,128,128]{1,2,0:T(8,128)S(1)} custom-call(f32[4,128,128]{2,1,0:T(8,128)S(1)} %get-tuple-element.25), custom_call_target="InvertDiagBlocksLowerTriangular" | custom-call | tf_op jit(solution)/shard_map/jit(_solve_triangular)/triangular_solve | solution.py:31
  311.1 22.4 %collective-permute-done = f32[96,512]{1,0:T(8,128)S(1)} collective-permute-done((f32[96,512]{1,0:T(8,128)S(1)}, f32[96,512]{1,0:T(8,128)S(1)}, u32[]{:S(2)}, u32[]{:S(2)}) %collective-permute-start) | collective-permute-done | bytes 196640 | tf_op jit(solution)/shard_map/ppermute | solution.py:16
  335.6 30.5 %shard_map.49 = f32[32,512]{1,0:T(8,128)} custom-call(f32[512,512]{1,0:T(8,128)} %fusion.159.block_ref), custom_call_target="tpu_custom_call" | custom-call | tf_op jit(solution)/shard_map/pallas_call | solution.py:100
  371.9 53.3 %shard_map.50 = f32[512,1024]{1,0:T(8,128)} custom-call(f32[32,1024]{1,0:T(8,128)} %pad_maximum_fusion.4.block_ref), custom_call_target="tpu_custom_call" | custom-call | tf_op jit(solution)/shard_map/pallas_call | solution.py:119
  438.4 11.7 %cholesky.446 = f32[128,128]{1,0:T(8,128)S(1)} custom-call(f32[128,128]{1,0:T(8,128)S(1)} %cholesky.599), custom_call_target="Cholesky" | custom-call | tf_op jit(solution)/shard_map/jit(cholesky)/cholesky | solution.py:176
  450.3 10.2 %custom-call.35 = f32[1,128,128]{1,2,0:T(8,128)S(1)} custom-call(f32[1,128,128]{2,1,0:T(8,128)S(1)} %get-tuple-element.93), custom_call_target="InvertDiagBlocksLowerTriangular" | custom-call | tf_op jit(solution)/shard_map/jit(cholesky)/cholesky | solution.py:176
  465.7 11.7 %cholesky.465 = f32[128,128]{1,0:T(8,128)S(1)} custom-call(f32[128,128]{1,0:T(8,128)S(1)} %cholesky.603), custom_call_target="Cholesky" | custom-call | tf_op jit(solution)/shard_map/jit(cholesky)/cholesky | solution.py:176
  477.6 9.8 %custom-call.36 = f32[1,128,128]{1,2,0:T(8,128)S(1)} custom-call(f32[1,128,128]{2,1,0:T(8,128)S(1)} %get-tuple-element.91), custom_call_target="InvertDiagBlocksLowerTriangular" | custom-call | tf_op jit(solution)/shard_map/jit(cholesky)/cholesky | solution.py:176
  492.2 12.7 %cholesky.486 = f32[128,128]{1,0:T(8,128)S(1)} custom-call(f32[128,128]{1,0:T(8,128)} %cholesky.608), custom_call_target="Cholesky" | custom-call | tf_op jit(solution)/shard_map/jit(cholesky)/cholesky | solution.py:176
  507.8 10.6 %custom-call.37 = f32[1,128,128]{1,2,0:T(8,128)S(1)} custom-call(f32[1,128,128]{2,1,0:T(8,128)} %get-tuple-element.89), custom_call_target="InvertDiagBlocksLowerTriangular" | custom-call | tf_op jit(solution)/shard_map/jit(cholesky)/cholesky | solution.py:176
  520.9 11.7 %cholesky.503 = f32[128,128]{1,0:T(8,128)S(1)} custom-call(f32[128,128]{1,0:T(8,128)S(1)} %convolution_subtract_fusion.16), custom_call_target="Cholesky" | custom-call | tf_op jit(solution)/shard_map/jit(cholesky)/cholesky | solution.py:176
  542.1 14.4 %while.7 = (s32[]{:T(128)}, f32[512,512]{0,1:T(8,128)}, s32[4,2]{0,1:T(2,128)S(1)}, f32[4,128,128]{2,1,0:T(8,128)}, s32[]{:T(128)}) while((s32[]{:T(128)}, f32[512,512]{0,1:T(8,128)}, s32[4,2]{0,1:T(2,128)S(1)}, f32[4,128,128]{2,1,0:T(8,128)}, s32[]{:T(128)}) %tuple.89), condition=%wide.while_cond.clone, body=%wide.while_body.clone.sunk | while | flops 2 | bytes 393829 | solution.py:31
  556.4 40.9 %custom-call.38 = f32[4,128,128]{1,2,0:T(8,128)} custom-call(f32[4,128,128]{2,1,0:T(8,128)} %get-tuple-element.26), custom_call_target="InvertDiagBlocksLowerTriangular" | custom-call | tf_op jit(solution)/shard_map/jit(_solve_triangular)/triangular_solve | solution.py:31
  636.5 30.6 %shard_map.51 = f32[32,512]{1,0:T(8,128)} custom-call(f32[512,512]{1,0:T(8,128)} %fusion.163.block_ref), custom_call_target="tpu_custom_call" | custom-call | tf_op jit(solution)/shard_map/pallas_call | solution.py:100
  677.7 55.6 %shard_map.52 = f32[512,1024]{1,0:T(8,128)} custom-call(f32[32,1024]{1,0:T(8,128)} %pad_maximum_fusion.5.block_ref), custom_call_target="tpu_custom_call" | custom-call | tf_op jit(solution)/shard_map/pallas_call | solution.py:119
  740.8 11.7 %cholesky.518 = f32[128,128]{1,0:T(8,128)S(1)} custom-call(f32[128,128]{1,0:T(8,128)S(1)} %cholesky.612), custom_call_target="Cholesky" | custom-call | tf_op jit(solution)/shard_map/jit(cholesky)/cholesky | solution.py:193
  763.2 11.9 %cholesky.537 = f32[128,128]{1,0:T(8,128)S(1)} custom-call(f32[128,128]{1,0:T(8,128)S(1)} %cholesky.616), custom_call_target="Cholesky" | custom-call | tf_op jit(solution)/shard_map/jit(cholesky)/cholesky | solution.py:193
  786.9 11.7 %cholesky.558 = f32[128,128]{1,0:T(8,128)S(1)} custom-call(f32[128,128]{1,0:T(8,128)S(1)} %cholesky.621), custom_call_target="Cholesky" | custom-call | tf_op jit(solution)/shard_map/jit(cholesky)/cholesky | solution.py:193
  799.4 10.2 %custom-call.41 = f32[1,128,128]{1,2,0:T(8,128)S(1)} custom-call(f32[1,128,128]{2,1,0:T(8,128)S(1)} %get-tuple-element.81), custom_call_target="InvertDiagBlocksLowerTriangular" | custom-call | tf_op jit(solution)/shard_map/jit(cholesky)/cholesky | solution.py:193
  810.2 11.7 %cholesky.575 = f32[128,128]{1,0:T(8,128)S(1)} custom-call(f32[128,128]{1,0:T(8,128)S(1)} %convolution_subtract_fusion.15), custom_call_target="Cholesky" | custom-call | tf_op jit(solution)/shard_map/jit(cholesky)/cholesky | solution.py:193
  827.2 14.4 %while.8 = (s32[]{:T(128)}, f32[512,512]{1,0:T(8,128)}, s32[4,2]{0,1:T(2,128)S(1)}, f32[4,128,128]{2,1,0:T(8,128)}, s32[]{:T(128)}) while((s32[]{:T(128)}, f32[512,512]{1,0:T(8,128)}, s32[4,2]{0,1:T(2,128)S(1)}, f32[4,128,128]{2,1,0:T(8,128)}, s32[]{:T(128)}) %tuple.90), condition=%wide.while_cond.clone.1, body=%wide.while_body.clone.1.sunk | while | flops 2 | bytes 132705 | solution.py:31
  841.6 40.3 %custom-call.42 = f32[4,128,128]{1,2,0:T(8,128)S(1)} custom-call(f32[4,128,128]{2,1,0:T(8,128)} %get-tuple-element.27), custom_call_target="InvertDiagBlocksLowerTriangular" | custom-call | tf_op jit(solution)/shard_map/jit(_solve_triangular)/triangular_solve | solution.py:31
  (234 shorter events, 231.3 us)
Async XLA Ops:
  7.2 82.9 %reduce-scatter.4.cloned.1.call-start = ((), (), s32[]{:S(2)}) async-start(), calls=%async_computation.2 | async-start | bytes 3342336
  28.1 112.1 %all-gather.2.cloned.1.call-start = ((), (), s32[]{:S(2)}) async-start(), calls=%async_computation.1 | async-start | bytes 6684672 | tf_op jit(solution)/shard_map/all_gather | solution.py:149
  92.2 197.5 %copy-start.2 = (f32[512,512]{1,0:T(8,128)}, f32[512,512]{1,0:T(8,128)S(1)}, u32[]{:S(2)}) copy-start(f32[512,512]{1,0:T(8,128)S(1)} %fusion.33) | copy-start | bytes 3145732
  148.7 1.0 copy-start.5
  290.5 7.7 slice-start
  290.9 7.3 slice-start.1
  304.6 308.4 %collective-permute-start.2 = (f32[512,512]{1,0:T(8,128)}, f32[512,512]{1,0:T(8,128)}, u32[]{:S(2)}, u32[]{:S(2)}) collective-permute-start(f32[512,512]{1,0:T(8,128)} %fusion), channel_id=1, source_target_pairs={{0,16},{16,0},{32,48},{48,32},{64,80},{80,64},{96,112},{112,96},{1... | collective-permute-start | bytes 3145736 | tf_op jit(solution)/shard_map/ppermute | solution.py:16
  307.8 25.7 %collective-permute-start = (f32[96,512]{1,0:T(8,128)S(1)}, f32[96,512]{1,0:T(8,128)S(1)}, u32[]{:S(2)}, u32[]{:S(2)}) collective-permute-start(f32[96,512]{1,0:T(8,128)S(1)} %fusion.99), channel_id=1, source_target_pairs={{0,16},{16,0},{32,48},{48,32},{64,80},{80,64},{96,112},{112,96},{1... | collective-permute-start | bytes 589832 | tf_op jit(solution)/shard_map/ppermute | solution.py:16
  366.9 4.3 collective-permute-start.1
  437.5 1.0 copy-start.6
  465.0 0.7 copy-start.7
  597.4 5.8 copy-start.8
  597.4 8.3 copy-start
  609.5 24.0 %copy-start.1 = (f32[512,512]{1,0:T(8,128)}, f32[512,512]{1,0:T(8,128)S(1)}, u32[]{:S(2)}) copy-start(f32[512,512]{1,0:T(8,128)S(1)} %fusion.40) | copy-start | bytes 3145732
  619.2 10.7 %collective-permute-start.4 = (f32[96,512]{1,0:T(8,128)S(1)}, f32[96,512]{1,0:T(8,128)S(1)}, u32[]{:S(2)}, u32[]{:S(2)}) collective-permute-start(f32[96,512]{1,0:T(8,128)S(1)} %fusion.97), channel_id=1, source_target_pairs={{0,48},{16,32},{32,16},{48,0},{64,112},{80,96},{96,80},{112,64},{1... | collective-permute-start | bytes 589832 | tf_op jit(solution)/shard_map/ppermute | solution.py:16
  624.8 7.7 collective-permute-start.3
  667.1 4.2 collective-permute-start.5
  672.2 4.9 collective-permute-start.6
  762.8 119.0 %copy-start.3 = (f32[512,512]{1,0:T(8,128)S(1)}, f32[512,512]{1,0:T(8,128)}, u32[]{:S(2)}) copy-start(f32[512,512]{1,0:T(8,128)} %copy-done.2) | copy-start | bytes 3145732
  841.6 46.1 %copy-start.4 = (f32[512,1024]{1,0:T(8,128)S(1)}, f32[512,1024]{1,0:T(8,128)}, u32[]{:S(2)}) copy-start(f32[512,1024]{1,0:T(8,128)} %shard_map.52) | copy-start | bytes 6291460
Sparse Core Ops, SparseCore 0:
  28.2 61.7 reduce-scatter.3
  92.2 47.9 all-gather.1

commit v4 on v3

--- a/solution.py
+++ b/solution.py
@@ -29,6 +29,44 @@
 def inverse_lower(factor):
     eye = jnp.eye(factor.shape[0], dtype=factor.dtype)
     return jax.scipy.linalg.solve_triangular(factor, eye, lower=True)
+
+
+def join_lower(upper_left, lower_left, lower_right):
+    top = jnp.concatenate([upper_left, jnp.zeros_like(upper_left)], axis=1)
+    return jnp.concatenate([top, jnp.concatenate([lower_left, lower_right], axis=1)], axis=0)
+
+
+def factor_pair(gram, block=128):
+    size = gram.shape[0]
+    panels = []
+    inverses = []
+    for start in range(0, size, block):
+        stop = start + block
+        column = gram[start:, start:stop]
+        if panels:
+            done = jnp.concatenate(panels, axis=1)
+            column = column - product(done[start:], done[start:stop].T)
+        diagonal = jnp.linalg.cholesky(column[:block])
+        inverse = inverse_lower(diagonal)
+        inverses.append(inverse)
+        below = product(column[block:], inverse.T)
+        panel = jnp.concatenate([diagonal, below], axis=0)
+        if start:
+            panel = jnp.concatenate([jnp.zeros((start, block), gram.dtype), panel], axis=0)
+        panels.append(panel)
+    factor = jnp.concatenate(panels, axis=1)
+    width = block
+    while len(inverses) > 1:
+        merged = []
+        for pair in range(0, len(inverses), 2):
+            first, second = inverses[pair], inverses[pair + 1]
+            lo = pair * width
+            coupling = factor[lo + width:lo + 2 * width, lo:lo + width]
+            lower_left = -product(second, product(coupling, first))
+            merged.append(join_lower(first, lower_left, second))
+        inverses = merged
+        width *= 2
+    return factor, inverses[0]
 
 
 MESH = pl.DeviceIdType.MESH
@@ -108,7 +146,7 @@
             pltpu.SemaphoreType.DMA((count,)),
         ],
         compiler_params=pltpu.CompilerParams(
-            collective_id=ident, has_side_effects=True
+            collective_id=ident
         ),
     )(block)
 
@@ -127,7 +165,7 @@
             pltpu.SemaphoreType.DMA((count,)),
         ],
         compiler_params=pltpu.CompilerParams(
-            collective_id=ident, has_side_effects=True
+            collective_id=ident
         ),
     )(block)
 
@@ -151,8 +189,8 @@
     )
     local = both[:, :rank_size]
     omega = both[:, rank_size:]
-    factor = jnp.linalg.cholesky(transposed(local, local))
-    basis = product(local, inverse_lower(factor).T)
+    factor, factor_inverse = factor_pair(transposed(local, local))
+    basis = product(local, factor_inverse.T)
     reduced = transposed(basis, omega)
     basis_rows = lax.dynamic_slice_in_dim(basis, tile * slice_cols, slice_cols, 0)
 
@@ -173,10 +211,10 @@
     other_part = swap(sample_part, "node", 1)
     pair = tile_gather(jnp.concatenate([sample_part, other_part], axis=1), 4)
     parent_sample, other_sample = pair[:, :rank_size], pair[:, rank_size:]
-    parent_factor = jnp.linalg.cholesky(
+    parent_factor, parent_inverse = factor_pair(
         transposed(parent_sample, parent_sample) + transposed(other_sample, other_sample)
     )
-    parent_inverse = inverse_lower(parent_factor).T
+    parent_inverse = parent_inverse.T
     transfer_own = product(parent_sample, parent_inverse)
     transfer_other = product(other_sample, parent_inverse)
     parent_reduced = transposed(transfer_own, reduced) + transposed(transfer_other, other_reduced)
@@ -190,10 +228,10 @@
     cousin_part = swap(grand_part, "node", 2)
     grand_pair = tile_gather(jnp.concatenate([grand_part, cousin_part], axis=1), 6)
     grand_sample, cousin_grand = grand_pair[:, :rank_size], grand_pair[:, rank_size:]
-    grand_factor = jnp.linalg.cholesky(
+    grand_factor, grand_inverse = factor_pair(
         transposed(grand_sample, grand_sample) + transposed(cousin_grand, cousin_grand)
     )
-    grand_transfer = product(grand_sample, inverse_lower(grand_factor).T)
+    grand_transfer = product(grand_sample, grand_inverse.T)
     leaf_out = (basis_rows * math.sqrt(leaf_rows))[None]
     one_rows = lax.dynamic_slice_in_dim(transfer_own, tile * out_rows, out_rows, 0)
     level_one = (one_rows * math.sqrt(2 * rank_size))[None]

time: 904 us -> 848 us (0.938)
  other arithmetic: 374 us -> 317 us
  matrix products: 125 us -> 141 us
    another operation x44 -> x36, other arithmetic: 241 us -> 159 us  [factor_pair(): diagonal = jnp.linalg.cholesky(column[:block])]
    dot_general x11 -> x47, matrix products: 29.1 us -> 67.1 us  [product(): jnp.dot(left, right, precision=HIGH, preferred_element_type=jnp.float32)]
    another operation x56 -> x14, local copies, waits for them, and re-layouts: 38.6 us -> 9.23 us  [inverse_lower(): return jax.scipy.linalg.solve_triangular(factor, eye, lower=True)]
    another operation x18 -> x0, matrix products: 17.5 us -> none  [the longest x6 9.44 us: on_device(): jnp.linalg.cholesky(transposed(parent_sample, parent_sample) + transposed...]
    another operation x7 -> x24, other arithmetic: 126 us -> 139 us  [inverse_lower(): return jax.scipy.linalg.solve_triangular(factor, eye, lower=True)]
    another operation x21 -> x12, matrix products: 17.3 us -> 7.27 us  [inverse_lower(): return jax.scipy.linalg.solve_triangular(factor, eye, lower=True)]
  transfers between devices with their start and end apart: 9 -> 9, of which waited for: 7 -> 7; matrix products, arithmetic and copies ran while one was open for 23% -> 24% of each run, Pallas kernels for 9% -> 10%
where the time goes in v4:
time: 848 us; the launch traced here: 841 us
  other arithmetic  317 us (37%)
  Pallas kernels  170 us (20%)
  waiting for transfers between devices  143 us (17%)
  matrix products  141 us (17%)
  local copies, waits for them, and re-layouts  47.9 us (6%)
  between operations  15.7 us (2%)
    another operation x36, other arithmetic, factor_pair(): diagonal = jnp.linalg.cholesky(column[:block])  159 us
    another operation x24, other arithmetic, inverse_lower(): return jax.scipy.linalg.solve_triangular(factor, eye, lower=True)  139 us
    pallas_call x2, Pallas kernels, tile_gather(): pl.pallas_call(functools.partial(gather_kernel, count), out_shape=jax.Sha...  109 us
    dot_general x47, matrix products, product(): jnp.dot(left, right, precision=HIGH, preferred_element_type=jnp.float32)  67.1 us
    dot_general x13, matrix products, transposed(): lax.dot_general(left, right, (((0,), (0,)), ((), ())), precision=HIGH, pr...  66.3 us
    pallas_call x2, Pallas kernels, tile_scatter(): pl.pallas_call(functools.partial(scatter_kernel, count), out_shape=jax.Sh...  61.1 us
    unnamed x3, waiting for transfers between devices  60.7 us
    all_gather x1, waiting for transfers between devices, on_device(): lax.all_gather(jnp.concatenate([sample_rows, owned], axis=1), 'tile', axi...  48.1 us
  transfers between devices with their start and end apart: 9, of which 7 were waited for; matrix products, arithmetic and copies ran while one was open for 24% of the time, Pallas kernels for 10%

profile of v4, /device:TPU:1, one launch (start us, length us, event | category | flops | bytes accessed | tf_op | source)
XLA Modules:
  0.0 841.3 jit_solution(14664970065244114305)
XLA Ops:
  7.2 18.4 %convolution_bitcast_fusion = f32[1536,512]{0,1:T(8,128)S(1)} fusion(f32[16,96,1536]{2,1,0:T(8,128)} %param.5, f32[16,96,512]{2,1,0:T(8,128)} %param.6, pred[16]{0:T(512)(128)(4,1)S(1)} %iota_compare_fusion.20), kind=kOutput, calls=%fused_computation | convolution fusion | flops 14496301056 | bytes 15728656 | tf_op jit(solution)/shard_map/dot_general | solution.py:24
  29.4 60.6 %reduce-scatter.4.cloned.1.call-done = f32[96,512]{1,0:T(8,128)} async-done(((f32[1536,512]{1,0:T(8,128)}), f32[96,512]{1,0:T(8,128)}) %reduce-scatter.4.cloned.1.call-update) | async-done | bytes 196624
  92.1 48.1 %all-gather.2.cloned.1.call-done = f32[1536,1024]{1,0:T(8,128)} async-done(((f32[96,1024]{1,0:T(8,128)}), f32[1536,1024]{1,0:T(8,128)}) %all-gather.2.cloned.1.call-update) | async-done | bytes 6291472 | tf_op jit(solution)/shard_map/all_gather | solution.py:187
  148.4 11.7 %cholesky.194 = f32[128,128]{1,0:T(8,128)S(1)} custom-call(f32[128,128]{1,0:T(8,128)S(1)} %get-tuple-element.28), custom_call_target="Cholesky" | custom-call | tf_op jit(solution)/shard_map/jit(cholesky)/cholesky | solution.py:49
  161.7 9.8 %custom-call.16 = f32[1,128,128]{1,2,0:T(8,128)S(1)} custom-call(f32[1,128,128]{2,1,0:T(8,128)S(1)} %copy.90), custom_call_target="InvertDiagBlocksLowerTriangular" | custom-call | tf_op jit(solution)/shard_map/jit(_solve_triangular)/triangular_solve | solution.py:31
  173.4 11.7 %cholesky.205 = f32[128,128]{1,0:T(8,128)S(1)} custom-call(f32[128,128]{1,0:T(8,128)S(1)} %fusion.203), custom_call_target="Cholesky" | custom-call | tf_op jit(solution)/shard_map/jit(cholesky)/cholesky | solution.py:49
  186.7 9.8 %custom-call.17 = f32[1,128,128]{1,2,0:T(8,128)S(1)} custom-call(f32[1,128,128]{2,1,0:T(8,128)S(1)} %copy.96), custom_call_target="InvertDiagBlocksLowerTriangular" | custom-call | tf_op jit(solution)/shard_map/jit(_solve_triangular)/triangular_solve | solution.py:31
  198.0 11.7 %cholesky.216 = f32[128,128]{1,0:T(8,128)S(1)} custom-call(f32[128,128]{1,0:T(8,128)S(1)} %fusion.201), custom_call_target="Cholesky" | custom-call | tf_op jit(solution)/shard_map/jit(cholesky)/cholesky | solution.py:49
  211.3 10.2 %custom-call.18 = f32[1,128,128]{1,2,0:T(8,128)S(1)} custom-call(f32[1,128,128]{2,1,0:T(8,128)S(1)} %copy.106), custom_call_target="InvertDiagBlocksLowerTriangular" | custom-call | tf_op jit(solution)/shard_map/jit(_solve_triangular)/triangular_solve | solution.py:31
  224.9 11.7 %cholesky.227 = f32[128,128]{1,0:T(8,128)S(1)} custom-call(f32[128,128]{1,0:T(8,128)S(1)} %fusion.199), custom_call_target="Cholesky" | custom-call | tf_op jit(solution)/shard_map/jit(cholesky)/cholesky | solution.py:49
  238.8 9.8 %custom-call.19 = f32[1,128,128]{1,2,0:T(8,128)S(1)} custom-call(f32[1,128,128]{2,1,0:T(8,128)S(1)} %copy.113), custom_call_target="InvertDiagBlocksLowerTriangular" | custom-call | tf_op jit(solution)/shard_map/jit(_solve_triangular)/triangular_solve | solution.py:31
  257.4 12.4 %fusion = f32[512,512]{1,0:T(8,128)} fusion(f32[1536,512]{1,0:T(8,128)S(1)} %fusion.3, f32[1536,1024]{1,0:T(8,128)} %all-gather.2.cloned.1.call-done), kind=kOutput, calls=%fused_computation.1 | convolution fusion | flops 4831838208 | bytes 7340032 | tf_op jit(solution)/shard_map/dot_general | solution.py:24
  276.3 22.4 %collective-permute-done = f32[96,512]{1,0:T(8,128)S(1)} collective-permute-done((f32[96,512]{1,0:T(8,128)S(1)}, f32[96,512]{1,0:T(8,128)S(1)}, u32[]{:S(2)}, u32[]{:S(2)}) %collective-permute-start) | collective-permute-done | bytes 196640 | tf_op jit(solution)/shard_map/ppermute | solution.py:16
  300.7 30.5 %shard_map.49 = f32[32,512]{1,0:T(8,128)} custom-call(f32[512,512]{1,0:T(8,128)} %fusion.247.block_ref), custom_call_target="tpu_custom_call" | custom-call | tf_op jit(solution)/shard_map/pallas_call | solution.py:138
  338.2 53.1 %shard_map.50 = f32[512,1024]{1,0:T(8,128)} custom-call(f32[32,1024]{1,0:T(8,128)} %pad_maximum_fusion.16.block_ref), custom_call_target="tpu_custom_call" | custom-call | tf_op jit(solution)/shard_map/pallas_call | solution.py:157
  400.2 11.7 %cholesky.238 = f32[128,128]{1,0:T(8,128)S(1)} custom-call(f32[128,128]{1,0:T(8,128)S(1)} %fusion.197), custom_call_target="Cholesky" | custom-call | tf_op jit(solution)/shard_map/jit(cholesky)/cholesky | solution.py:49
  414.2 10.0 %custom-call.20 = f32[1,128,128]{1,2,0:T(8,128)S(1)} custom-call(f32[1,128,128]{2,1,0:T(8,128)S(1)} %copy.121), custom_call_target="InvertDiagBlocksLowerTriangular" | custom-call | tf_op jit(solution)/shard_map/jit(_solve_triangular)/triangular_solve | solution.py:31
  435.8 13.2 %cholesky.249 = f32[128,128]{1,0:T(8,128)} custom-call(f32[128,128]{1,0:T(8,128)} %fusion.195), custom_call_target="Cholesky" | custom-call | tf_op jit(solution)/shard_map/jit(cholesky)/cholesky | solution.py:49
  455.9 11.3 %custom-call.21 = f32[1,128,128]{1,2,0:T(8,128)} custom-call(f32[1,128,128]{2,1,0:T(8,128)} %copy.126), custom_call_target="InvertDiagBlocksLowerTriangular" | custom-call | tf_op jit(solution)/shard_map/jit(_solve_triangular)/triangular_solve | solution.py:31
  479.7 13.5 %cholesky.260 = f32[128,128]{1,0:T(8,128)} custom-call(f32[128,128]{1,0:T(8,128)} %fusion.193), custom_call_target="Cholesky" | custom-call | tf_op jit(solution)/shard_map/jit(cholesky)/cholesky | solution.py:49
  500.2 11.3 %custom-call.22 = f32[1,128,128]{1,2,0:T(8,128)} custom-call(f32[1,128,128]{2,1,0:T(8,128)} %copy.135), custom_call_target="InvertDiagBlocksLowerTriangular" | custom-call | tf_op jit(solution)/shard_map/jit(_solve_triangular)/triangular_solve | solution.py:31
  528.5 13.2 %cholesky.271 = f32[128,128]{1,0:T(8,128)} custom-call(f32[128,128]{1,0:T(8,128)} %fusion.191), custom_call_target="Cholesky" | custom-call | tf_op jit(solution)/shard_map/jit(cholesky)/cholesky | solution.py:49
  548.4 11.3 %custom-call.23 = f32[1,128,128]{1,2,0:T(8,128)} custom-call(f32[1,128,128]{2,1,0:T(8,128)} %copy.141), custom_call_target="InvertDiagBlocksLowerTriangular" | custom-call | tf_op jit(solution)/shard_map/jit(_solve_triangular)/triangular_solve | solution.py:31
  597.1 30.7 %shard_map.51 = f32[32,512]{1,0:T(8,128)} custom-call(f32[512,512]{1,0:T(8,128)} %fusion.252.block_ref), custom_call_target="tpu_custom_call" | custom-call | tf_op jit(solution)/shard_map/pallas_call | solution.py:138
  638.6 55.6 %shard_map.52 = f32[512,1024]{1,0:T(8,128)} custom-call(f32[32,1024]{1,0:T(8,128)} %pad_maximum_fusion.17.block_ref), custom_call_target="tpu_custom_call" | custom-call | tf_op jit(solution)/shard_map/pallas_call | solution.py:157
  701.3 11.7 %cholesky.282 = f32[128,128]{1,0:T(8,128)S(1)} custom-call(f32[128,128]{1,0:T(8,128)S(1)} %fusion.189), custom_call_target="Cholesky" | custom-call | tf_op jit(solution)/shard_map/jit(cholesky)/cholesky | solution.py:49
  714.3 9.8 %custom-call.24 = f32[1,128,128]{1,2,0:T(8,128)S(1)} custom-call(f32[1,128,128]{2,1,0:T(8,128)S(1)} %get-tuple-element.9), custom_call_target="InvertDiagBlocksLowerTriangular" | custom-call | tf_op jit(solution)/shard_map/jit(_solve_triangular)/triangular_solve | solution.py:31
  726.4 11.9 %cholesky.293 = f32[128,128]{1,0:T(8,128)S(1)} custom-call(f32[128,128]{1,0:T(8,128)S(1)} %fusion.187), custom_call_target="Cholesky" | custom-call | tf_op jit(solution)/shard_map/jit(cholesky)/cholesky | solution.py:49
  739.8 9.8 %custom-call.25 = f32[1,128,128]{1,2,0:T(8,128)S(1)} custom-call(f32[1,128,128]{2,1,0:T(8,128)S(1)} %get-tuple-element.7), custom_call_target="InvertDiagBlocksLowerTriangular" | custom-call | tf_op jit(solution)/shard_map/jit(_solve_triangular)/triangular_solve | solution.py:31
  757.9 13.2 %cholesky.304 = f32[128,128]{1,0:T(8,128)} custom-call(f32[128,128]{1,0:T(8,128)} %fusion.185), custom_call_target="Cholesky" | custom-call | tf_op jit(solution)/shard_map/jit(cholesky)/cholesky | solution.py:49
  774.7 11.5 %custom-call.26 = f32[1,128,128]{1,2,0:T(8,128)} custom-call(f32[1,128,128]{2,1,0:T(8,128)} %get-tuple-element.5), custom_call_target="InvertDiagBlocksLowerTriangular" | custom-call | tf_op jit(solution)/shard_map/jit(_solve_triangular)/triangular_solve | solution.py:31
  803.5 11.7 %cholesky.315 = f32[128,128]{1,0:T(8,128)S(1)} custom-call(f32[128,128]{1,0:T(8,128)S(1)} %fusion.183), custom_call_target="Cholesky" | custom-call | tf_op jit(solution)/shard_map/jit(cholesky)/cholesky | solution.py:49
  (279 shorter events, 232.4 us)
Async XLA Ops:
  7.2 82.9 %reduce-scatter.4.cloned.1.call-start = ((), (), s32[]{:S(2)}) async-start(), calls=%async_computation.2 | async-start | bytes 3342336
  28.1 112.2 %all-gather.2.cloned.1.call-start = ((), (), s32[]{:S(2)}) async-start(), calls=%async_computation.1 | async-start | bytes 6684672 | tf_op jit(solution)/shard_map/all_gather | solution.py:187
  161.6 62.6 %copy-start.12 = (f32[128,128]{0,1:T(8,128)}, f32[128,128]{0,1:T(8,128)S(1)}, u32[]{:S(2)}) copy-start(f32[128,128]{0,1:T(8,128)S(1)} %get-tuple-element.26) | copy-start | bytes 196612
  186.6 37.6 %copy-start.13 = (f32[128,128]{0,1:T(8,128)}, f32[128,128]{0,1:T(8,128)S(1)}, u32[]{:S(2)}) copy-start(f32[128,128]{0,1:T(8,128)S(1)} %get-tuple-element.24) | copy-start | bytes 196612
  197.1 27.6 %copy-start.7 = (f32[256,128]{0,1:T(8,128)}, f32[256,128]{0,1:T(8,128)S(1)}, u32[]{:S(2)}) copy-start(f32[256,128]{0,1:T(8,128)S(1)} %fusion.155) | copy-start | bytes 393220
  211.2 38.1 %copy-start.22 = (f32[128,128]{0,1:T(8,128)}, f32[128,128]{0,1:T(8,128)S(1)}, u32[]{:S(2)}) copy-start(f32[128,128]{0,1:T(8,128)S(1)} %get-tuple-element.22) | copy-start | bytes 196612
  222.5 26.9 %copy-start.23 = (f32[128,128]{0,1:T(8,128)}, f32[128,128]{0,1:T(8,128)S(1)}, u32[]{:S(2)}) copy-start(f32[128,128]{0,1:T(8,128)S(1)} %copy.108) | copy-start | bytes 196612
  222.5 26.9 %copy-start.10 = (f32[128,256]{1,0:T(8,128)}, f32[128,256]{1,0:T(8,128)S(1)}, u32[]{:S(2)}) copy-start(f32[128,256]{1,0:T(8,128)S(1)} %concatenate.158) | copy-start | bytes 393220
  269.8 304.8 %collective-permute-start.2 = (f32[512,512]{1,0:T(8,128)}, f32[512,512]{1,0:T(8,128)}, u32[]{:S(2)}, u32[]{:S(2)}) collective-permute-start(f32[512,512]{1,0:T(8,128)} %fusion), channel_id=1, source_target_pairs={{0,16},{16,0},{32,48},{48,32},{64,80},{80,64},{96,112},{112,96},{1... | collective-permute-start | bytes 3145736 | tf_op jit(solution)/shard_map/ppermute | solution.py:16
  273.0 25.7 %collective-permute-start = (f32[96,512]{1,0:T(8,128)S(1)}, f32[96,512]{1,0:T(8,128)S(1)}, u32[]{:S(2)}, u32[]{:S(2)}) collective-permute-start(f32[96,512]{1,0:T(8,128)S(1)} %fusion.146), channel_id=1, source_target_pairs={{0,16},{16,0},{32,48},{48,32},{64,80},{80,64},{96,112},{112,96},{1... | collective-permute-start | bytes 589832 | tf_op jit(solution)/shard_map/ppermute | solution.py:16
  332.1 5.4 collective-permute-start.1
  398.3 1.0 copy-start.3
  424.4 1.5 copy-start.8
  425.9 0.7 copy-start.6
  473.3 0.8 copy-start.4
  512.6 1.2 copy-start.15
  563.0 6.2 copy-start.1
  563.0 6.2 copy-start.28
  563.0 6.2 copy-start.29
  563.0 6.2 copy-start.30
  571.0 23.1 %copy-start = (f32[512,512]{1,0:T(8,128)}, f32[512,512]{1,0:T(8,128)S(1)}, u32[]{:S(2)}) copy-start(f32[512,512]{1,0:T(8,128)S(1)} %fusion.35) | copy-start | bytes 3145732
  579.6 7.9 copy-start.20
  580.4 7.1 collective-permute-start.4
  585.4 7.7 collective-permute-start.3
  627.8 4.2 collective-permute-start.5
  632.8 5.1 collective-permute-start.6
  724.4 26.7 %copy-start.9 = (f32[128,128]{1,0:T(8,128)}, f32[128,128]{1,0:T(8,128)S(1)}, u32[]{:S(2)}) copy-start(f32[128,128]{1,0:T(8,128)S(1)} %fusion.63) | copy-start | bytes 196612
  749.8 1.3 copy-start.16
  750.2 1.0 copy-start.11
  752.3 0.8 copy-start.5
  753.1 76.1 %copy-start.2 = (f32[512,1024]{1,0:T(8,128)S(1)}, f32[512,1024]{1,0:T(8,128)}, u32[]{:S(2)}) copy-start(f32[512,1024]{1,0:T(8,128)} %shard_map.52) | copy-start | bytes 6291460
  787.3 1.2 copy-start.14
  (8 other events, 5.1 us)
Sparse Core Ops, SparseCore 0:
  28.2 61.7 reduce-scatter.3
  92.2 47.9 all-gather.1

commit v5 on v4

--- a/solution.py
+++ b/solution.py
@@ -200,16 +200,19 @@
 
     panel_one = product(basis_rows, reduced)
     sibling_rows = swap(panel_one, "node", 1)
-    other_reduced = swap(reduced, "node", 1)
     near_meet = meet(jnp.bitwise_xor(node, 1))
     cousin_meet = meet(jnp.bitwise_xor(node, 2))
     further_meet = meet(jnp.bitwise_xor(node, 3))
 
     near_part = tile_scatter(transposed(near_meet, sibling_rows), 3)
+    late_reduced, near_part = lax.optimization_barrier((reduced, near_part))
+    other_reduced = swap(late_reduced, "node", 1)
     chunk = near_part.shape[0]
     sample_part = lax.dynamic_slice_in_dim(factor.T, tile * chunk, chunk, 0) - near_part
     other_part = swap(sample_part, "node", 1)
-    pair = tile_gather(jnp.concatenate([sample_part, other_part], axis=1), 4)
+    pair = lax.all_gather(
+        jnp.concatenate([sample_part, other_part], axis=1), "tile", axis=0, tiled=True
+    )
     parent_sample, other_sample = pair[:, :rank_size], pair[:, rank_size:]
     parent_factor, parent_inverse = factor_pair(
         transposed(parent_sample, parent_sample) + transposed(other_sample, other_sample)
@@ -226,7 +229,9 @@
     far_pair = far_part + swap(far_part, "node", 1)
     grand_part = lax.dynamic_slice_in_dim(parent_factor.T, tile * chunk, chunk, 0) - far_pair
     cousin_part = swap(grand_part, "node", 2)
-    grand_pair = tile_gather(jnp.concatenate([grand_part, cousin_part], axis=1), 6)
+    grand_pair = lax.all_gather(
+        jnp.concatenate([grand_part, cousin_part], axis=1), "tile", axis=0, tiled=True
+    )
     grand_sample, cousin_grand = grand_pair[:, :rank_size], grand_pair[:, rank_size:]
     grand_factor, grand_inverse = factor_pair(
         transposed(grand_sample, grand_sample) + transposed(cousin_grand, cousin_grand)

time: 848 us -> 779 us (0.919)
  Pallas kernels: 170 us -> 61.3 us
  waiting for transfers between devices: 143 us -> 198 us
    pallas_call x2 -> x0, Pallas kernels: 109 us -> none  [tile_gather(): pl.pallas_call(functools.partial(gather_kernel, count), out_shape=jax.Sha...]
    all_gather x0 -> x2, waiting for transfers between devices: none -> 71.4 us  [the longest x1 37.6 us: on_device(): lax.all_gather(jnp.concatenate([grand_part, cousin_part], axis=1), 'tile'...]
    ppermute x7, waiting for transfers between devices: 34.3 us -> 18.1 us  [swap(): lax.ppermute(block, axis, [(low, low ^ mask) for low in range(count)])]
    unnamed x3 -> x5, waiting for transfers between devices: 60.7 us -> 60.9 us
  transfers between devices with their start and end apart: 9 -> 11, of which waited for: 7 -> 10; matrix products, arithmetic and copies ran while one was open for 24% -> 25% of each run, Pallas kernels for 10% -> 0%
where the time goes in v5:
time: 779 us; the launch traced here: 773 us
  other arithmetic  311 us (40%)
  waiting for transfers between devices  198 us (25%)
  matrix products  137 us (18%)
  Pallas kernels  61.3 us (8%)
  local copies, waits for them, and re-layouts  40.9 us (5%)
  between operations  15.4 us (2%)
  starting transfers between devices  9.46 us (1%)
    another operation x36, other arithmetic, factor_pair(): diagonal = jnp.linalg.cholesky(column[:block])  157 us
    another operation x24, other arithmetic, inverse_lower(): return jax.scipy.linalg.solve_triangular(factor, eye, lower=True)  137 us
    dot_general x13, matrix products, transposed(): lax.dot_general(left, right, (((0,), (0,)), ((), ())), precision=HIGH, pr...  66.3 us
    dot_general x47, matrix products, product(): jnp.dot(left, right, precision=HIGH, preferred_element_type=jnp.float32)  63.8 us
    pallas_call x2, Pallas kernels, tile_scatter(): pl.pallas_call(functools.partial(scatter_kernel, count), out_shape=jax.Sh...  61.3 us
    unnamed x5, waiting for transfers between devices  60.9 us
    all_gather x1, waiting for transfers between devices, on_device(): lax.all_gather(jnp.concatenate([sample_rows, owned], axis=1), 'tile', axi...  47.9 us
    all_gather x1, waiting for transfers between devices, on_device(): lax.all_gather(jnp.concatenate([grand_part, cousin_part], axis=1), 'tile'...  37.6 us
  transfers between devices with their start and end apart: 11, of which 10 were waited for; matrix products, arithmetic and copies ran while one was open for 25% of the time, Pallas kernels for 0%

profile of v5, /device:TPU:1, one launch (start us, length us, event | category | flops | bytes accessed | tf_op | source)
XLA Modules:
  0.0 772.6 jit_solution(1718526902815098112)
XLA Ops:
  7.2 18.4 %convolution_bitcast_fusion = f32[1536,512]{0,1:T(8,128)S(1)} fusion(f32[16,96,1536]{2,1,0:T(8,128)} %param.5, f32[16,96,512]{2,1,0:T(8,128)} %param.6, pred[16]{0:T(512)(128)(4,1)S(1)} %iota_compare_fusion.20), kind=kOutput, calls=%fused_computation | convolution fusion | flops 14496301056 | bytes 15728656 | tf_op jit(solution)/shard_map/dot_general | solution.py:24
  29.2 60.8 %reduce-scatter.4.cloned.1.call-done = f32[96,512]{1,0:T(8,128)} async-done(((f32[1536,512]{1,0:T(8,128)}), f32[96,512]{1,0:T(8,128)}) %reduce-scatter.4.cloned.1.call-update) | async-done | bytes 196624
  92.3 47.9 %all-gather.4.cloned.1.call-done = f32[1536,1024]{1,0:T(8,128)} async-done(((f32[96,1024]{1,0:T(8,128)}), f32[1536,1024]{1,0:T(8,128)}) %all-gather.4.cloned.1.call-update) | async-done | bytes 6291472 | tf_op jit(solution)/shard_map/all_gather | solution.py:187
  148.4 11.7 %cholesky.194 = f32[128,128]{1,0:T(8,128)S(1)} custom-call(f32[128,128]{1,0:T(8,128)S(1)} %get-tuple-element.32), custom_call_target="Cholesky" | custom-call | tf_op jit(solution)/shard_map/jit(cholesky)/cholesky | solution.py:49
  161.7 9.8 %custom-call.16 = f32[1,128,128]{1,2,0:T(8,128)S(1)} custom-call(f32[1,128,128]{2,1,0:T(8,128)S(1)} %copy.90), custom_call_target="InvertDiagBlocksLowerTriangular" | custom-call | tf_op jit(solution)/shard_map/jit(_solve_triangular)/triangular_solve | solution.py:31
  173.4 11.7 %cholesky.205 = f32[128,128]{1,0:T(8,128)S(1)} custom-call(f32[128,128]{1,0:T(8,128)S(1)} %fusion.203), custom_call_target="Cholesky" | custom-call | tf_op jit(solution)/shard_map/jit(cholesky)/cholesky | solution.py:49
  186.7 9.8 %custom-call.17 = f32[1,128,128]{1,2,0:T(8,128)S(1)} custom-call(f32[1,128,128]{2,1,0:T(8,128)S(1)} %copy.96), custom_call_target="InvertDiagBlocksLowerTriangular" | custom-call | tf_op jit(solution)/shard_map/jit(_solve_triangular)/triangular_solve | solution.py:31
  198.0 11.7 %cholesky.216 = f32[128,128]{1,0:T(8,128)S(1)} custom-call(f32[128,128]{1,0:T(8,128)S(1)} %fusion.201), custom_call_target="Cholesky" | custom-call | tf_op jit(solution)/shard_map/jit(cholesky)/cholesky | solution.py:49
  211.3 10.3 %custom-call.18 = f32[1,128,128]{1,2,0:T(8,128)S(1)} custom-call(f32[1,128,128]{2,1,0:T(8,128)S(1)} %copy.106), custom_call_target="InvertDiagBlocksLowerTriangular" | custom-call | tf_op jit(solution)/shard_map/jit(_solve_triangular)/triangular_solve | solution.py:31
  224.9 11.7 %cholesky.227 = f32[128,128]{1,0:T(8,128)S(1)} custom-call(f32[128,128]{1,0:T(8,128)S(1)} %fusion.199), custom_call_target="Cholesky" | custom-call | tf_op jit(solution)/shard_map/jit(cholesky)/cholesky | solution.py:49
  238.8 9.8 %custom-call.19 = f32[1,128,128]{1,2,0:T(8,128)S(1)} custom-call(f32[1,128,128]{2,1,0:T(8,128)S(1)} %copy.113), custom_call_target="InvertDiagBlocksLowerTriangular" | custom-call | tf_op jit(solution)/shard_map/jit(_solve_triangular)/triangular_solve | solution.py:31
  257.4 12.4 %fusion = f32[512,512]{1,0:T(8,128)} fusion(f32[1536,512]{1,0:T(8,128)S(1)} %fusion.3, f32[1536,1024]{1,0:T(8,128)} %all-gather.4.cloned.1.call-done), kind=kOutput, calls=%fused_computation.1 | convolution fusion | flops 4831838208 | bytes 7340032 | tf_op jit(solution)/shard_map/dot_general | solution.py:24
  280.1 30.5 %shard_map.49 = f32[32,512]{1,0:T(8,128)} custom-call(f32[512,512]{1,0:T(8,128)} %fusion.247.block_ref), custom_call_target="tpu_custom_call" | custom-call | tf_op jit(solution)/shard_map/pallas_call | solution.py:138
  321.6 33.8 %all-gather.6.cloned.1.call-done = f32[512,1024]{1,0:T(8,128)} async-done(((f32[32,1024]{1,0:T(8,128)}), f32[512,1024]{1,0:T(8,128)}) %all-gather.6.cloned.1.call-update) | async-done | bytes 2097168 | tf_op jit(solution)/shard_map/all_gather | solution.py:213
  364.3 11.7 %cholesky.238 = f32[128,128]{1,0:T(8,128)S(1)} custom-call(f32[128,128]{1,0:T(8,128)S(1)} %fusion.197), custom_call_target="Cholesky" | custom-call | tf_op jit(solution)/shard_map/jit(cholesky)/cholesky | solution.py:49
  378.3 9.8 %custom-call.20 = f32[1,128,128]{1,2,0:T(8,128)S(1)} custom-call(f32[1,128,128]{2,1,0:T(8,128)S(1)} %copy.121), custom_call_target="InvertDiagBlocksLowerTriangular" | custom-call | tf_op jit(solution)/shard_map/jit(_solve_triangular)/triangular_solve | solution.py:31
  399.8 13.3 %cholesky.249 = f32[128,128]{1,0:T(8,128)} custom-call(f32[128,128]{1,0:T(8,128)} %fusion.195), custom_call_target="Cholesky" | custom-call | tf_op jit(solution)/shard_map/jit(cholesky)/cholesky | solution.py:49
  420.0 11.3 %custom-call.21 = f32[1,128,128]{1,2,0:T(8,128)} custom-call(f32[1,128,128]{2,1,0:T(8,128)} %copy.126), custom_call_target="InvertDiagBlocksLowerTriangular" | custom-call | tf_op jit(solution)/shard_map/jit(_solve_triangular)/triangular_solve | solution.py:31
  443.9 13.2 %cholesky.260 = f32[128,128]{1,0:T(8,128)} custom-call(f32[128,128]{1,0:T(8,128)} %fusion.193), custom_call_target="Cholesky" | custom-call | tf_op jit(solution)/shard_map/jit(cholesky)/cholesky | solution.py:49
  464.0 11.6 %custom-call.22 = f32[1,128,128]{1,2,0:T(8,128)} custom-call(f32[1,128,128]{2,1,0:T(8,128)} %copy.135), custom_call_target="InvertDiagBlocksLowerTriangular" | custom-call | tf_op jit(solution)/shard_map/jit(_solve_triangular)/triangular_solve | solution.py:31
  492.6 13.2 %cholesky.271 = f32[128,128]{1,0:T(8,128)} custom-call(f32[128,128]{1,0:T(8,128)} %fusion.191), custom_call_target="Cholesky" | custom-call | tf_op jit(solution)/shard_map/jit(cholesky)/cholesky | solution.py:49
  512.5 11.3 %custom-call.23 = f32[1,128,128]{1,2,0:T(8,128)} custom-call(f32[1,128,128]{2,1,0:T(8,128)} %copy.141), custom_call_target="InvertDiagBlocksLowerTriangular" | custom-call | tf_op jit(solution)/shard_map/jit(_solve_triangular)/triangular_solve | solution.py:31
  561.5 30.8 %shard_map.50 = f32[32,512]{1,0:T(8,128)} custom-call(f32[512,512]{1,0:T(8,128)} %fusion.252.block_ref), custom_call_target="tpu_custom_call" | custom-call | tf_op jit(solution)/shard_map/pallas_call | solution.py:138
  605.4 37.6 %all-gather.8.cloned.1.call-done = f32[512,1024]{1,0:T(8,128)} async-done(((f32[32,1024]{1,0:T(8,128)}), f32[512,1024]{1,0:T(8,128)}) %all-gather.8.cloned.1.call-update) | async-done | bytes 2097168 | tf_op jit(solution)/shard_map/all_gather | solution.py:232
  650.0 11.7 %cholesky.282 = f32[128,128]{1,0:T(8,128)S(1)} custom-call(f32[128,128]{1,0:T(8,128)S(1)} %fusion.189), custom_call_target="Cholesky" | custom-call | tf_op jit(solution)/shard_map/jit(cholesky)/cholesky | solution.py:49
  663.1 9.8 %custom-call.24 = f32[1,128,128]{1,2,0:T(8,128)S(1)} custom-call(f32[1,128,128]{2,1,0:T(8,128)S(1)} %get-tuple-element.13), custom_call_target="InvertDiagBlocksLowerTriangular" | custom-call | tf_op jit(solution)/shard_map/jit(_solve_triangular)/triangular_solve | solution.py:31
  674.6 11.9 %cholesky.293 = f32[128,128]{1,0:T(8,128)S(1)} custom-call(f32[128,128]{1,0:T(8,128)S(1)} %fusion.187), custom_call_target="Cholesky" | custom-call | tf_op jit(solution)/shard_map/jit(cholesky)/cholesky | solution.py:49
  687.8 9.8 %custom-call.25 = f32[1,128,128]{1,2,0:T(8,128)S(1)} custom-call(f32[1,128,128]{2,1,0:T(8,128)S(1)} %get-tuple-element.11), custom_call_target="InvertDiagBlocksLowerTriangular" | custom-call | tf_op jit(solution)/shard_map/jit(_solve_triangular)/triangular_solve | solution.py:31
  699.7 11.7 %cholesky.304 = f32[128,128]{1,0:T(8,128)S(1)} custom-call(f32[128,128]{1,0:T(8,128)S(1)} %fusion.185), custom_call_target="Cholesky" | custom-call | tf_op jit(solution)/shard_map/jit(cholesky)/cholesky | solution.py:49
  713.4 10.0 %custom-call.26 = f32[1,128,128]{1,2,0:T(8,128)S(1)} custom-call(f32[1,128,128]{2,1,0:T(8,128)S(1)} %get-tuple-element.9), custom_call_target="InvertDiagBlocksLowerTriangular" | custom-call | tf_op jit(solution)/shard_map/jit(_solve_triangular)/triangular_solve | solution.py:31
  735.0 11.7 %cholesky.315 = f32[128,128]{1,0:T(8,128)S(1)} custom-call(f32[128,128]{1,0:T(8,128)S(1)} %fusion.183), custom_call_target="Cholesky" | custom-call | tf_op jit(solution)/shard_map/jit(cholesky)/cholesky | solution.py:49
  748.1 9.8 %custom-call.27 = f32[1,128,128]{1,2,0:T(8,128)S(1)} custom-call(f32[1,128,128]{2,1,0:T(8,128)S(1)} %fusion.157), custom_call_target="InvertDiagBlocksLowerTriangular" | custom-call | tf_op jit(solution)/shard_map/jit(_solve_triangular)/triangular_solve | solution.py:31
  (275 shorter events, 216.6 us)
Async XLA Ops:
  7.2 82.9 %reduce-scatter.4.cloned.1.call-start = ((), (), s32[]{:S(2)}) async-start(), calls=%async_computation.4 | async-start | bytes 3342336
  28.1 112.2 %all-gather.4.cloned.1.call-start = ((), (), s32[]{:S(2)}) async-start(), calls=%async_computation.1 | async-start | bytes 6684672 | tf_op jit(solution)/shard_map/all_gather | solution.py:187
  92.1 263.3 %all-gather.6.cloned.1.call-start = ((), (), s32[]{:S(2)}) async-start(), calls=%async_computation.2 | async-start | bytes 2228224 | tf_op jit(solution)/shard_map/all_gather | solution.py:213
  161.6 62.6 %copy-start.11 = (f32[128,128]{0,1:T(8,128)}, f32[128,128]{0,1:T(8,128)S(1)}, u32[]{:S(2)}) copy-start(f32[128,128]{0,1:T(8,128)S(1)} %get-tuple-element.30) | copy-start | bytes 196612
  186.6 37.6 %copy-start.12 = (f32[128,128]{0,1:T(8,128)}, f32[128,128]{0,1:T(8,128)S(1)}, u32[]{:S(2)}) copy-start(f32[128,128]{0,1:T(8,128)S(1)} %get-tuple-element.28) | copy-start | bytes 196612
  197.1 27.6 %copy-start.6 = (f32[256,128]{0,1:T(8,128)}, f32[256,128]{0,1:T(8,128)S(1)}, u32[]{:S(2)}) copy-start(f32[256,128]{0,1:T(8,128)S(1)} %fusion.155) | copy-start | bytes 393220
  211.2 38.1 %copy-start.18 = (f32[128,128]{0,1:T(8,128)}, f32[128,128]{0,1:T(8,128)S(1)}, u32[]{:S(2)}) copy-start(f32[128,128]{0,1:T(8,128)S(1)} %get-tuple-element.26) | copy-start | bytes 196612
  222.5 26.9 %copy-start.19 = (f32[128,128]{0,1:T(8,128)}, f32[128,128]{0,1:T(8,128)S(1)}, u32[]{:S(2)}) copy-start(f32[128,128]{0,1:T(8,128)S(1)} %copy.108) | copy-start | bytes 196612
  222.5 26.9 %copy-start.9 = (f32[128,256]{1,0:T(8,128)}, f32[128,256]{1,0:T(8,128)S(1)}, u32[]{:S(2)}) copy-start(f32[128,256]{1,0:T(8,128)S(1)} %concatenate.158) | copy-start | bytes 393220
  271.7 6.3 collective-permute-start
  311.5 4.1 collective-permute-start.1
  316.2 326.7 %all-gather.8.cloned.1.call-start = ((), (), s32[]{:S(2)}) async-start(), calls=%async_computation.3 | async-start | bytes 2228224 | tf_op jit(solution)/shard_map/all_gather | solution.py:232
  320.0 218.7 %collective-permute-start.2 = (f32[512,512]{1,0:T(8,128)}, f32[512,512]{1,0:T(8,128)}, u32[]{:S(2)}, u32[]{:S(2)}) collective-permute-start(f32[512,512]{1,0:T(8,128)} %fusion), channel_id=1, source_target_pairs={{0,16},{16,0},{32,48},{48,32},{64,80},{80,64},{96,112},{112,96},{1... | collective-permute-start | bytes 3145736 | tf_op jit(solution)/shard_map/ppermute | solution.py:16
  362.4 1.0 copy-start.1
  388.4 1.5 copy-start.7
  437.4 0.8 copy-start.2
  476.8 1.2 copy-start.13
  527.1 6.0 copy-start.4
  527.1 6.0 copy-start.24
  527.1 6.0 copy-start.25
  527.1 6.0 copy-start.26
  535.2 23.5 %copy-start = (f32[512,512]{1,0:T(8,128)}, f32[512,512]{1,0:T(8,128)S(1)}, u32[]{:S(2)}) copy-start(f32[512,512]{1,0:T(8,128)S(1)} %fusion.35) | copy-start | bytes 3145732
  543.7 8.3 %copy-start.16 = (f32[96,512]{1,0:T(8,128)S(1)}, f32[96,512]{1,0:T(8,128)}, u32[]{:S(2)}) copy-start(f32[96,512]{1,0:T(8,128)} %fusion.38) | copy-start | bytes 589828
  544.5 7.5 collective-permute-start.4
  550.0 7.5 collective-permute-start.3
  592.4 4.1 collective-permute-start.5
  597.4 5.1 collective-permute-start.6
  673.2 53.3 %copy-start.8 = (f32[128,128]{1,0:T(8,128)}, f32[128,128]{1,0:T(8,128)S(1)}, u32[]{:S(2)}) copy-start(f32[128,128]{1,0:T(8,128)S(1)} %fusion.63) | copy-start | bytes 196612
  698.2 28.4 %copy-start.10 = (f32[256,128]{0,1:T(8,128)}, f32[256,128]{0,1:T(8,128)S(1)}, u32[]{:S(2)}) copy-start(f32[256,128]{0,1:T(8,128)S(1)} %fusion.149) | copy-start | bytes 393220
  698.3 28.3 %copy-start.23 = (f32[128,128]{1,0:T(8,128)}, f32[128,128]{1,0:T(8,128)S(1)}, u32[]{:S(2)}) copy-start(f32[128,128]{1,0:T(8,128)S(1)} %copy.151) | copy-start | bytes 196612
  698.4 15.0 %copy-start.20 = (f32[128,128]{0,1:T(8,128)}, f32[128,128]{0,1:T(8,128)S(1)}, u32[]{:S(2)}) copy-start(f32[128,128]{0,1:T(8,128)S(1)} %copy.154) | copy-start | bytes 196612
  727.8 33.0 %copy-start.5 = (f32[512,1024]{1,0:T(8,128)S(1)}, f32[512,1024]{1,0:T(8,128)}, u32[]{:S(2)}) copy-start(f32[512,1024]{1,0:T(8,128)} %all-gather.8.cloned.1.call-done) | copy-start | bytes 6291460
  (6 other events, 3.8 us)
Sparse Core Ops, SparseCore 0:
  28.2 61.7 reduce-scatter.3
  92.2 47.9 all-gather.3
  316.4 39.0 all-gather.5
  603.3 39.5 all-gather.7

commit v6 on v5

--- a/solution.py
+++ b/solution.py
@@ -9,6 +9,8 @@
 from jax.sharding import PartitionSpec as P
 
 HIGH = lax.Precision.HIGHEST
+MESH = pl.DeviceIdType.MESH
+VMEM = pltpu.VMEM
 
 
 def swap(block, axis, mask):
@@ -29,6 +31,43 @@
 def inverse_lower(factor):
     eye = jnp.eye(factor.shape[0], dtype=factor.dtype)
     return jax.scipy.linalg.solve_triangular(factor, eye, lower=True)
+
+
+def block_kernel(gram_ref, upper_ref, inverse_ref, work_ref):
+    size = gram_ref.shape[0]
+    work_ref[...] = gram_ref[...]
+    lane = lax.broadcasted_iota(jnp.int32, (1, size), 1)
+    row = lax.broadcasted_iota(jnp.int32, (size, size), 0)
+    inverse_ref[...] = (row == lax.broadcasted_iota(jnp.int32, (size, size), 1)).astype(jnp.float32)
+
+    def step(index, carry):
+        current = work_ref[pl.ds(index, 1), :]
+        pivot = jnp.sum(jnp.where(lane == index, current, 0.0), axis=1, keepdims=True)
+        root = jnp.sqrt(pivot)
+        column = jnp.where(lane >= index, current / root, 0.0)
+        upper_ref[pl.ds(index, 1), :] = column
+        spread = jnp.transpose(jnp.broadcast_to(column, (size, size)))
+        work_ref[...] = work_ref[...] - spread * column
+        solved = inverse_ref[pl.ds(index, 1), :] / root
+        below = jnp.where(row > index, spread, 0.0)
+        inverse_ref[...] = inverse_ref[...] - below * solved
+        inverse_ref[pl.ds(index, 1), :] = solved
+        return carry
+
+    lax.fori_loop(0, size, step, 0)
+
+
+def factor_block(gram):
+    size = gram.shape[0]
+    shape = jax.ShapeDtypeStruct((size, size), gram.dtype)
+    upper, inverse = pl.pallas_call(
+        block_kernel,
+        out_shape=(shape, shape),
+        in_specs=[pl.BlockSpec(memory_space=VMEM)],
+        out_specs=(pl.BlockSpec(memory_space=VMEM), pl.BlockSpec(memory_space=VMEM)),
+        scratch_shapes=[VMEM((size, size), gram.dtype)],
+    )(gram)
+    return upper.T, inverse
 
 
 def join_lower(upper_left, lower_left, lower_right):
@@ -46,8 +85,7 @@
         if panels:
             done = jnp.concatenate(panels, axis=1)
             column = column - product(done[start:], done[start:stop].T)
-        diagonal = jnp.linalg.cholesky(column[:block])
-        inverse = inverse_lower(diagonal)
+        diagonal, inverse = factor_block(column[:block])
         inverses.append(inverse)
         below = product(column[block:], inverse.T)
         panel = jnp.concatenate([diagonal, below], axis=0)
@@ -67,10 +105,6 @@
         inverses = merged
         width *= 2
     return factor, inverses[0]
-
-
-MESH = pl.DeviceIdType.MESH
-VMEM = pltpu.VMEM
 
 
 def greet(count):

time: 779 us -> 787 us (1.010)
  Pallas kernels: 61.3 us -> 383 us
  other arithmetic: 311 us -> 10.6 us
  local copies, waits for them, and re-layouts: 40.9 us -> 22 us
    pallas_call x0 -> x12, Pallas kernels: none -> 322 us  [factor_block(): pl.pallas_call(block_kernel, out_shape=(shape, shape), in_specs=[pl.Block...]
    another operation x60 -> x0, other arithmetic: 294 us -> none  [the longest x36 157 us: factor_pair(): diagonal = jnp.linalg.cholesky(column[:block])]
    another operation x24 -> x2, local copies, waits for them, and re-layouts: 13.8 us -> 0.02 us  [the longest x14 8.6 us: inverse_lower(): return jax.scipy.linalg.solve_triangular(factor, eye, lower=True)]
    dot_general x47, matrix products: 63.8 us -> 73.3 us  [product(): jnp.dot(left, right, precision=HIGH, preferred_element_type=jnp.float32)]
  transfers between devices with their start and end apart: 11 -> 11, of which waited for: 10 -> 10; matrix products, arithmetic and copies ran while one was open for 25% -> 7% of each run, Pallas kernels for 0% -> 14%
where the time goes in v6:
time: 787 us; the launch traced here: 777 us
  Pallas kernels  383 us (49%)
  waiting for transfers between devices  199 us (25%)
  matrix products  140 us (18%)
  local copies, waits for them, and re-layouts  22 us (3%)
  between operations  14.7 us (2%)
  other arithmetic  10.6 us (1%)
  starting transfers between devices  9.04 us (1%)
    pallas_call x12, Pallas kernels, factor_block(): pl.pallas_call(block_kernel, out_shape=(shape, shape), in_specs=[pl.Block...  322 us
    dot_general x47, matrix products, product(): jnp.dot(left, right, precision=HIGH, preferred_element_type=jnp.float32)  73.3 us
    dot_general x13, matrix products, transposed(): lax.dot_general(left, right, (((0,), (0,)), ((), ())), precision=HIGH, pr...  66.3 us
    pallas_call x2, Pallas kernels, tile_scatter(): pl.pallas_call(functools.partial(scatter_kernel, count), out_shape=jax.Sh...  61.3 us
    unnamed x5, waiting for transfers between devices  60.9 us
    all_gather x1, waiting for transfers between devices, on_device(): lax.all_gather(jnp.concatenate([sample_rows, owned], axis=1), 'tile', axi...  48 us
    all_gather x1, waiting for transfers between devices, on_device(): lax.all_gather(jnp.concatenate([grand_part, cousin_part], axis=1), 'tile'...  37.6 us
    all_gather x1, waiting for transfers between devices, on_device(): lax.all_gather(jnp.concatenate([sample_part, other_part], axis=1), 'tile'...  34 us
  transfers between devices with their start and end apart: 11, of which 10 were waited for; matrix products, arithmetic and copies ran while one was open for 7% of the time, Pallas kernels for 14%

profile of v6, /device:TPU:1, one launch (start us, length us, event | category | flops | bytes accessed | tf_op | source)
XLA Modules:
  0.0 777.5 jit_solution(9077334435844162392)
XLA Ops:
  7.2 18.4 %convolution_bitcast_fusion = f32[1536,512]{0,1:T(8,128)S(1)} fusion(f32[16,96,1536]{2,1,0:T(8,128)} %param.2, f32[16,96,512]{2,1,0:T(8,128)} %param.3, pred[16]{0:T(512)(128)(4,1)S(1)} %iota_compare_fusion.4), kind=kOutput, calls=%fused_computation | convolution fusion | flops 14496301056 | bytes 15728656 | tf_op jit(solution)/shard_map/dot_general | solution.py:26
  29.2 60.8 %reduce-scatter.4.cloned.1.call-done = f32[96,512]{1,0:T(8,128)} async-done(((f32[1536,512]{1,0:T(8,128)}), f32[96,512]{1,0:T(8,128)}) %reduce-scatter.4.cloned.1.call-update) | async-done | bytes 196624
  92.1 48.0 %all-gather.4.cloned.1.call-done = f32[1536,1024]{1,0:T(8,128)} async-done(((f32[96,1024]{1,0:T(8,128)}), f32[1536,1024]{1,0:T(8,128)}) %all-gather.4.cloned.1.call-update) | async-done | bytes 6291472 | tf_op jit(solution)/shard_map/all_gather | solution.py:221
  140.1 8.0 %fusion.5 = f32[512,512]{1,0:T(8,128)S(1)} fusion(f32[1536,1024]{1,0:T(8,128)} %all-gather.4.cloned.1.call-done), kind=kOutput, calls=%fused_computation.6 | convolution fusion | flops 4831838208 | bytes 4194304 | tf_op jit(solution)/shard_map/dot_general | solution.py:26
  148.8 27.2 %shard_map.49 = (f32[128,128]{1,0:T(8,128)}, f32[128,128]{1,0:T(8,128)}) custom-call(f32[128,128]{1,0:T(8,128)} %slice.201.gram_ref), custom_call_target="tpu_custom_call" | custom-call | tf_op jit(solution)/shard_map/pallas_call | solution.py:63
  179.4 26.8 %shard_map.50 = (f32[128,128]{1,0:T(8,128)}, f32[128,128]{1,0:T(8,128)}) custom-call(f32[128,128]{1,0:T(8,128)} %slice.205.gram_ref), custom_call_target="tpu_custom_call" | custom-call | tf_op jit(solution)/shard_map/pallas_call | solution.py:63
  209.5 26.8 %shard_map.51 = (f32[128,128]{1,0:T(8,128)}, f32[128,128]{1,0:T(8,128)}) custom-call(f32[128,128]{1,0:T(8,128)} %slice.210.gram_ref), custom_call_target="tpu_custom_call" | custom-call | tf_op jit(solution)/shard_map/pallas_call | solution.py:63
  243.1 26.8 %shard_map.52 = (f32[128,128]{1,0:T(8,128)}, f32[128,128]{1,0:T(8,128)}) custom-call(f32[128,128]{1,0:T(8,128)} %convolution_subtract_fusion.8.gram_ref), custom_call_target="tpu_custom_call" | custom-call | tf_op jit(solution)/shard_map/pallas_call | solution.py:63
  272.2 7.1 fusion.3
  279.3 12.5 %fusion = f32[512,512]{1,0:T(8,128)} fusion(f32[1536,512]{1,0:T(8,128)S(1)} %fusion.3, f32[1536,1024]{1,0:T(8,128)} %all-gather.4.cloned.1.call-done), kind=kOutput, calls=%fused_computation.1 | convolution fusion | flops 4831838208 | bytes 7340032 | tf_op jit(solution)/shard_map/dot_general | solution.py:26
  302.1 30.5 %shard_map.53 = f32[32,512]{1,0:T(8,128)} custom-call(f32[512,512]{1,0:T(8,128)} %fusion.193.block_ref), custom_call_target="tpu_custom_call" | custom-call | tf_op jit(solution)/shard_map/pallas_call | solution.py:172
  338.4 3.7 fusion.38
  343.5 34.0 %all-gather.6.cloned.1.call-done = f32[512,1024]{1,0:T(8,128)} async-done(((f32[32,1024]{1,0:T(8,128)}), f32[512,1024]{1,0:T(8,128)}) %all-gather.6.cloned.1.call-update) | async-done | bytes 2097168 | tf_op jit(solution)/shard_map/all_gather | solution.py:247
  377.5 3.4 fusion.33
  380.9 3.4 convolution_add_fusion.2
  385.9 26.8 %shard_map.54 = (f32[128,128]{1,0:T(8,128)}, f32[128,128]{1,0:T(8,128)}) custom-call(f32[128,128]{1,0:T(8,128)} %slice.216.gram_ref), custom_call_target="tpu_custom_call" | custom-call | tf_op jit(solution)/shard_map/pallas_call | solution.py:63
  420.8 26.8 %shard_map.55 = (f32[128,128]{1,0:T(8,128)}, f32[128,128]{1,0:T(8,128)}) custom-call(f32[128,128]{1,0:T(8,128)} %slice.220.gram_ref), custom_call_target="tpu_custom_call" | custom-call | tf_op jit(solution)/shard_map/pallas_call | solution.py:63
  453.4 26.8 %shard_map.56 = (f32[128,128]{1,0:T(8,128)}, f32[128,128]{1,0:T(8,128)}) custom-call(f32[128,128]{1,0:T(8,128)} %slice.225.gram_ref), custom_call_target="tpu_custom_call" | custom-call | tf_op jit(solution)/shard_map/pallas_call | solution.py:63
  493.7 26.8 %shard_map.57 = (f32[128,128]{1,0:T(8,128)}, f32[128,128]{1,0:T(8,128)}) custom-call(f32[128,128]{1,0:T(8,128)} %convolution_subtract_fusion.7.gram_ref), custom_call_target="tpu_custom_call" | custom-call | tf_op jit(solution)/shard_map/pallas_call | solution.py:63
  523.1 3.2 fusion.31
  528.2 3.5 fusion.195
  546.3 4.5 collective-permute-done.3
  554.7 30.8 %shard_map.58 = f32[32,512]{1,0:T(8,128)} custom-call(f32[512,512]{1,0:T(8,128)} %fusion.198.block_ref), custom_call_target="tpu_custom_call" | custom-call | tf_op jit(solution)/shard_map/pallas_call | solution.py:172
  585.7 4.0 collective-permute-done.5
  592.0 3.5 collective-permute-done.6
  598.4 37.6 %all-gather.8.cloned.1.call-done = f32[512,1024]{1,0:T(8,128)} async-done(((f32[32,1024]{1,0:T(8,128)}), f32[512,1024]{1,0:T(8,128)}) %all-gather.8.cloned.1.call-update) | async-done | bytes 2097168 | tf_op jit(solution)/shard_map/all_gather | solution.py:266
  635.9 3.4 fusion.12
  639.3 3.4 convolution_add_fusion
  643.4 26.8 %shard_map.59 = (f32[128,128]{1,0:T(8,128)}, f32[128,128]{1,0:T(8,128)}) custom-call(f32[128,128]{1,0:T(8,128)} %slice.230.gram_ref), custom_call_target="tpu_custom_call" | custom-call | tf_op jit(solution)/shard_map/pallas_call | solution.py:63
  673.6 26.8 %shard_map.60 = (f32[128,128]{1,0:T(8,128)}, f32[128,128]{1,0:T(8,128)}) custom-call(f32[128,128]{1,0:T(8,128)} %slice.234.gram_ref), custom_call_target="tpu_custom_call" | custom-call | tf_op jit(solution)/shard_map/pallas_call | solution.py:63
  703.7 26.8 %shard_map.61 = (f32[128,128]{1,0:T(8,128)}, f32[128,128]{1,0:T(8,128)}) custom-call(f32[128,128]{1,0:T(8,128)} %slice.239.gram_ref), custom_call_target="tpu_custom_call" | custom-call | tf_op jit(solution)/shard_map/pallas_call | solution.py:63
  736.4 26.8 %shard_map.62 = (f32[128,128]{1,0:T(8,128)}, f32[128,128]{1,0:T(8,128)}) custom-call(f32[128,128]{1,0:T(8,128)} %convolution_subtract_fusion.6.gram_ref), custom_call_target="tpu_custom_call" | custom-call | tf_op jit(solution)/shard_map/pallas_call | solution.py:63
  (153 shorter events, 117.3 us)
Async XLA Ops:
  7.2 82.8 %reduce-scatter.4.cloned.1.call-start = ((), (), s32[]{:S(2)}) async-start(), calls=%async_computation.4 | async-start | bytes 3342336
  28.0 112.1 %all-gather.4.cloned.1.call-start = ((), (), s32[]{:S(2)}) async-start(), calls=%async_computation.1 | async-start | bytes 6684672 | tf_op jit(solution)/shard_map/all_gather | solution.py:221
  92.1 285.4 %all-gather.6.cloned.1.call-start = ((), (), s32[]{:S(2)}) async-start(), calls=%async_computation.2 | async-start | bytes 2228224 | tf_op jit(solution)/shard_map/all_gather | solution.py:247
  176.0 64.6 %copy-start.8 = (f32[128,128]{1,0:T(8,128)S(1)}, f32[128,128]{1,0:T(8,128)}, u32[]{:S(2)}) copy-start(f32[128,128]{1,0:T(8,128)} %get-tuple-element.28) | copy-start | bytes 196612
  176.0 66.0 %copy-start.13 = (f32[128,128]{1,0:T(8,128)S(1)}, f32[128,128]{1,0:T(8,128)}, u32[]{:S(2)}) copy-start(f32[128,128]{1,0:T(8,128)} %get-tuple-element.30) | copy-start | bytes 196612
  206.1 34.5 %copy-start.10 = (f32[128,128]{1,0:T(8,128)S(1)}, f32[128,128]{1,0:T(8,128)}, u32[]{:S(2)}) copy-start(f32[128,128]{1,0:T(8,128)} %get-tuple-element.29) | copy-start | bytes 196612
  206.1 35.8 %copy-start.14 = (f32[128,128]{1,0:T(8,128)S(1)}, f32[128,128]{1,0:T(8,128)}, u32[]{:S(2)}) copy-start(f32[128,128]{1,0:T(8,128)} %get-tuple-element.31) | copy-start | bytes 196612
  207.3 63.6 %copy-start.6 = (f32[256,128]{0,1:T(8,128)}, f32[256,128]{0,1:T(8,128)S(1)}, u32[]{:S(2)}) copy-start(f32[256,128]{0,1:T(8,128)S(1)} %fusion.131) | copy-start | bytes 393220
  238.6 32.3 %copy-start.15 = (f32[128,128]{0,1:T(8,128)}, f32[128,128]{0,1:T(8,128)S(1)}, u32[]{:S(2)}) copy-start(f32[128,128]{0,1:T(8,128)S(1)} %copy.27) | copy-start | bytes 196612
  239.5 31.5 %copy-start.7 = (f32[128,256]{1,0:T(8,128)}, f32[128,256]{1,0:T(8,128)S(1)}, u32[]{:S(2)}) copy-start(f32[128,256]{1,0:T(8,128)S(1)} %concatenate.158) | copy-start | bytes 393220
  293.8 6.3 collective-permute-start
  333.5 4.1 collective-permute-start.1
  338.3 297.6 %all-gather.8.cloned.1.call-start = ((), (), s32[]{:S(2)}) async-start(), calls=%async_computation.3 | async-start | bytes 2228224 | tf_op jit(solution)/shard_map/all_gather | solution.py:266
  342.1 189.7 %collective-permute-start.2 = (f32[512,512]{1,0:T(8,128)}, f32[512,512]{1,0:T(8,128)}, u32[]{:S(2)}, u32[]{:S(2)}) collective-permute-start(f32[512,512]{1,0:T(8,128)} %fusion), channel_id=1, source_target_pairs={{0,16},{16,0},{32,48},{48,32},{64,80},{80,64},{96,112},{112,96},{1... | collective-permute-start | bytes 3145736 | tf_op jit(solution)/shard_map/ppermute | solution.py:18
  384.3 1.0 copy-start.1
  414.0 0.7 copy-start.3
  448.8 3.3 copy-start.5
  449.8 0.8 copy-start.2
  520.4 5.9 copy-start.4
  520.4 5.9 copy-start.18
  520.4 5.9 copy-start.21
  520.4 5.9 copy-start.22
  528.2 23.6 %copy-start = (f32[512,512]{1,0:T(8,128)}, f32[512,512]{1,0:T(8,128)S(1)}, u32[]{:S(2)}) copy-start(f32[512,512]{1,0:T(8,128)S(1)} %fusion.35) | copy-start | bytes 3145732
  536.8 8.5 %copy-start.12 = (f32[96,512]{1,0:T(8,128)S(1)}, f32[96,512]{1,0:T(8,128)}, u32[]{:S(2)}) copy-start(f32[96,512]{1,0:T(8,128)} %fusion.38) | copy-start | bytes 589828
  537.5 7.7 collective-permute-start.4
  543.2 7.5 collective-permute-start.3
  585.6 4.1 collective-permute-start.5
  590.6 4.9 collective-permute-start.6
  670.2 64.5 %copy-start.9 = (f32[128,128]{1,0:T(8,128)S(1)}, f32[128,128]{1,0:T(8,128)}, u32[]{:S(2)}) copy-start(f32[128,128]{1,0:T(8,128)} %get-tuple-element.46) | copy-start | bytes 196612
  670.2 65.1 %copy-start.19 = (f32[128,128]{1,0:T(8,128)S(1)}, f32[128,128]{1,0:T(8,128)}, u32[]{:S(2)}) copy-start(f32[128,128]{1,0:T(8,128)} %get-tuple-element.48) | copy-start | bytes 196612
  700.3 34.3 %copy-start.11 = (f32[128,128]{1,0:T(8,128)S(1)}, f32[128,128]{1,0:T(8,128)}, u32[]{:S(2)}) copy-start(f32[128,128]{1,0:T(8,128)} %get-tuple-element.47) | copy-start | bytes 196612
  700.3 34.9 %copy-start.20 = (f32[128,128]{1,0:T(8,128)S(1)}, f32[128,128]{1,0:T(8,128)}, u32[]{:S(2)}) copy-start(f32[128,128]{1,0:T(8,128)} %get-tuple-element.49) | copy-start | bytes 196612
  (2 other events, 1.3 us)
Sparse Core Ops, SparseCore 0:
  28.2 61.7 reduce-scatter.3
  92.2 47.9 all-gather.3
  338.4 39.0 all-gather.5
  596.3 39.5 all-gather.7

commit v7 on v5

--- a/solution.py
+++ b/solution.py
@@ -190,13 +190,13 @@
     local = both[:, :rank_size]
     omega = both[:, rank_size:]
     factor, factor_inverse = factor_pair(transposed(local, local))
-    basis = product(local, factor_inverse.T)
-    reduced = transposed(basis, omega)
-    basis_rows = lax.dynamic_slice_in_dim(basis, tile * slice_cols, slice_cols, 0)
+    reduced = product(factor_inverse, transposed(local, omega))
+    local_rows = lax.dynamic_slice_in_dim(local, tile * slice_cols, slice_cols, 0)
+    basis_rows = product(local_rows, factor_inverse.T)
 
     def meet(target):
         piece = lax.dynamic_index_in_dim(schur, target, 0, keepdims=False)
-        return product(piece, basis)
+        return product(product(piece, local), factor_inverse.T)
 
     panel_one = product(basis_rows, reduced)
     sibling_rows = swap(panel_one, "node", 1)

time: 779 us -> 691 us (0.89)
  local copies, waits for them, and re-layouts: 40.9 us -> 12.5 us
  other arithmetic: 311 us -> 284 us
  matrix products: 137 us -> 111 us
    dot_general x47 -> x51, matrix products: 63.8 us -> 47.3 us  [product(): jnp.dot(left, right, precision=HIGH, preferred_element_type=jnp.float32)]
    another operation x24, other arithmetic: 137 us -> 127 us  [inverse_lower(): return jax.scipy.linalg.solve_triangular(factor, eye, lower=True)]
  transfers between devices with their start and end apart: 11 -> 11, of which waited for: 10 -> 8; matrix products, arithmetic and copies ran while one was open for 25% -> 20% of each run, Pallas kernels for 0% -> 0%
where the time goes in v7:
time: 691 us; the launch traced here: 687 us
  other arithmetic  284 us (41%)
  waiting for transfers between devices  191 us (28%)
  matrix products  111 us (16%)
  Pallas kernels  62.2 us (9%)
  between operations  16 us (2%)
  local copies, waits for them, and re-layouts  12.5 us (2%)
  starting transfers between devices  10 us (1%)
    another operation x36, other arithmetic, factor_pair(): diagonal = jnp.linalg.cholesky(column[:block])  150 us
    another operation x24, other arithmetic, inverse_lower(): return jax.scipy.linalg.solve_triangular(factor, eye, lower=True)  127 us
    pallas_call x2, Pallas kernels, tile_scatter(): pl.pallas_call(functools.partial(scatter_kernel, count), out_shape=jax.Sh...  62.2 us
    unnamed x5, waiting for transfers between devices  60.9 us
    dot_general x13, matrix products, transposed(): lax.dot_general(left, right, (((0,), (0,)), ((), ())), precision=HIGH, pr...  60.4 us
    all_gather x1, waiting for transfers between devices, on_device(): lax.all_gather(jnp.concatenate([sample_rows, owned], axis=1), 'tile', axi...  47.9 us
    dot_general x51, matrix products, product(): jnp.dot(left, right, precision=HIGH, preferred_element_type=jnp.float32)  47.3 us
    all_gather x1, waiting for transfers between devices, on_device(): lax.all_gather(jnp.concatenate([grand_part, cousin_part], axis=1), 'tile'...  39 us
  transfers between devices with their start and end apart: 11, of which 8 were waited for; matrix products, arithmetic and copies ran while one was open for 20% of the time, Pallas kernels for 0%

profile of v7, /device:TPU:1, one launch (start us, length us, event | category | flops | bytes accessed | tf_op | source)
XLA Modules:
  0.0 686.9 jit_solution(2678254822936574147)
XLA Ops:
  7.2 18.4 %convolution_bitcast_fusion = f32[1536,512]{0,1:T(8,128)S(1)} fusion(f32[16,96,1536]{2,1,0:T(8,128)} %param.5, f32[16,96,512]{2,1,0:T(8,128)} %param.6, pred[16]{0:T(512)(128)(4,1)S(1)} %iota_compare_fusion.19), kind=kOutput, calls=%fused_computation | convolution fusion | flops 14496301056 | bytes 15728656 | tf_op jit(solution)/shard_map/dot_general | solution.py:24
  29.2 60.8 %reduce-scatter.4.cloned.1.call-done = f32[96,512]{1,0:T(8,128)} async-done(((f32[1536,512]{1,0:T(8,128)}), f32[96,512]{1,0:T(8,128)}) %reduce-scatter.4.cloned.1.call-update) | async-done | bytes 196624
  92.3 47.9 %all-gather.4.cloned.1.call-done = f32[1536,1024]{1,0:T(8,128)} async-done(((f32[96,1024]{1,0:T(8,128)}), f32[1536,1024]{1,0:T(8,128)}) %all-gather.4.cloned.1.call-update) | async-done | bytes 6291472 | tf_op jit(solution)/shard_map/all_gather | solution.py:187
  148.4 11.7 %cholesky.194 = f32[128,128]{1,0:T(8,128)S(1)} custom-call(f32[128,128]{1,0:T(8,128)S(1)} %get-tuple-element.32), custom_call_target="Cholesky" | custom-call | tf_op jit(solution)/shard_map/jit(cholesky)/cholesky | solution.py:49
  161.7 9.8 %custom-call.16 = f32[1,128,128]{1,2,0:T(8,128)S(1)} custom-call(f32[1,128,128]{2,1,0:T(8,128)S(1)} %copy.91), custom_call_target="InvertDiagBlocksLowerTriangular" | custom-call | tf_op jit(solution)/shard_map/jit(_solve_triangular)/triangular_solve | solution.py:31
  173.0 11.7 %cholesky.205 = f32[128,128]{1,0:T(8,128)S(1)} custom-call(f32[128,128]{1,0:T(8,128)S(1)} %fusion.187), custom_call_target="Cholesky" | custom-call | tf_op jit(solution)/shard_map/jit(cholesky)/cholesky | solution.py:49
  186.4 9.8 %custom-call.17 = f32[1,128,128]{1,2,0:T(8,128)S(1)} custom-call(f32[1,128,128]{2,1,0:T(8,128)S(1)} %copy.97), custom_call_target="InvertDiagBlocksLowerTriangular" | custom-call | tf_op jit(solution)/shard_map/jit(_solve_triangular)/triangular_solve | solution.py:31
  198.9 12.2 %cholesky.216 = f32[128,128]{1,0:T(8,128)S(1)} custom-call(f32[128,128]{1,0:T(8,128)S(1)} %fusion.185), custom_call_target="Cholesky" | custom-call | tf_op jit(solution)/shard_map/jit(cholesky)/cholesky | solution.py:49
  212.7 9.8 %custom-call.18 = f32[1,128,128]{1,2,0:T(8,128)S(1)} custom-call(f32[1,128,128]{2,1,0:T(8,128)S(1)} %copy.107), custom_call_target="InvertDiagBlocksLowerTriangular" | custom-call | tf_op jit(solution)/shard_map/jit(_solve_triangular)/triangular_solve | solution.py:31
  224.2 11.7 %cholesky.227 = f32[128,128]{1,0:T(8,128)S(1)} custom-call(f32[128,128]{1,0:T(8,128)S(1)} %fusion.183), custom_call_target="Cholesky" | custom-call | tf_op jit(solution)/shard_map/jit(cholesky)/cholesky | solution.py:49
  238.1 9.8 %custom-call.19 = f32[1,128,128]{1,2,0:T(8,128)S(1)} custom-call(f32[1,128,128]{2,1,0:T(8,128)S(1)} %copy.114), custom_call_target="InvertDiagBlocksLowerTriangular" | custom-call | tf_op jit(solution)/shard_map/jit(_solve_triangular)/triangular_solve | solution.py:31
  249.0 8.2 %fusion = f32[512,512]{1,0:T(8,128)S(1)} fusion(f32[1536,1024]{1,0:T(8,128)} %all-gather.4.cloned.1.call-done), kind=kOutput, calls=%fused_computation.1 | convolution fusion | flops 4831838208 | bytes 7340032 | tf_op jit(solution)/shard_map/dot_general | solution.py:24
  271.6 30.8 %shard_map.49 = f32[32,512]{1,0:T(8,128)} custom-call(f32[512,512]{1,0:T(8,128)} %fusion.238.block_ref), custom_call_target="tpu_custom_call" | custom-call | tf_op jit(solution)/shard_map/pallas_call | solution.py:138
  320.1 27.2 %all-gather.6.cloned.1.call-done = f32[512,1024]{1,0:T(8,128)} async-done(((f32[32,1024]{1,0:T(8,128)}), f32[512,1024]{1,0:T(8,128)}) %all-gather.6.cloned.1.call-update) | async-done | bytes 2097168 | tf_op jit(solution)/shard_map/all_gather | solution.py:213
  354.3 11.7 %cholesky.238 = f32[128,128]{1,0:T(8,128)S(1)} custom-call(f32[128,128]{1,0:T(8,128)S(1)} %fusion.181), custom_call_target="Cholesky" | custom-call | tf_op jit(solution)/shard_map/jit(cholesky)/cholesky | solution.py:49
  367.7 9.8 %custom-call.20 = f32[1,128,128]{1,2,0:T(8,128)S(1)} custom-call(f32[1,128,128]{2,1,0:T(8,128)S(1)} %copy.123), custom_call_target="InvertDiagBlocksLowerTriangular" | custom-call | tf_op jit(solution)/shard_map/jit(_solve_triangular)/triangular_solve | solution.py:31
  379.2 11.9 %cholesky.249 = f32[128,128]{1,0:T(8,128)S(1)} custom-call(f32[128,128]{1,0:T(8,128)S(1)} %fusion.179), custom_call_target="Cholesky" | custom-call | tf_op jit(solution)/shard_map/jit(cholesky)/cholesky | solution.py:49
  392.7 9.8 %custom-call.21 = f32[1,128,128]{1,2,0:T(8,128)S(1)} custom-call(f32[1,128,128]{2,1,0:T(8,128)S(1)} %copy.128), custom_call_target="InvertDiagBlocksLowerTriangular" | custom-call | tf_op jit(solution)/shard_map/jit(_solve_triangular)/triangular_solve | solution.py:31
  406.1 11.7 %cholesky.260 = f32[128,128]{1,0:T(8,128)S(1)} custom-call(f32[128,128]{1,0:T(8,128)S(1)} %fusion.177), custom_call_target="Cholesky" | custom-call | tf_op jit(solution)/shard_map/jit(cholesky)/cholesky | solution.py:49
  419.5 10.2 %custom-call.22 = f32[1,128,128]{1,2,0:T(8,128)S(1)} custom-call(f32[1,128,128]{2,1,0:T(8,128)S(1)} %copy.137), custom_call_target="InvertDiagBlocksLowerTriangular" | custom-call | tf_op jit(solution)/shard_map/jit(_solve_triangular)/triangular_solve | solution.py:31
  431.2 11.7 %cholesky.271 = f32[128,128]{1,0:T(8,128)S(1)} custom-call(f32[128,128]{1,0:T(8,128)S(1)} %fusion.175), custom_call_target="Cholesky" | custom-call | tf_op jit(solution)/shard_map/jit(cholesky)/cholesky | solution.py:49
  445.3 9.8 %custom-call.23 = f32[1,128,128]{1,2,0:T(8,128)S(1)} custom-call(f32[1,128,128]{2,1,0:T(8,128)S(1)} %copy.143), custom_call_target="InvertDiagBlocksLowerTriangular" | custom-call | tf_op jit(solution)/shard_map/jit(_solve_triangular)/triangular_solve | solution.py:31
  486.1 31.4 %shard_map.50 = f32[32,512]{1,0:T(8,128)} custom-call(f32[512,512]{1,0:T(8,128)} %fusion.244.block_ref), custom_call_target="tpu_custom_call" | custom-call | tf_op jit(solution)/shard_map/pallas_call | solution.py:138
  529.7 39.0 %all-gather.8.cloned.1.call-done = f32[512,1024]{1,0:T(8,128)} async-done(((f32[32,1024]{1,0:T(8,128)}), f32[512,1024]{1,0:T(8,128)}) %all-gather.8.cloned.1.call-update) | async-done | bytes 2097168 | tf_op jit(solution)/shard_map/all_gather | solution.py:232
  575.7 11.7 %cholesky.282 = f32[128,128]{1,0:T(8,128)S(1)} custom-call(f32[128,128]{1,0:T(8,128)S(1)} %fusion.173), custom_call_target="Cholesky" | custom-call | tf_op jit(solution)/shard_map/jit(cholesky)/cholesky | solution.py:49
  588.8 9.8 %custom-call.24 = f32[1,128,128]{1,2,0:T(8,128)S(1)} custom-call(f32[1,128,128]{2,1,0:T(8,128)S(1)} %get-tuple-element.13), custom_call_target="InvertDiagBlocksLowerTriangular" | custom-call | tf_op jit(solution)/shard_map/jit(_solve_triangular)/triangular_solve | solution.py:31
  600.2 11.9 %cholesky.293 = f32[128,128]{1,0:T(8,128)S(1)} custom-call(f32[128,128]{1,0:T(8,128)S(1)} %fusion.171), custom_call_target="Cholesky" | custom-call | tf_op jit(solution)/shard_map/jit(cholesky)/cholesky | solution.py:49
  613.5 9.8 %custom-call.25 = f32[1,128,128]{1,2,0:T(8,128)S(1)} custom-call(f32[1,128,128]{2,1,0:T(8,128)S(1)} %get-tuple-element.11), custom_call_target="InvertDiagBlocksLowerTriangular" | custom-call | tf_op jit(solution)/shard_map/jit(_solve_triangular)/triangular_solve | solution.py:31
  627.1 11.7 %cholesky.304 = f32[128,128]{1,0:T(8,128)S(1)} custom-call(f32[128,128]{1,0:T(8,128)S(1)} %fusion.169), custom_call_target="Cholesky" | custom-call | tf_op jit(solution)/shard_map/jit(cholesky)/cholesky | solution.py:49
  640.2 10.0 %custom-call.26 = f32[1,128,128]{1,2,0:T(8,128)S(1)} custom-call(f32[1,128,128]{2,1,0:T(8,128)S(1)} %get-tuple-element.9), custom_call_target="InvertDiagBlocksLowerTriangular" | custom-call | tf_op jit(solution)/shard_map/jit(_solve_triangular)/triangular_solve | solution.py:31
  651.8 11.7 %cholesky.315 = f32[128,128]{1,0:T(8,128)S(1)} custom-call(f32[128,128]{1,0:T(8,128)S(1)} %fusion.167), custom_call_target="Cholesky" | custom-call | tf_op jit(solution)/shard_map/jit(cholesky)/cholesky | solution.py:49
  664.8 9.8 %custom-call.27 = f32[1,128,128]{1,2,0:T(8,128)S(1)} custom-call(f32[1,128,128]{2,1,0:T(8,128)S(1)} %fusion.141), custom_call_target="InvertDiagBlocksLowerTriangular" | custom-call | tf_op jit(solution)/shard_map/jit(_solve_triangular)/triangular_solve | solution.py:31
  (313 shorter events, 147.6 us)
Async XLA Ops:
  7.2 82.8 %reduce-scatter.4.cloned.1.call-start = ((), (), s32[]{:S(2)}) async-start(), calls=%async_computation.4 | async-start | bytes 3342336
  28.1 112.1 %all-gather.4.cloned.1.call-start = ((), (), s32[]{:S(2)}) async-start(), calls=%async_computation.1 | async-start | bytes 6684672 | tf_op jit(solution)/shard_map/all_gather | solution.py:187
  92.1 255.1 %all-gather.6.cloned.1.call-start = ((), (), s32[]{:S(2)}) async-start(), calls=%async_computation.2 | async-start | bytes 2228224 | tf_op jit(solution)/shard_map/all_gather | solution.py:213
  161.6 61.9 %copy-start.9 = (f32[128,128]{0,1:T(8,128)}, f32[128,128]{0,1:T(8,128)S(1)}, u32[]{:S(2)}) copy-start(f32[128,128]{0,1:T(8,128)S(1)} %get-tuple-element.30) | copy-start | bytes 196612
  186.3 37.3 %copy-start.12 = (f32[128,128]{0,1:T(8,128)}, f32[128,128]{0,1:T(8,128)S(1)}, u32[]{:S(2)}) copy-start(f32[128,128]{0,1:T(8,128)S(1)} %get-tuple-element.28) | copy-start | bytes 196612
  197.7 59.6 %copy-start.33 = (f32[256,256]{1,0:T(8,128)}, f32[256,256]{1,0:T(8,128)S(1)}, u32[]{:S(2)}) copy-start(f32[256,256]{1,0:T(8,128)S(1)} %select_maximum_fusion.8) | copy-start | bytes 786436
  212.6 44.7 %copy-start.17 = (f32[128,128]{0,1:T(8,128)}, f32[128,128]{0,1:T(8,128)S(1)}, u32[]{:S(2)}) copy-start(f32[128,128]{0,1:T(8,128)S(1)} %get-tuple-element.26) | copy-start | bytes 196612
  223.2 34.1 %copy-start.20 = (f32[128,128]{0,1:T(8,128)}, f32[128,128]{0,1:T(8,128)S(1)}, u32[]{:S(2)}) copy-start(f32[128,128]{0,1:T(8,128)S(1)} %copy.109) | copy-start | bytes 196612
  223.4 33.9 %copy-start.22 = (f32[128,256]{1,0:T(8,128)}, f32[128,256]{1,0:T(8,128)S(1)}, u32[]{:S(2)}) copy-start(f32[128,256]{1,0:T(8,128)S(1)} %concatenate.158) | copy-start | bytes 393220
  263.2 6.3 collective-permute-start
  268.5 33.8 %copy-start.4 = (f32[256,128]{0,1:T(8,128)S(1)}, f32[256,128]{0,1:T(8,128)}, u32[]{:S(2)}) copy-start(f32[256,128]{0,1:T(8,128)} %copy-done.3) | copy-start | bytes 393220
  268.5 33.8 %copy-start.10 = (f32[128,128]{0,1:T(8,128)S(1)}, f32[128,128]{0,1:T(8,128)}, u32[]{:S(2)}) copy-start(f32[128,128]{0,1:T(8,128)} %copy-done.9) | copy-start | bytes 196612
  268.5 33.8 %copy-start.13 = (f32[128,128]{0,1:T(8,128)S(1)}, f32[128,128]{0,1:T(8,128)}, u32[]{:S(2)}) copy-start(f32[128,128]{0,1:T(8,128)} %copy-done.12) | copy-start | bytes 196612
  268.6 33.8 %copy-start.18 = (f32[128,128]{0,1:T(8,128)S(1)}, f32[128,128]{0,1:T(8,128)}, u32[]{:S(2)}) copy-start(f32[128,128]{0,1:T(8,128)} %copy-done.17) | copy-start | bytes 196612
  271.5 40.6 %copy-start.24 = (f32[128,256]{1,0:T(8,128)S(1)}, f32[128,256]{1,0:T(8,128)}, u32[]{:S(2)}) copy-start(f32[128,256]{1,0:T(8,128)} %copy-done.22) | copy-start | bytes 393220
  271.5 40.6 %copy-start.27 = (f32[256,256]{1,0:T(8,128)S(1)}, f32[256,256]{1,0:T(8,128)}, u32[]{:S(2)}) copy-start(f32[256,256]{1,0:T(8,128)} %copy-done.26) | copy-start | bytes 786436
  271.5 40.6 %copy-start.30 = (f32[128,128]{1,0:T(8,128)S(1)}, f32[128,128]{1,0:T(8,128)}, u32[]{:S(2)}) copy-start(f32[128,128]{1,0:T(8,128)} %copy-done.29) | copy-start | bytes 196612
  271.5 40.6 %copy-start.35 = (f32[256,256]{1,0:T(8,128)S(1)}, f32[256,256]{1,0:T(8,128)}, u32[]{:S(2)}) copy-start(f32[256,256]{1,0:T(8,128)} %copy-done.33) | copy-start | bytes 786436
  271.5 40.6 %copy-start.39 = (f32[128,128]{1,0:T(8,128)S(1)}, f32[128,128]{1,0:T(8,128)}, u32[]{:S(2)}) copy-start(f32[128,128]{1,0:T(8,128)} %copy-done.37) | copy-start | bytes 196612
  303.3 4.1 collective-permute-start.1
  308.0 260.6 %all-gather.8.cloned.1.call-start = ((), (), s32[]{:S(2)}) async-start(), calls=%async_computation.3 | async-start | bytes 2228224 | tf_op jit(solution)/shard_map/all_gather | solution.py:232
  318.5 146.0 %collective-permute-start.2 = (f32[512,512]{1,0:T(8,128)S(1)}, f32[512,512]{1,0:T(8,128)}, u32[]{:S(2)}, u32[]{:S(2)}) collective-permute-start(f32[512,512]{1,0:T(8,128)S(1)} %copy-done.1), channel_id=1, source_target_pairs={{0,16},{16,0},{32,48},{48,32},{64,80},{80,64},{96,112},{112,96},{1... | collective-permute-start | bytes 3145736 | tf_op jit(solution)/shard_map/ppermute | solution.py:16
  367.6 63.0 %copy-start.8 = (f32[128,128]{0,1:T(8,128)}, f32[128,128]{0,1:T(8,128)S(1)}, u32[]{:S(2)}) copy-start(f32[128,128]{0,1:T(8,128)S(1)} %get-tuple-element.22) | copy-start | bytes 196612
  392.6 38.5 %copy-start.11 = (f32[128,128]{0,1:T(8,128)}, f32[128,128]{0,1:T(8,128)S(1)}, u32[]{:S(2)}) copy-start(f32[128,128]{0,1:T(8,128)S(1)} %get-tuple-element.20) | copy-start | bytes 196612
  406.0 49.8 %copy-start.15 = (f32[256,256]{1,0:T(8,128)S(1)}, f32[256,256]{1,0:T(8,128)}, u32[]{:S(2)}) copy-start(f32[256,256]{1,0:T(8,128)} %fusion.85) | copy-start | bytes 786436
  419.4 39.9 %copy-start.16 = (f32[128,128]{0,1:T(8,128)}, f32[128,128]{0,1:T(8,128)S(1)}, u32[]{:S(2)}) copy-start(f32[128,128]{0,1:T(8,128)S(1)} %get-tuple-element.18) | copy-start | bytes 196612
  470.3 10.8 %collective-permute-start.4 = (f32[96,512]{1,0:T(8,128)S(1)}, f32[96,512]{1,0:T(8,128)S(1)}, u32[]{:S(2)}, u32[]{:S(2)}) collective-permute-start(f32[96,512]{1,0:T(8,128)S(1)} %fusion.242), channel_id=1, source_target_pairs={{0,48},{16,32},{32,16},{48,0},{64,112},{80,96},{96,80},{112,64},{1... | collective-permute-start | bytes 589832 | tf_op jit(solution)/shard_map/ppermute | solution.py:16
  473.8 8.4 %collective-permute-start.3 = (f32[96,512]{1,0:T(8,128)S(1)}, f32[96,512]{1,0:T(8,128)S(1)}, u32[]{:S(2)}, u32[]{:S(2)}) collective-permute-start(f32[96,512]{1,0:T(8,128)S(1)} %fusion.242), channel_id=1, source_target_pairs={{0,32},{16,48},{32,0},{48,16},{64,96},{80,112},{96,64},{112,80},{1... | collective-permute-start | bytes 589832 | tf_op jit(solution)/shard_map/ppermute | solution.py:16
  483.2 45.1 %copy-start.7 = (f32[96,512]{1,0:T(8,128)S(1)}, f32[96,512]{1,0:T(8,128)}, u32[]{:S(2)}) copy-start(f32[96,512]{1,0:T(8,128)} %copy-done.5) | copy-start | bytes 589828
  517.5 4.1 collective-permute-start.5
  522.5 5.1 collective-permute-start.6
  627.0 48.3 %copy-start.14 = (f32[256,256]{1,0:T(8,128)S(1)}, f32[256,256]{1,0:T(8,128)}, u32[]{:S(2)}) copy-start(f32[256,256]{1,0:T(8,128)} %fusion.82) | copy-start | bytes 786436
  (23 other events, 268.7 us)
Sparse Core Ops, SparseCore 0:
  28.2 61.7 reduce-scatter.3
  92.2 47.9 all-gather.3
  308.2 39.0 all-gather.5
  528.4 40.1 all-gather.7

commit v8 on v7

--- a/solution.py
+++ b/solution.py
@@ -219,8 +219,10 @@
     )
     parent_inverse = parent_inverse.T
     transfer_own = product(parent_sample, parent_inverse)
-    transfer_other = product(other_sample, parent_inverse)
-    parent_reduced = transposed(transfer_own, reduced) + transposed(transfer_other, other_reduced)
+    parent_reduced = product(
+        parent_inverse.T,
+        transposed(parent_sample, reduced) + transposed(other_sample, other_reduced),
+    )
     panel_two = product(basis_rows, product(transfer_own, parent_reduced))
     cousin_rows = swap(panel_two, "node", 2)
     further_rows = swap(panel_two, "node", 3)
@@ -236,11 +238,10 @@
     grand_factor, grand_inverse = factor_pair(
         transposed(grand_sample, grand_sample) + transposed(cousin_grand, cousin_grand)
     )
-    grand_transfer = product(grand_sample, grand_inverse.T)
     leaf_out = (basis_rows * math.sqrt(leaf_rows))[None]
     one_rows = lax.dynamic_slice_in_dim(transfer_own, tile * out_rows, out_rows, 0)
     level_one = (one_rows * math.sqrt(2 * rank_size))[None]
-    two_rows = product(one_rows, grand_transfer)
+    two_rows = product(product(one_rows, grand_sample), grand_inverse.T)
     level_two = (two_rows * (2.0 * math.sqrt(rank_size)))[None]
     return (leaf_out, level_one, level_two)
 

time: 691 us -> 752 us (1.088)
  local copies, waits for them, and re-layouts: 12.5 us -> 36.3 us
  other arithmetic: 284 us -> 304 us
  matrix products: 111 us -> 126 us
    dot_general x51, matrix products: 47.3 us -> 58.1 us  [product(): jnp.dot(left, right, precision=HIGH, preferred_element_type=jnp.float32)]
    another operation x24, other arithmetic: 127 us -> 135 us  [inverse_lower(): return jax.scipy.linalg.solve_triangular(factor, eye, lower=True)]
  transfers between devices with their start and end apart: 11 -> 11, of which waited for: 8 -> 8; matrix products, arithmetic and copies ran while one was open for 20% -> 22% of each run, Pallas kernels for 0% -> 0%
where the time goes in v8:
time: 752 us; the launch traced here: 746 us
  other arithmetic  304 us (40%)
  waiting for transfers between devices  191 us (25%)
  matrix products  126 us (17%)
  Pallas kernels  62.1 us (8%)
  local copies, waits for them, and re-layouts  36.3 us (5%)
  between operations  16.1 us (2%)
  starting transfers between devices  10 us (1%)
    another operation x36, other arithmetic, factor_pair(): diagonal = jnp.linalg.cholesky(column[:block])  157 us
    another operation x24, other arithmetic, inverse_lower(): return jax.scipy.linalg.solve_triangular(factor, eye, lower=True)  135 us
    pallas_call x2, Pallas kernels, tile_scatter(): pl.pallas_call(functools.partial(scatter_kernel, count), out_shape=jax.Sh...  62.1 us
    dot_general x13, matrix products, transposed(): lax.dot_general(left, right, (((0,), (0,)), ((), ())), precision=HIGH, pr...  61.8 us
    unnamed x5, waiting for transfers between devices  60.9 us
    dot_general x51, matrix products, product(): jnp.dot(left, right, precision=HIGH, preferred_element_type=jnp.float32)  58.1 us
    all_gather x1, waiting for transfers between devices, on_device(): lax.all_gather(jnp.concatenate([sample_rows, owned], axis=1), 'tile', axi...  47.9 us
    all_gather x1, waiting for transfers between devices, on_device(): lax.all_gather(jnp.concatenate([grand_part, cousin_part], axis=1), 'tile'...  39 us
  transfers between devices with their start and end apart: 11, of which 8 were waited for; matrix products, arithmetic and copies ran while one was open for 22% of the time, Pallas kernels for 0%

profile of v8, /device:TPU:1, one launch (start us, length us, event | category | flops | bytes accessed | tf_op | source)
XLA Modules:
  0.0 746.2 jit_solution(16210667029306954850)
XLA Ops:
  7.2 18.4 %convolution_bitcast_fusion = f32[1536,512]{0,1:T(8,128)S(1)} fusion(f32[16,96,1536]{2,1,0:T(8,128)} %param.5, f32[16,96,512]{2,1,0:T(8,128)} %param.6, pred[16]{0:T(512)(128)(4,1)S(1)} %iota_compare_fusion.19), kind=kOutput, calls=%fused_computation | convolution fusion | flops 14496301056 | bytes 15728656 | tf_op jit(solution)/shard_map/dot_general | solution.py:24
  29.2 60.8 %reduce-scatter.4.cloned.1.call-done = f32[96,512]{1,0:T(8,128)} async-done(((f32[1536,512]{1,0:T(8,128)}), f32[96,512]{1,0:T(8,128)}) %reduce-scatter.4.cloned.1.call-update) | async-done | bytes 196624
  92.3 47.9 %all-gather.4.cloned.1.call-done = f32[1536,1024]{1,0:T(8,128)} async-done(((f32[96,1024]{1,0:T(8,128)}), f32[1536,1024]{1,0:T(8,128)}) %all-gather.4.cloned.1.call-update) | async-done | bytes 6291472 | tf_op jit(solution)/shard_map/all_gather | solution.py:187
  148.4 11.7 %cholesky.194 = f32[128,128]{1,0:T(8,128)S(1)} custom-call(f32[128,128]{1,0:T(8,128)S(1)} %get-tuple-element.32), custom_call_target="Cholesky" | custom-call | tf_op jit(solution)/shard_map/jit(cholesky)/cholesky | solution.py:49
  161.7 9.8 %custom-call.16 = f32[1,128,128]{1,2,0:T(8,128)S(1)} custom-call(f32[1,128,128]{2,1,0:T(8,128)S(1)} %copy.91), custom_call_target="InvertDiagBlocksLowerTriangular" | custom-call | tf_op jit(solution)/shard_map/jit(_solve_triangular)/triangular_solve | solution.py:31
  173.0 11.7 %cholesky.205 = f32[128,128]{1,0:T(8,128)S(1)} custom-call(f32[128,128]{1,0:T(8,128)S(1)} %fusion.189), custom_call_target="Cholesky" | custom-call | tf_op jit(solution)/shard_map/jit(cholesky)/cholesky | solution.py:49
  186.4 9.8 %custom-call.17 = f32[1,128,128]{1,2,0:T(8,128)S(1)} custom-call(f32[1,128,128]{2,1,0:T(8,128)S(1)} %copy.97), custom_call_target="InvertDiagBlocksLowerTriangular" | custom-call | tf_op jit(solution)/shard_map/jit(_solve_triangular)/triangular_solve | solution.py:31
  198.9 12.2 %cholesky.216 = f32[128,128]{1,0:T(8,128)S(1)} custom-call(f32[128,128]{1,0:T(8,128)S(1)} %fusion.187), custom_call_target="Cholesky" | custom-call | tf_op jit(solution)/shard_map/jit(cholesky)/cholesky | solution.py:49
  212.7 9.8 %custom-call.18 = f32[1,128,128]{1,2,0:T(8,128)S(1)} custom-call(f32[1,128,128]{2,1,0:T(8,128)S(1)} %copy.107), custom_call_target="InvertDiagBlocksLowerTriangular" | custom-call | tf_op jit(solution)/shard_map/jit(_solve_triangular)/triangular_solve | solution.py:31
  224.2 11.7 %cholesky.227 = f32[128,128]{1,0:T(8,128)S(1)} custom-call(f32[128,128]{1,0:T(8,128)S(1)} %fusion.185), custom_call_target="Cholesky" | custom-call | tf_op jit(solution)/shard_map/jit(cholesky)/cholesky | solution.py:49
  238.1 9.8 %custom-call.19 = f32[1,128,128]{1,2,0:T(8,128)S(1)} custom-call(f32[1,128,128]{2,1,0:T(8,128)S(1)} %copy.114), custom_call_target="InvertDiagBlocksLowerTriangular" | custom-call | tf_op jit(solution)/shard_map/jit(_solve_triangular)/triangular_solve | solution.py:31
  249.0 8.3 %fusion = f32[512,512]{1,0:T(8,128)S(1)} fusion(f32[1536,1024]{1,0:T(8,128)} %all-gather.4.cloned.1.call-done), kind=kOutput, calls=%fused_computation.1 | convolution fusion | flops 4831838208 | bytes 7340032 | tf_op jit(solution)/shard_map/dot_general | solution.py:24
  271.5 30.7 %shard_map.49 = f32[32,512]{1,0:T(8,128)} custom-call(f32[512,512]{1,0:T(8,128)} %fusion.240.block_ref), custom_call_target="tpu_custom_call" | custom-call | tf_op jit(solution)/shard_map/pallas_call | solution.py:138
  320.0 27.2 %all-gather.6.cloned.1.call-done = f32[512,1024]{1,0:T(8,128)} async-done(((f32[32,1024]{1,0:T(8,128)}), f32[512,1024]{1,0:T(8,128)}) %all-gather.6.cloned.1.call-update) | async-done | bytes 2097168 | tf_op jit(solution)/shard_map/all_gather | solution.py:213
  354.3 11.7 %cholesky.238 = f32[128,128]{1,0:T(8,128)S(1)} custom-call(f32[128,128]{1,0:T(8,128)S(1)} %fusion.183), custom_call_target="Cholesky" | custom-call | tf_op jit(solution)/shard_map/jit(cholesky)/cholesky | solution.py:49
  367.7 9.8 %custom-call.20 = f32[1,128,128]{1,2,0:T(8,128)S(1)} custom-call(f32[1,128,128]{2,1,0:T(8,128)S(1)} %copy.123), custom_call_target="InvertDiagBlocksLowerTriangular" | custom-call | tf_op jit(solution)/shard_map/jit(_solve_triangular)/triangular_solve | solution.py:31
  379.7 11.9 %cholesky.249 = f32[128,128]{1,0:T(8,128)S(1)} custom-call(f32[128,128]{1,0:T(8,128)S(1)} %fusion.181), custom_call_target="Cholesky" | custom-call | tf_op jit(solution)/shard_map/jit(cholesky)/cholesky | solution.py:49
  393.2 9.8 %custom-call.21 = f32[1,128,128]{1,2,0:T(8,128)S(1)} custom-call(f32[1,128,128]{2,1,0:T(8,128)S(1)} %copy.128), custom_call_target="InvertDiagBlocksLowerTriangular" | custom-call | tf_op jit(solution)/shard_map/jit(_solve_triangular)/triangular_solve | solution.py:31
  410.0 13.2 %cholesky.260 = f32[128,128]{1,0:T(8,128)} custom-call(f32[128,128]{1,0:T(8,128)} %fusion.179), custom_call_target="Cholesky" | custom-call | tf_op jit(solution)/shard_map/jit(cholesky)/cholesky | solution.py:49
  430.1 11.7 %custom-call.22 = f32[1,128,128]{1,2,0:T(8,128)} custom-call(f32[1,128,128]{2,1,0:T(8,128)} %copy.137), custom_call_target="InvertDiagBlocksLowerTriangular" | custom-call | tf_op jit(solution)/shard_map/jit(_solve_triangular)/triangular_solve | solution.py:31
  453.7 13.2 %cholesky.271 = f32[128,128]{1,0:T(8,128)} custom-call(f32[128,128]{1,0:T(8,128)} %fusion.177), custom_call_target="Cholesky" | custom-call | tf_op jit(solution)/shard_map/jit(cholesky)/cholesky | solution.py:49
  473.7 11.3 %custom-call.23 = f32[1,128,128]{1,2,0:T(8,128)} custom-call(f32[1,128,128]{2,1,0:T(8,128)} %copy.143), custom_call_target="InvertDiagBlocksLowerTriangular" | custom-call | tf_op jit(solution)/shard_map/jit(_solve_triangular)/triangular_solve | solution.py:31
  523.0 31.4 %shard_map.50 = f32[32,512]{1,0:T(8,128)} custom-call(f32[512,512]{1,0:T(8,128)} %fusion.245.block_ref), custom_call_target="tpu_custom_call" | custom-call | tf_op jit(solution)/shard_map/pallas_call | solution.py:138
  566.6 39.0 %all-gather.8.cloned.1.call-done = f32[512,1024]{1,0:T(8,128)} async-done(((f32[32,1024]{1,0:T(8,128)}), f32[512,1024]{1,0:T(8,128)}) %all-gather.8.cloned.1.call-update) | async-done | bytes 2097168 | tf_op jit(solution)/shard_map/all_gather | solution.py:234
  612.6 11.7 %cholesky.282 = f32[128,128]{1,0:T(8,128)S(1)} custom-call(f32[128,128]{1,0:T(8,128)S(1)} %fusion.175), custom_call_target="Cholesky" | custom-call | tf_op jit(solution)/shard_map/jit(cholesky)/cholesky | solution.py:49
  625.7 9.8 %custom-call.24 = f32[1,128,128]{1,2,0:T(8,128)S(1)} custom-call(f32[1,128,128]{2,1,0:T(8,128)S(1)} %get-tuple-element.13), custom_call_target="InvertDiagBlocksLowerTriangular" | custom-call | tf_op jit(solution)/shard_map/jit(_solve_triangular)/triangular_solve | solution.py:31
  637.1 11.9 %cholesky.293 = f32[128,128]{1,0:T(8,128)S(1)} custom-call(f32[128,128]{1,0:T(8,128)S(1)} %fusion.173), custom_call_target="Cholesky" | custom-call | tf_op jit(solution)/shard_map/jit(cholesky)/cholesky | solution.py:49
  650.3 9.8 %custom-call.25 = f32[1,128,128]{1,2,0:T(8,128)S(1)} custom-call(f32[1,128,128]{2,1,0:T(8,128)S(1)} %get-tuple-element.11), custom_call_target="InvertDiagBlocksLowerTriangular" | custom-call | tf_op jit(solution)/shard_map/jit(_solve_triangular)/triangular_solve | solution.py:31
  670.1 13.2 %cholesky.304 = f32[128,128]{1,0:T(8,128)} custom-call(f32[128,128]{1,0:T(8,128)} %fusion.171), custom_call_target="Cholesky" | custom-call | tf_op jit(solution)/shard_map/jit(cholesky)/cholesky | solution.py:49
  686.9 11.4 %custom-call.26 = f32[1,128,128]{1,2,0:T(8,128)} custom-call(f32[1,128,128]{2,1,0:T(8,128)} %get-tuple-element.9), custom_call_target="InvertDiagBlocksLowerTriangular" | custom-call | tf_op jit(solution)/shard_map/jit(_solve_triangular)/triangular_solve | solution.py:31
  710.6 11.7 %cholesky.315 = f32[128,128]{1,0:T(8,128)S(1)} custom-call(f32[128,128]{1,0:T(8,128)S(1)} %fusion.169), custom_call_target="Cholesky" | custom-call | tf_op jit(solution)/shard_map/jit(cholesky)/cholesky | solution.py:49
  723.6 9.8 %custom-call.27 = f32[1,128,128]{1,2,0:T(8,128)S(1)} custom-call(f32[1,128,128]{2,1,0:T(8,128)S(1)} %fusion.143), custom_call_target="InvertDiagBlocksLowerTriangular" | custom-call | tf_op jit(solution)/shard_map/jit(_solve_triangular)/triangular_solve | solution.py:31
  (357 shorter events, 198.2 us)
Async XLA Ops:
  7.2 82.8 %reduce-scatter.4.cloned.1.call-start = ((), (), s32[]{:S(2)}) async-start(), calls=%async_computation.4 | async-start | bytes 3342336
  28.0 112.1 %all-gather.4.cloned.1.call-start = ((), (), s32[]{:S(2)}) async-start(), calls=%async_computation.1 | async-start | bytes 6684672 | tf_op jit(solution)/shard_map/all_gather | solution.py:187
  92.1 255.1 %all-gather.6.cloned.1.call-start = ((), (), s32[]{:S(2)}) async-start(), calls=%async_computation.2 | async-start | bytes 2228224 | tf_op jit(solution)/shard_map/all_gather | solution.py:213
  161.6 61.9 %copy-start.19 = (f32[128,128]{0,1:T(8,128)}, f32[128,128]{0,1:T(8,128)S(1)}, u32[]{:S(2)}) copy-start(f32[128,128]{0,1:T(8,128)S(1)} %get-tuple-element.30) | copy-start | bytes 196612
  186.2 37.3 %copy-start.23 = (f32[128,128]{0,1:T(8,128)}, f32[128,128]{0,1:T(8,128)S(1)}, u32[]{:S(2)}) copy-start(f32[128,128]{0,1:T(8,128)S(1)} %get-tuple-element.28) | copy-start | bytes 196612
  197.6 59.6 %copy-start.54 = (f32[256,256]{1,0:T(8,128)}, f32[256,256]{1,0:T(8,128)S(1)}, u32[]{:S(2)}) copy-start(f32[256,256]{1,0:T(8,128)S(1)} %select_maximum_fusion.8) | copy-start | bytes 786436
  212.5 44.7 %copy-start.31 = (f32[128,128]{0,1:T(8,128)}, f32[128,128]{0,1:T(8,128)S(1)}, u32[]{:S(2)}) copy-start(f32[128,128]{0,1:T(8,128)S(1)} %get-tuple-element.26) | copy-start | bytes 196612
  263.2 6.3 collective-permute-start
  271.5 40.6 %copy-start.43 = (f32[128,256]{1,0:T(8,128)S(1)}, f32[128,256]{1,0:T(8,128)}, u32[]{:S(2)}) copy-start(f32[128,256]{1,0:T(8,128)} %copy-done.41) | copy-start | bytes 393220
  271.5 40.6 %copy-start.47 = (f32[256,256]{1,0:T(8,128)S(1)}, f32[256,256]{1,0:T(8,128)}, u32[]{:S(2)}) copy-start(f32[256,256]{1,0:T(8,128)} %copy-done.46) | copy-start | bytes 786436
  271.5 40.6 %copy-start.50 = (f32[128,128]{1,0:T(8,128)S(1)}, f32[128,128]{1,0:T(8,128)}, u32[]{:S(2)}) copy-start(f32[128,128]{1,0:T(8,128)} %copy-done.49) | copy-start | bytes 196612
  271.5 40.6 %copy-start.56 = (f32[256,256]{1,0:T(8,128)S(1)}, f32[256,256]{1,0:T(8,128)}, u32[]{:S(2)}) copy-start(f32[256,256]{1,0:T(8,128)} %copy-done.54) | copy-start | bytes 786436
  271.5 40.6 %copy-start.60 = (f32[128,128]{1,0:T(8,128)S(1)}, f32[128,128]{1,0:T(8,128)}, u32[]{:S(2)}) copy-start(f32[128,128]{1,0:T(8,128)} %copy-done.58) | copy-start | bytes 196612
  303.2 4.1 collective-permute-start.1
  308.0 297.6 %all-gather.8.cloned.1.call-start = ((), (), s32[]{:S(2)}) async-start(), calls=%async_computation.3 | async-start | bytes 2228224 | tf_op jit(solution)/shard_map/all_gather | solution.py:234
  318.4 175.9 %collective-permute-start.2 = (f32[512,512]{1,0:T(8,128)S(1)}, f32[512,512]{1,0:T(8,128)}, u32[]{:S(2)}, u32[]{:S(2)}) collective-permute-start(f32[512,512]{1,0:T(8,128)S(1)} %copy-done.3), channel_id=1, source_target_pairs={{0,16},{16,0},{32,48},{48,32},{64,80},{80,64},{96,112},{112,96},{1... | collective-permute-start | bytes 3145736 | tf_op jit(solution)/shard_map/ppermute | solution.py:16
  354.2 50.3 %copy-start.5 = (f32[512,512]{0,1:T(8,128)}, f32[512,512]{0,1:T(8,128)S(1)}, u32[]{:S(2)}) copy-start(f32[512,512]{0,1:T(8,128)S(1)} %convolution_add_fusion.2) | copy-start | bytes 3145732
  367.5 36.9 %copy-start.17 = (f32[128,128]{0,1:T(8,128)}, f32[128,128]{0,1:T(8,128)S(1)}, u32[]{:S(2)}) copy-start(f32[128,128]{0,1:T(8,128)S(1)} %get-tuple-element.22) | copy-start | bytes 196612
  406.3 88.0 %copy-start = (f32[512,1024]{1,0:T(8,128)S(1)}, f32[512,1024]{1,0:T(8,128)}, u32[]{:S(2)}) copy-start(f32[512,1024]{1,0:T(8,128)} %all-gather.6.cloned.1.call-done) | copy-start | bytes 6291460
  507.1 10.8 %collective-permute-start.4 = (f32[96,512]{1,0:T(8,128)S(1)}, f32[96,512]{1,0:T(8,128)S(1)}, u32[]{:S(2)}, u32[]{:S(2)}) collective-permute-start(f32[96,512]{1,0:T(8,128)S(1)} %fusion.243), channel_id=1, source_target_pairs={{0,48},{16,32},{32,16},{48,0},{64,112},{80,96},{96,80},{112,64},{1... | collective-permute-start | bytes 589832 | tf_op jit(solution)/shard_map/ppermute | solution.py:16
  510.6 8.4 %collective-permute-start.3 = (f32[96,512]{1,0:T(8,128)S(1)}, f32[96,512]{1,0:T(8,128)S(1)}, u32[]{:S(2)}, u32[]{:S(2)}) collective-permute-start(f32[96,512]{1,0:T(8,128)S(1)} %fusion.243), channel_id=1, source_target_pairs={{0,32},{16,48},{32,0},{48,16},{64,96},{80,112},{96,64},{112,80},{1... | collective-permute-start | bytes 589832 | tf_op jit(solution)/shard_map/ppermute | solution.py:16
  519.0 39.6 %copy-start.8 = (f32[256,128]{0,1:T(8,128)S(1)}, f32[256,128]{0,1:T(8,128)}, u32[]{:S(2)}) copy-start(f32[256,128]{0,1:T(8,128)} %copy-done.7) | copy-start | bytes 393220
  519.0 39.6 %copy-start.18 = (f32[128,128]{0,1:T(8,128)S(1)}, f32[128,128]{0,1:T(8,128)}, u32[]{:S(2)}) copy-start(f32[128,128]{0,1:T(8,128)} %copy-done.17) | copy-start | bytes 196612
  519.0 39.5 %copy-start.22 = (f32[128,128]{0,1:T(8,128)S(1)}, f32[128,128]{0,1:T(8,128)}, u32[]{:S(2)}) copy-start(f32[128,128]{0,1:T(8,128)} %copy-done.21) | copy-start | bytes 196612
  519.0 39.5 %copy-start.30 = (f32[128,128]{0,1:T(8,128)S(1)}, f32[128,128]{0,1:T(8,128)}, u32[]{:S(2)}) copy-start(f32[128,128]{0,1:T(8,128)} %get-tuple-element.18) | copy-start | bytes 196612
  519.0 39.5 %copy-start.33 = (f32[128,128]{0,1:T(8,128)S(1)}, f32[128,128]{0,1:T(8,128)}, u32[]{:S(2)}) copy-start(f32[128,128]{0,1:T(8,128)} %copy.138) | copy-start | bytes 196612
  519.0 39.5 %copy-start.52 = (f32[128,128]{0,1:T(8,128)S(1)}, f32[128,128]{0,1:T(8,128)}, u32[]{:S(2)}) copy-start(f32[128,128]{0,1:T(8,128)} %get-tuple-element.16) | copy-start | bytes 196612
  520.1 45.2 %copy-start.13 = (f32[96,512]{1,0:T(8,128)S(1)}, f32[96,512]{1,0:T(8,128)}, u32[]{:S(2)}) copy-start(f32[96,512]{1,0:T(8,128)} %copy-done.11) | copy-start | bytes 589828
  554.4 4.1 collective-permute-start.5
  559.5 5.1 collective-permute-start.6
  612.5 49.6 %copy-start.4 = (f32[512,512]{0,1:T(8,128)}, f32[512,512]{0,1:T(8,128)S(1)}, u32[]{:S(2)}) copy-start(f32[512,512]{0,1:T(8,128)S(1)} %convolution_add_fusion) | copy-start | bytes 3145732
  662.1 74.2 %copy-start.1 = (f32[512,1024]{1,0:T(8,128)S(1)}, f32[512,1024]{1,0:T(8,128)}, u32[]{:S(2)}) copy-start(f32[512,1024]{1,0:T(8,128)} %all-gather.8.cloned.1.call-done) | copy-start | bytes 6291460
  (45 other events, 503.3 us)
Sparse Core Ops, SparseCore 0:
  28.2 61.7 reduce-scatter.3
  92.2 47.9 all-gather.3
  308.1 39.0 all-gather.5
  565.4 40.1 all-gather.7

commit v9 on v7

--- a/solution.py
+++ b/solution.py
@@ -224,8 +224,10 @@
     panel_two = product(basis_rows, product(transfer_own, parent_reduced))
     cousin_rows = swap(panel_two, "node", 2)
     further_rows = swap(panel_two, "node", 3)
-    far_sum = transposed(cousin_meet, cousin_rows) + transposed(further_meet, further_rows)
-    far_part = tile_scatter(transposed(transfer_own, far_sum), 5)
+    cousin_side = product(cousin_meet, transfer_own)
+    further_side = product(further_meet, transfer_own)
+    far_sum = transposed(cousin_side, cousin_rows) + transposed(further_side, further_rows)
+    far_part = tile_scatter(far_sum, 5)
     far_pair = far_part + swap(far_part, "node", 1)
     grand_part = lax.dynamic_slice_in_dim(parent_factor.T, tile * chunk, chunk, 0) - far_pair
     cousin_part = swap(grand_part, "node", 2)

time: 691 us -> 689 us (level)
    dot_general x13 -> x12, matrix products: 60.4 us -> 58.6 us  [transposed(): lax.dot_general(left, right, (((0,), (0,)), ((), ())), precision=HIGH, pr...]
    dot_general x51 -> x53, matrix products: 47.3 us -> 48.8 us  [product(): jnp.dot(left, right, precision=HIGH, preferred_element_type=jnp.float32)]
where the time goes in v9:
time: 689 us; the launch traced here: 685 us
  other arithmetic  284 us (41%)
  waiting for transfers between devices  191 us (28%)
  matrix products  111 us (16%)
  Pallas kernels  61.3 us (9%)
  between operations  16 us (2%)
  local copies, waits for them, and re-layouts  12.5 us (2%)
  starting transfers between devices  9.9 us (1%)
    another operation x36, other arithmetic, factor_pair(): diagonal = jnp.linalg.cholesky(column[:block])  150 us
    another operation x24, other arithmetic, inverse_lower(): return jax.scipy.linalg.solve_triangular(factor, eye, lower=True)  127 us
    pallas_call x2, Pallas kernels, tile_scatter(): pl.pallas_call(functools.partial(scatter_kernel, count), out_shape=jax.Sh...  61.3 us
    unnamed x5, waiting for transfers between devices  60.9 us
    dot_general x12, matrix products, transposed(): lax.dot_general(left, right, (((0,), (0,)), ((), ())), precision=HIGH, pr...  58.6 us
    dot_general x53, matrix products, product(): jnp.dot(left, right, precision=HIGH, preferred_element_type=jnp.float32)  48.8 us
    all_gather x1, waiting for transfers between devices, on_device(): lax.all_gather(jnp.concatenate([sample_rows, owned], axis=1), 'tile', axi...  47.9 us
    all_gather x1, waiting for transfers between devices, on_device(): lax.all_gather(jnp.concatenate([grand_part, cousin_part], axis=1), 'tile'...  38.9 us
  transfers between devices with their start and end apart: 11, of which 8 were waited for; matrix products, arithmetic and copies ran while one was open for 20% of the time, Pallas kernels for 0%

profile of v9, /device:TPU:1, one launch (start us, length us, event | category | flops | bytes accessed | tf_op | source)
XLA Modules:
  0.0 684.8 jit_solution(8237640723774720690)
XLA Ops:
  7.2 18.4 %convolution_bitcast_fusion = f32[1536,512]{0,1:T(8,128)S(1)} fusion(f32[16,96,1536]{2,1,0:T(8,128)} %param.5, f32[16,96,512]{2,1,0:T(8,128)} %param.6, pred[16]{0:T(512)(128)(4,1)S(1)} %iota_compare_fusion.19), kind=kOutput, calls=%fused_computation | convolution fusion | flops 14496301056 | bytes 15728656 | tf_op jit(solution)/shard_map/dot_general | solution.py:24
  29.2 60.8 %reduce-scatter.4.cloned.1.call-done = f32[96,512]{1,0:T(8,128)} async-done(((f32[1536,512]{1,0:T(8,128)}), f32[96,512]{1,0:T(8,128)}) %reduce-scatter.4.cloned.1.call-update) | async-done | bytes 196624
  92.3 47.9 %all-gather.4.cloned.1.call-done = f32[1536,1024]{1,0:T(8,128)} async-done(((f32[96,1024]{1,0:T(8,128)}), f32[1536,1024]{1,0:T(8,128)}) %all-gather.4.cloned.1.call-update) | async-done | bytes 6291472 | tf_op jit(solution)/shard_map/all_gather | solution.py:187
  148.4 11.7 %cholesky.194 = f32[128,128]{1,0:T(8,128)S(1)} custom-call(f32[128,128]{1,0:T(8,128)S(1)} %get-tuple-element.32), custom_call_target="Cholesky" | custom-call | tf_op jit(solution)/shard_map/jit(cholesky)/cholesky | solution.py:49
  161.7 9.8 %custom-call.16 = f32[1,128,128]{1,2,0:T(8,128)S(1)} custom-call(f32[1,128,128]{2,1,0:T(8,128)S(1)} %copy.91), custom_call_target="InvertDiagBlocksLowerTriangular" | custom-call | tf_op jit(solution)/shard_map/jit(_solve_triangular)/triangular_solve | solution.py:31
  173.0 11.7 %cholesky.205 = f32[128,128]{1,0:T(8,128)S(1)} custom-call(f32[128,128]{1,0:T(8,128)S(1)} %fusion.187), custom_call_target="Cholesky" | custom-call | tf_op jit(solution)/shard_map/jit(cholesky)/cholesky | solution.py:49
  186.4 9.8 %custom-call.17 = f32[1,128,128]{1,2,0:T(8,128)S(1)} custom-call(f32[1,128,128]{2,1,0:T(8,128)S(1)} %copy.97), custom_call_target="InvertDiagBlocksLowerTriangular" | custom-call | tf_op jit(solution)/shard_map/jit(_solve_triangular)/triangular_solve | solution.py:31
  198.9 12.2 %cholesky.216 = f32[128,128]{1,0:T(8,128)S(1)} custom-call(f32[128,128]{1,0:T(8,128)S(1)} %fusion.185), custom_call_target="Cholesky" | custom-call | tf_op jit(solution)/shard_map/jit(cholesky)/cholesky | solution.py:49
  212.7 9.8 %custom-call.18 = f32[1,128,128]{1,2,0:T(8,128)S(1)} custom-call(f32[1,128,128]{2,1,0:T(8,128)S(1)} %copy.107), custom_call_target="InvertDiagBlocksLowerTriangular" | custom-call | tf_op jit(solution)/shard_map/jit(_solve_triangular)/triangular_solve | solution.py:31
  224.2 11.7 %cholesky.227 = f32[128,128]{1,0:T(8,128)S(1)} custom-call(f32[128,128]{1,0:T(8,128)S(1)} %fusion.183), custom_call_target="Cholesky" | custom-call | tf_op jit(solution)/shard_map/jit(cholesky)/cholesky | solution.py:49
  238.1 9.8 %custom-call.19 = f32[1,128,128]{1,2,0:T(8,128)S(1)} custom-call(f32[1,128,128]{2,1,0:T(8,128)S(1)} %copy.114), custom_call_target="InvertDiagBlocksLowerTriangular" | custom-call | tf_op jit(solution)/shard_map/jit(_solve_triangular)/triangular_solve | solution.py:31
  249.0 8.3 %fusion = f32[512,512]{1,0:T(8,128)S(1)} fusion(f32[1536,1024]{1,0:T(8,128)} %all-gather.4.cloned.1.call-done), kind=kOutput, calls=%fused_computation.1 | convolution fusion | flops 4831838208 | bytes 7340032 | tf_op jit(solution)/shard_map/dot_general | solution.py:24
  271.6 30.7 %shard_map.49 = f32[32,512]{1,0:T(8,128)} custom-call(f32[512,512]{1,0:T(8,128)} %fusion.238.block_ref), custom_call_target="tpu_custom_call" | custom-call | tf_op jit(solution)/shard_map/pallas_call | solution.py:138
  321.0 26.2 %all-gather.6.cloned.1.call-done = f32[512,1024]{1,0:T(8,128)} async-done(((f32[32,1024]{1,0:T(8,128)}), f32[512,1024]{1,0:T(8,128)}) %all-gather.6.cloned.1.call-update) | async-done | bytes 2097168 | tf_op jit(solution)/shard_map/all_gather | solution.py:213
  354.4 11.7 %cholesky.238 = f32[128,128]{1,0:T(8,128)S(1)} custom-call(f32[128,128]{1,0:T(8,128)S(1)} %fusion.181), custom_call_target="Cholesky" | custom-call | tf_op jit(solution)/shard_map/jit(cholesky)/cholesky | solution.py:49
  367.7 9.8 %custom-call.20 = f32[1,128,128]{1,2,0:T(8,128)S(1)} custom-call(f32[1,128,128]{2,1,0:T(8,128)S(1)} %copy.123), custom_call_target="InvertDiagBlocksLowerTriangular" | custom-call | tf_op jit(solution)/shard_map/jit(_solve_triangular)/triangular_solve | solution.py:31
  379.2 11.9 %cholesky.249 = f32[128,128]{1,0:T(8,128)S(1)} custom-call(f32[128,128]{1,0:T(8,128)S(1)} %fusion.179), custom_call_target="Cholesky" | custom-call | tf_op jit(solution)/shard_map/jit(cholesky)/cholesky | solution.py:49
  392.7 9.8 %custom-call.21 = f32[1,128,128]{1,2,0:T(8,128)S(1)} custom-call(f32[1,128,128]{2,1,0:T(8,128)S(1)} %copy.128), custom_call_target="InvertDiagBlocksLowerTriangular" | custom-call | tf_op jit(solution)/shard_map/jit(_solve_triangular)/triangular_solve | solution.py:31
  406.1 11.7 %cholesky.260 = f32[128,128]{1,0:T(8,128)S(1)} custom-call(f32[128,128]{1,0:T(8,128)S(1)} %fusion.177), custom_call_target="Cholesky" | custom-call | tf_op jit(solution)/shard_map/jit(cholesky)/cholesky | solution.py:49
  419.5 10.2 %custom-call.22 = f32[1,128,128]{1,2,0:T(8,128)S(1)} custom-call(f32[1,128,128]{2,1,0:T(8,128)S(1)} %copy.137), custom_call_target="InvertDiagBlocksLowerTriangular" | custom-call | tf_op jit(solution)/shard_map/jit(_solve_triangular)/triangular_solve | solution.py:31
  431.2 11.7 %cholesky.271 = f32[128,128]{1,0:T(8,128)S(1)} custom-call(f32[128,128]{1,0:T(8,128)S(1)} %fusion.175), custom_call_target="Cholesky" | custom-call | tf_op jit(solution)/shard_map/jit(cholesky)/cholesky | solution.py:49
  445.1 9.8 %custom-call.23 = f32[1,128,128]{1,2,0:T(8,128)S(1)} custom-call(f32[1,128,128]{2,1,0:T(8,128)S(1)} %copy.143), custom_call_target="InvertDiagBlocksLowerTriangular" | custom-call | tf_op jit(solution)/shard_map/jit(_solve_triangular)/triangular_solve | solution.py:31
  484.9 30.5 %shard_map.50 = f32[32,512]{1,0:T(8,128)} custom-call(f32[512,512]{1,0:T(8,128)} %convolution_add_fusion.3.block_ref), custom_call_target="tpu_custom_call" | custom-call | tf_op jit(solution)/shard_map/pallas_call | solution.py:138
  527.6 38.9 %all-gather.8.cloned.1.call-done = f32[512,1024]{1,0:T(8,128)} async-done(((f32[32,1024]{1,0:T(8,128)}), f32[512,1024]{1,0:T(8,128)}) %all-gather.8.cloned.1.call-update) | async-done | bytes 2097168 | tf_op jit(solution)/shard_map/all_gather | solution.py:234
  573.6 11.7 %cholesky.282 = f32[128,128]{1,0:T(8,128)S(1)} custom-call(f32[128,128]{1,0:T(8,128)S(1)} %fusion.173), custom_call_target="Cholesky" | custom-call | tf_op jit(solution)/shard_map/jit(cholesky)/cholesky | solution.py:49
  586.7 9.8 %custom-call.24 = f32[1,128,128]{1,2,0:T(8,128)S(1)} custom-call(f32[1,128,128]{2,1,0:T(8,128)S(1)} %get-tuple-element.13), custom_call_target="InvertDiagBlocksLowerTriangular" | custom-call | tf_op jit(solution)/shard_map/jit(_solve_triangular)/triangular_solve | solution.py:31
  598.1 11.9 %cholesky.293 = f32[128,128]{1,0:T(8,128)S(1)} custom-call(f32[128,128]{1,0:T(8,128)S(1)} %fusion.171), custom_call_target="Cholesky" | custom-call | tf_op jit(solution)/shard_map/jit(cholesky)/cholesky | solution.py:49
  611.4 9.8 %custom-call.25 = f32[1,128,128]{1,2,0:T(8,128)S(1)} custom-call(f32[1,128,128]{2,1,0:T(8,128)S(1)} %get-tuple-element.11), custom_call_target="InvertDiagBlocksLowerTriangular" | custom-call | tf_op jit(solution)/shard_map/jit(_solve_triangular)/triangular_solve | solution.py:31
  625.0 11.7 %cholesky.304 = f32[128,128]{1,0:T(8,128)S(1)} custom-call(f32[128,128]{1,0:T(8,128)S(1)} %fusion.169), custom_call_target="Cholesky" | custom-call | tf_op jit(solution)/shard_map/jit(cholesky)/cholesky | solution.py:49
  638.1 10.0 %custom-call.26 = f32[1,128,128]{1,2,0:T(8,128)S(1)} custom-call(f32[1,128,128]{2,1,0:T(8,128)S(1)} %get-tuple-element.9), custom_call_target="InvertDiagBlocksLowerTriangular" | custom-call | tf_op jit(solution)/shard_map/jit(_solve_triangular)/triangular_solve | solution.py:31
  649.7 11.7 %cholesky.315 = f32[128,128]{1,0:T(8,128)S(1)} custom-call(f32[128,128]{1,0:T(8,128)S(1)} %fusion.167), custom_call_target="Cholesky" | custom-call | tf_op jit(solution)/shard_map/jit(cholesky)/cholesky | solution.py:49
  662.7 9.8 %custom-call.27 = f32[1,128,128]{1,2,0:T(8,128)S(1)} custom-call(f32[1,128,128]{2,1,0:T(8,128)S(1)} %fusion.141), custom_call_target="InvertDiagBlocksLowerTriangular" | custom-call | tf_op jit(solution)/shard_map/jit(_solve_triangular)/triangular_solve | solution.py:31
  (316 shorter events, 147.4 us)
Async XLA Ops:
  7.2 82.8 %reduce-scatter.4.cloned.1.call-start = ((), (), s32[]{:S(2)}) async-start(), calls=%async_computation.4 | async-start | bytes 3342336
  28.1 112.1 %all-gather.4.cloned.1.call-start = ((), (), s32[]{:S(2)}) async-start(), calls=%async_computation.1 | async-start | bytes 6684672 | tf_op jit(solution)/shard_map/all_gather | solution.py:187
  92.1 255.2 %all-gather.6.cloned.1.call-start = ((), (), s32[]{:S(2)}) async-start(), calls=%async_computation.2 | async-start | bytes 2228224 | tf_op jit(solution)/shard_map/all_gather | solution.py:213
  161.6 61.9 %copy-start.11 = (f32[128,128]{0,1:T(8,128)}, f32[128,128]{0,1:T(8,128)S(1)}, u32[]{:S(2)}) copy-start(f32[128,128]{0,1:T(8,128)S(1)} %get-tuple-element.30) | copy-start | bytes 196612
  186.2 37.3 %copy-start.15 = (f32[128,128]{0,1:T(8,128)}, f32[128,128]{0,1:T(8,128)S(1)}, u32[]{:S(2)}) copy-start(f32[128,128]{0,1:T(8,128)S(1)} %get-tuple-element.28) | copy-start | bytes 196612
  197.6 59.6 %copy-start.36 = (f32[256,256]{1,0:T(8,128)}, f32[256,256]{1,0:T(8,128)S(1)}, u32[]{:S(2)}) copy-start(f32[256,256]{1,0:T(8,128)S(1)} %select_maximum_fusion.8) | copy-start | bytes 786436
  212.5 44.7 %copy-start.21 = (f32[128,128]{0,1:T(8,128)}, f32[128,128]{0,1:T(8,128)S(1)}, u32[]{:S(2)}) copy-start(f32[128,128]{0,1:T(8,128)S(1)} %get-tuple-element.26) | copy-start | bytes 196612
  263.2 6.3 collective-permute-start
  271.5 40.6 %copy-start.29 = (f32[128,256]{1,0:T(8,128)S(1)}, f32[128,256]{1,0:T(8,128)}, u32[]{:S(2)}) copy-start(f32[128,256]{1,0:T(8,128)} %copy-done.27) | copy-start | bytes 393220
  271.5 40.6 %copy-start.31 = (f32[256,256]{1,0:T(8,128)S(1)}, f32[256,256]{1,0:T(8,128)}, u32[]{:S(2)}) copy-start(f32[256,256]{1,0:T(8,128)} %copy-done.30) | copy-start | bytes 786436
  271.5 40.6 %copy-start.33 = (f32[128,128]{1,0:T(8,128)S(1)}, f32[128,128]{1,0:T(8,128)}, u32[]{:S(2)}) copy-start(f32[128,128]{1,0:T(8,128)} %copy-done.32) | copy-start | bytes 196612
  271.5 40.6 %copy-start.38 = (f32[256,256]{1,0:T(8,128)S(1)}, f32[256,256]{1,0:T(8,128)}, u32[]{:S(2)}) copy-start(f32[256,256]{1,0:T(8,128)} %copy-done.36) | copy-start | bytes 786436
  271.5 40.6 %copy-start.41 = (f32[128,128]{1,0:T(8,128)S(1)}, f32[128,128]{1,0:T(8,128)}, u32[]{:S(2)}) copy-start(f32[128,128]{1,0:T(8,128)} %copy-done.39) | copy-start | bytes 196612
  303.3 4.1 collective-permute-start.1
  308.0 258.6 %all-gather.8.cloned.1.call-start = ((), (), s32[]{:S(2)}) async-start(), calls=%async_computation.3 | async-start | bytes 2228224 | tf_op jit(solution)/shard_map/all_gather | solution.py:234
  319.4 144.9 %collective-permute-start.2 = (f32[512,512]{1,0:T(8,128)S(1)}, f32[512,512]{1,0:T(8,128)}, u32[]{:S(2)}, u32[]{:S(2)}) collective-permute-start(f32[512,512]{1,0:T(8,128)S(1)} %copy-done.1), channel_id=1, source_target_pairs={{0,16},{16,0},{32,48},{48,32},{64,80},{80,64},{96,112},{112,96},{1... | collective-permute-start | bytes 3145736 | tf_op jit(solution)/shard_map/ppermute | solution.py:16
  367.6 63.0 %copy-start.9 = (f32[128,128]{0,1:T(8,128)}, f32[128,128]{0,1:T(8,128)S(1)}, u32[]{:S(2)}) copy-start(f32[128,128]{0,1:T(8,128)S(1)} %get-tuple-element.22) | copy-start | bytes 196612
  392.6 38.5 %copy-start.13 = (f32[128,128]{0,1:T(8,128)}, f32[128,128]{0,1:T(8,128)S(1)}, u32[]{:S(2)}) copy-start(f32[128,128]{0,1:T(8,128)S(1)} %get-tuple-element.20) | copy-start | bytes 196612
  406.0 49.6 %copy-start.18 = (f32[256,256]{1,0:T(8,128)S(1)}, f32[256,256]{1,0:T(8,128)}, u32[]{:S(2)}) copy-start(f32[256,256]{1,0:T(8,128)} %fusion.85) | copy-start | bytes 786436
  419.4 39.7 %copy-start.19 = (f32[128,128]{0,1:T(8,128)}, f32[128,128]{0,1:T(8,128)S(1)}, u32[]{:S(2)}) copy-start(f32[128,128]{0,1:T(8,128)S(1)} %get-tuple-element.18) | copy-start | bytes 196612
  470.1 11.8 %collective-permute-start.4 = (f32[96,512]{1,0:T(8,128)S(1)}, f32[96,512]{1,0:T(8,128)S(1)}, u32[]{:S(2)}, u32[]{:S(2)}) collective-permute-start(f32[96,512]{1,0:T(8,128)S(1)} %fusion.243), channel_id=1, source_target_pairs={{0,48},{16,32},{32,16},{48,0},{64,112},{80,96},{96,80},{112,64},{1... | collective-permute-start | bytes 589832 | tf_op jit(solution)/shard_map/ppermute | solution.py:16
  472.6 10.2 %collective-permute-start.3 = (f32[96,512]{1,0:T(8,128)S(1)}, f32[96,512]{1,0:T(8,128)S(1)}, u32[]{:S(2)}, u32[]{:S(2)}) collective-permute-start(f32[96,512]{1,0:T(8,128)S(1)} %fusion.243), channel_id=1, source_target_pairs={{0,32},{16,48},{32,0},{48,16},{64,96},{80,112},{96,64},{112,80},{1... | collective-permute-start | bytes 589832 | tf_op jit(solution)/shard_map/ppermute | solution.py:16
  473.9 46.0 %copy-start.3 = (f32[256,128]{0,1:T(8,128)S(1)}, f32[256,128]{0,1:T(8,128)}, u32[]{:S(2)}) copy-start(f32[256,128]{0,1:T(8,128)} %copy-done.2) | copy-start | bytes 393220
  473.9 46.0 %copy-start.10 = (f32[128,128]{0,1:T(8,128)S(1)}, f32[128,128]{0,1:T(8,128)}, u32[]{:S(2)}) copy-start(f32[128,128]{0,1:T(8,128)} %copy-done.9) | copy-start | bytes 196612
  473.9 46.0 %copy-start.14 = (f32[128,128]{0,1:T(8,128)S(1)}, f32[128,128]{0,1:T(8,128)}, u32[]{:S(2)}) copy-start(f32[128,128]{0,1:T(8,128)} %copy-done.13) | copy-start | bytes 196612
  473.9 46.0 %copy-start.20 = (f32[128,128]{0,1:T(8,128)S(1)}, f32[128,128]{0,1:T(8,128)}, u32[]{:S(2)}) copy-start(f32[128,128]{0,1:T(8,128)} %copy-done.19) | copy-start | bytes 196612
  473.9 46.0 %copy-start.24 = (f32[128,128]{0,1:T(8,128)S(1)}, f32[128,128]{0,1:T(8,128)}, u32[]{:S(2)}) copy-start(f32[128,128]{0,1:T(8,128)} %copy-done.23) | copy-start | bytes 196612
  474.0 46.0 %copy-start.34 = (f32[128,128]{0,1:T(8,128)S(1)}, f32[128,128]{0,1:T(8,128)}, u32[]{:S(2)}) copy-start(f32[128,128]{0,1:T(8,128)} %get-tuple-element.16) | copy-start | bytes 196612
  474.7 51.6 %copy-start.8 = (f32[96,512]{1,0:T(8,128)S(1)}, f32[96,512]{1,0:T(8,128)}, u32[]{:S(2)}) copy-start(f32[96,512]{1,0:T(8,128)} %copy-done.6) | copy-start | bytes 589828
  515.4 4.5 collective-permute-start.5
  520.9 4.7 collective-permute-start.6
  624.9 48.3 %copy-start.17 = (f32[256,256]{1,0:T(8,128)S(1)}, f32[256,256]{1,0:T(8,128)}, u32[]{:S(2)}) copy-start(f32[256,256]{1,0:T(8,128)} %fusion.82) | copy-start | bytes 786436
  (24 other events, 439.4 us)
Sparse Core Ops, SparseCore 0:
  28.2 61.7 reduce-scatter.3
  92.2 47.9 all-gather.3
  308.2 39.0 all-gather.5
  526.4 40.1 all-gather.7

commit v10 on v9

--- a/solution.py
+++ b/solution.py
@@ -238,11 +238,10 @@
     grand_factor, grand_inverse = factor_pair(
         transposed(grand_sample, grand_sample) + transposed(cousin_grand, cousin_grand)
     )
-    grand_transfer = product(grand_sample, grand_inverse.T)
     leaf_out = (basis_rows * math.sqrt(leaf_rows))[None]
     one_rows = lax.dynamic_slice_in_dim(transfer_own, tile * out_rows, out_rows, 0)
     level_one = (one_rows * math.sqrt(2 * rank_size))[None]
-    two_rows = product(one_rows, grand_transfer)
+    two_rows = product(product(one_rows, grand_sample), grand_inverse.T)
     level_two = (two_rows * (2.0 * math.sqrt(rank_size)))[None]
     return (leaf_out, level_one, level_two)
 

time: 689 us -> 712 us (1.033)
  local copies, waits for them, and re-layouts: 12.5 us -> 21.2 us
  transfers between devices with their start and end apart: 11 -> 11, of which waited for: 8 -> 8; matrix products, arithmetic and copies ran while one was open for 20% -> 19% of each run, Pallas kernels for 0% -> 0%
where the time goes in v10:
time: 712 us; the launch traced here: 708 us
  other arithmetic  291 us (41%)
  waiting for transfers between devices  191 us (27%)
  matrix products  117 us (16%)
  Pallas kernels  61.2 us (9%)
  local copies, waits for them, and re-layouts  21.2 us (3%)
  between operations  16.1 us (2%)
  starting transfers between devices  9.91 us (1%)
    another operation x36, other arithmetic, factor_pair(): diagonal = jnp.linalg.cholesky(column[:block])  152 us
    another operation x24, other arithmetic, inverse_lower(): return jax.scipy.linalg.solve_triangular(factor, eye, lower=True)  130 us
    pallas_call x2, Pallas kernels, tile_scatter(): pl.pallas_call(functools.partial(scatter_kernel, count), out_shape=jax.Sh...  61.2 us
    unnamed x5, waiting for transfers between devices  60.9 us
    dot_general x12, matrix products, transposed(): lax.dot_general(left, right, (((0,), (0,)), ((), ())), precision=HIGH, pr...  58.5 us
    dot_general x53, matrix products, product(): jnp.dot(left, right, precision=HIGH, preferred_element_type=jnp.float32)  54.3 us
    all_gather x1, waiting for transfers between devices, on_device(): lax.all_gather(jnp.concatenate([sample_rows, owned], axis=1), 'tile', axi...  47.9 us
    all_gather x1, waiting for transfers between devices, on_device(): lax.all_gather(jnp.concatenate([grand_part, cousin_part], axis=1), 'tile'...  39 us
  transfers between devices with their start and end apart: 11, of which 8 were waited for; matrix products, arithmetic and copies ran while one was open for 19% of the time, Pallas kernels for 0%

profile of v10, /device:TPU:1, one launch (start us, length us, event | category | flops | bytes accessed | tf_op | source)
XLA Modules:
  0.0 707.6 jit_solution(13170561810467306705)
XLA Ops:
  7.2 18.4 %convolution_bitcast_fusion = f32[1536,512]{0,1:T(8,128)S(1)} fusion(f32[16,96,1536]{2,1,0:T(8,128)} %param.5, f32[16,96,512]{2,1,0:T(8,128)} %param.6, pred[16]{0:T(512)(128)(4,1)S(1)} %iota_compare_fusion.19), kind=kOutput, calls=%fused_computation | convolution fusion | flops 14496301056 | bytes 15728656 | tf_op jit(solution)/shard_map/dot_general | solution.py:24
  29.2 60.8 %reduce-scatter.4.cloned.1.call-done = f32[96,512]{1,0:T(8,128)} async-done(((f32[1536,512]{1,0:T(8,128)}), f32[96,512]{1,0:T(8,128)}) %reduce-scatter.4.cloned.1.call-update) | async-done | bytes 196624
  92.3 47.9 %all-gather.4.cloned.1.call-done = f32[1536,1024]{1,0:T(8,128)} async-done(((f32[96,1024]{1,0:T(8,128)}), f32[1536,1024]{1,0:T(8,128)}) %all-gather.4.cloned.1.call-update) | async-done | bytes 6291472 | tf_op jit(solution)/shard_map/all_gather | solution.py:187
  148.4 11.7 %cholesky.194 = f32[128,128]{1,0:T(8,128)S(1)} custom-call(f32[128,128]{1,0:T(8,128)S(1)} %get-tuple-element.32), custom_call_target="Cholesky" | custom-call | tf_op jit(solution)/shard_map/jit(cholesky)/cholesky | solution.py:49
  161.7 9.8 %custom-call.16 = f32[1,128,128]{1,2,0:T(8,128)S(1)} custom-call(f32[1,128,128]{2,1,0:T(8,128)S(1)} %copy.91), custom_call_target="InvertDiagBlocksLowerTriangular" | custom-call | tf_op jit(solution)/shard_map/jit(_solve_triangular)/triangular_solve | solution.py:31
  173.0 11.7 %cholesky.205 = f32[128,128]{1,0:T(8,128)S(1)} custom-call(f32[128,128]{1,0:T(8,128)S(1)} %fusion.187), custom_call_target="Cholesky" | custom-call | tf_op jit(solution)/shard_map/jit(cholesky)/cholesky | solution.py:49
  186.4 9.8 %custom-call.17 = f32[1,128,128]{1,2,0:T(8,128)S(1)} custom-call(f32[1,128,128]{2,1,0:T(8,128)S(1)} %copy.97), custom_call_target="InvertDiagBlocksLowerTriangular" | custom-call | tf_op jit(solution)/shard_map/jit(_solve_triangular)/triangular_solve | solution.py:31
  198.9 12.2 %cholesky.216 = f32[128,128]{1,0:T(8,128)S(1)} custom-call(f32[128,128]{1,0:T(8,128)S(1)} %fusion.185), custom_call_target="Cholesky" | custom-call | tf_op jit(solution)/shard_map/jit(cholesky)/cholesky | solution.py:49
  212.7 9.8 %custom-call.18 = f32[1,128,128]{1,2,0:T(8,128)S(1)} custom-call(f32[1,128,128]{2,1,0:T(8,128)S(1)} %copy.107), custom_call_target="InvertDiagBlocksLowerTriangular" | custom-call | tf_op jit(solution)/shard_map/jit(_solve_triangular)/triangular_solve | solution.py:31
  224.2 11.7 %cholesky.227 = f32[128,128]{1,0:T(8,128)S(1)} custom-call(f32[128,128]{1,0:T(8,128)S(1)} %fusion.183), custom_call_target="Cholesky" | custom-call | tf_op jit(solution)/shard_map/jit(cholesky)/cholesky | solution.py:49
  238.1 9.8 %custom-call.19 = f32[1,128,128]{1,2,0:T(8,128)S(1)} custom-call(f32[1,128,128]{2,1,0:T(8,128)S(1)} %copy.114), custom_call_target="InvertDiagBlocksLowerTriangular" | custom-call | tf_op jit(solution)/shard_map/jit(_solve_triangular)/triangular_solve | solution.py:31
  249.0 8.3 %fusion = f32[512,512]{1,0:T(8,128)S(1)} fusion(f32[1536,1024]{1,0:T(8,128)} %all-gather.4.cloned.1.call-done), kind=kOutput, calls=%fused_computation.1 | convolution fusion | flops 4831838208 | bytes 7340032 | tf_op jit(solution)/shard_map/dot_general | solution.py:24
  271.5 30.7 %shard_map.49 = f32[32,512]{1,0:T(8,128)} custom-call(f32[512,512]{1,0:T(8,128)} %fusion.238.block_ref), custom_call_target="tpu_custom_call" | custom-call | tf_op jit(solution)/shard_map/pallas_call | solution.py:138
  321.0 26.2 %all-gather.6.cloned.1.call-done = f32[512,1024]{1,0:T(8,128)} async-done(((f32[32,1024]{1,0:T(8,128)}), f32[512,1024]{1,0:T(8,128)}) %all-gather.6.cloned.1.call-update) | async-done | bytes 2097168 | tf_op jit(solution)/shard_map/all_gather | solution.py:213
  354.3 11.7 %cholesky.238 = f32[128,128]{1,0:T(8,128)S(1)} custom-call(f32[128,128]{1,0:T(8,128)S(1)} %fusion.181), custom_call_target="Cholesky" | custom-call | tf_op jit(solution)/shard_map/jit(cholesky)/cholesky | solution.py:49
  367.7 9.8 %custom-call.20 = f32[1,128,128]{1,2,0:T(8,128)S(1)} custom-call(f32[1,128,128]{2,1,0:T(8,128)S(1)} %copy.123), custom_call_target="InvertDiagBlocksLowerTriangular" | custom-call | tf_op jit(solution)/shard_map/jit(_solve_triangular)/triangular_solve | solution.py:31
  379.1 11.9 %cholesky.249 = f32[128,128]{1,0:T(8,128)S(1)} custom-call(f32[128,128]{1,0:T(8,128)S(1)} %fusion.179), custom_call_target="Cholesky" | custom-call | tf_op jit(solution)/shard_map/jit(cholesky)/cholesky | solution.py:49
  392.6 9.8 %custom-call.21 = f32[1,128,128]{1,2,0:T(8,128)S(1)} custom-call(f32[1,128,128]{2,1,0:T(8,128)S(1)} %copy.128), custom_call_target="InvertDiagBlocksLowerTriangular" | custom-call | tf_op jit(solution)/shard_map/jit(_solve_triangular)/triangular_solve | solution.py:31
  406.1 11.7 %cholesky.260 = f32[128,128]{1,0:T(8,128)S(1)} custom-call(f32[128,128]{1,0:T(8,128)S(1)} %fusion.177), custom_call_target="Cholesky" | custom-call | tf_op jit(solution)/shard_map/jit(cholesky)/cholesky | solution.py:49
  419.4 10.2 %custom-call.22 = f32[1,128,128]{1,2,0:T(8,128)S(1)} custom-call(f32[1,128,128]{2,1,0:T(8,128)S(1)} %copy.137), custom_call_target="InvertDiagBlocksLowerTriangular" | custom-call | tf_op jit(solution)/shard_map/jit(_solve_triangular)/triangular_solve | solution.py:31
  431.2 11.7 %cholesky.271 = f32[128,128]{1,0:T(8,128)S(1)} custom-call(f32[128,128]{1,0:T(8,128)S(1)} %fusion.175), custom_call_target="Cholesky" | custom-call | tf_op jit(solution)/shard_map/jit(cholesky)/cholesky | solution.py:49
  445.2 9.8 %custom-call.23 = f32[1,128,128]{1,2,0:T(8,128)S(1)} custom-call(f32[1,128,128]{2,1,0:T(8,128)S(1)} %copy.143), custom_call_target="InvertDiagBlocksLowerTriangular" | custom-call | tf_op jit(solution)/shard_map/jit(_solve_triangular)/triangular_solve | solution.py:31
  485.0 30.5 %shard_map.50 = f32[32,512]{1,0:T(8,128)} custom-call(f32[512,512]{1,0:T(8,128)} %convolution_add_fusion.3.block_ref), custom_call_target="tpu_custom_call" | custom-call | tf_op jit(solution)/shard_map/pallas_call | solution.py:138
  527.7 39.0 %all-gather.8.cloned.1.call-done = f32[512,1024]{1,0:T(8,128)} async-done(((f32[32,1024]{1,0:T(8,128)}), f32[512,1024]{1,0:T(8,128)}) %all-gather.8.cloned.1.call-update) | async-done | bytes 2097168 | tf_op jit(solution)/shard_map/all_gather | solution.py:234
  573.6 11.7 %cholesky.282 = f32[128,128]{1,0:T(8,128)S(1)} custom-call(f32[128,128]{1,0:T(8,128)S(1)} %fusion.173), custom_call_target="Cholesky" | custom-call | tf_op jit(solution)/shard_map/jit(cholesky)/cholesky | solution.py:49
  586.7 9.8 %custom-call.24 = f32[1,128,128]{1,2,0:T(8,128)S(1)} custom-call(f32[1,128,128]{2,1,0:T(8,128)S(1)} %get-tuple-element.13), custom_call_target="InvertDiagBlocksLowerTriangular" | custom-call | tf_op jit(solution)/shard_map/jit(_solve_triangular)/triangular_solve | solution.py:31
  598.2 11.9 %cholesky.293 = f32[128,128]{1,0:T(8,128)S(1)} custom-call(f32[128,128]{1,0:T(8,128)S(1)} %fusion.171), custom_call_target="Cholesky" | custom-call | tf_op jit(solution)/shard_map/jit(cholesky)/cholesky | solution.py:49
  611.4 9.8 %custom-call.25 = f32[1,128,128]{1,2,0:T(8,128)S(1)} custom-call(f32[1,128,128]{2,1,0:T(8,128)S(1)} %get-tuple-element.11), custom_call_target="InvertDiagBlocksLowerTriangular" | custom-call | tf_op jit(solution)/shard_map/jit(_solve_triangular)/triangular_solve | solution.py:31
  631.3 13.2 %cholesky.304 = f32[128,128]{1,0:T(8,128)} custom-call(f32[128,128]{1,0:T(8,128)} %fusion.169), custom_call_target="Cholesky" | custom-call | tf_op jit(solution)/shard_map/jit(cholesky)/cholesky | solution.py:49
  648.2 11.5 %custom-call.26 = f32[1,128,128]{1,2,0:T(8,128)} custom-call(f32[1,128,128]{2,1,0:T(8,128)} %get-tuple-element.9), custom_call_target="InvertDiagBlocksLowerTriangular" | custom-call | tf_op jit(solution)/shard_map/jit(_solve_triangular)/triangular_solve | solution.py:31
  672.0 11.7 %cholesky.315 = f32[128,128]{1,0:T(8,128)S(1)} custom-call(f32[128,128]{1,0:T(8,128)S(1)} %fusion.167), custom_call_target="Cholesky" | custom-call | tf_op jit(solution)/shard_map/jit(cholesky)/cholesky | solution.py:49
  685.0 9.8 %custom-call.27 = f32[1,128,128]{1,2,0:T(8,128)S(1)} custom-call(f32[1,128,128]{2,1,0:T(8,128)S(1)} %fusion.141), custom_call_target="InvertDiagBlocksLowerTriangular" | custom-call | tf_op jit(solution)/shard_map/jit(_solve_triangular)/triangular_solve | solution.py:31
  (336 shorter events, 167.3 us)
Async XLA Ops:
  7.2 82.8 %reduce-scatter.4.cloned.1.call-start = ((), (), s32[]{:S(2)}) async-start(), calls=%async_computation.4 | async-start | bytes 3342336
  28.0 112.1 %all-gather.4.cloned.1.call-start = ((), (), s32[]{:S(2)}) async-start(), calls=%async_computation.1 | async-start | bytes 6684672 | tf_op jit(solution)/shard_map/all_gather | solution.py:187
  92.1 255.1 %all-gather.6.cloned.1.call-start = ((), (), s32[]{:S(2)}) async-start(), calls=%async_computation.2 | async-start | bytes 2228224 | tf_op jit(solution)/shard_map/all_gather | solution.py:213
  161.6 61.9 %copy-start.15 = (f32[128,128]{0,1:T(8,128)}, f32[128,128]{0,1:T(8,128)S(1)}, u32[]{:S(2)}) copy-start(f32[128,128]{0,1:T(8,128)S(1)} %get-tuple-element.30) | copy-start | bytes 196612
  197.6 59.6 %copy-start.46 = (f32[256,256]{1,0:T(8,128)}, f32[256,256]{1,0:T(8,128)S(1)}, u32[]{:S(2)}) copy-start(f32[256,256]{1,0:T(8,128)S(1)} %select_maximum_fusion.8) | copy-start | bytes 786436
  212.5 44.7 %copy-start.26 = (f32[128,128]{0,1:T(8,128)}, f32[128,128]{0,1:T(8,128)S(1)}, u32[]{:S(2)}) copy-start(f32[128,128]{0,1:T(8,128)S(1)} %get-tuple-element.26) | copy-start | bytes 196612
  263.2 6.3 collective-permute-start
  271.5 40.6 %copy-start.39 = (f32[128,256]{1,0:T(8,128)S(1)}, f32[128,256]{1,0:T(8,128)}, u32[]{:S(2)}) copy-start(f32[128,256]{1,0:T(8,128)} %copy-done.37) | copy-start | bytes 393220
  271.5 40.6 %copy-start.41 = (f32[256,256]{1,0:T(8,128)S(1)}, f32[256,256]{1,0:T(8,128)}, u32[]{:S(2)}) copy-start(f32[256,256]{1,0:T(8,128)} %copy-done.40) | copy-start | bytes 786436
  271.5 40.6 %copy-start.43 = (f32[128,128]{1,0:T(8,128)S(1)}, f32[128,128]{1,0:T(8,128)}, u32[]{:S(2)}) copy-start(f32[128,128]{1,0:T(8,128)} %copy-done.42) | copy-start | bytes 196612
  271.5 40.6 %copy-start.48 = (f32[256,256]{1,0:T(8,128)S(1)}, f32[256,256]{1,0:T(8,128)}, u32[]{:S(2)}) copy-start(f32[256,256]{1,0:T(8,128)} %copy-done.46) | copy-start | bytes 786436
  271.5 40.6 %copy-start.51 = (f32[128,128]{1,0:T(8,128)S(1)}, f32[128,128]{1,0:T(8,128)}, u32[]{:S(2)}) copy-start(f32[128,128]{1,0:T(8,128)} %copy-done.49) | copy-start | bytes 196612
  303.2 4.1 collective-permute-start.1
  308.0 258.6 %all-gather.8.cloned.1.call-start = ((), (), s32[]{:S(2)}) async-start(), calls=%async_computation.3 | async-start | bytes 2228224 | tf_op jit(solution)/shard_map/all_gather | solution.py:234
  319.4 145.0 %collective-permute-start.2 = (f32[512,512]{1,0:T(8,128)S(1)}, f32[512,512]{1,0:T(8,128)}, u32[]{:S(2)}, u32[]{:S(2)}) collective-permute-start(f32[512,512]{1,0:T(8,128)S(1)} %copy-done.2), channel_id=1, source_target_pairs={{0,16},{16,0},{32,48},{48,32},{64,80},{80,64},{96,112},{112,96},{1... | collective-permute-start | bytes 3145736 | tf_op jit(solution)/shard_map/ppermute | solution.py:16
  367.6 63.0 %copy-start.13 = (f32[128,128]{0,1:T(8,128)}, f32[128,128]{0,1:T(8,128)S(1)}, u32[]{:S(2)}) copy-start(f32[128,128]{0,1:T(8,128)S(1)} %get-tuple-element.22) | copy-start | bytes 196612
  392.5 38.5 %copy-start.17 = (f32[128,128]{0,1:T(8,128)}, f32[128,128]{0,1:T(8,128)S(1)}, u32[]{:S(2)}) copy-start(f32[128,128]{0,1:T(8,128)S(1)} %get-tuple-element.20) | copy-start | bytes 196612
  405.9 49.7 %copy-start.22 = (f32[256,256]{1,0:T(8,128)S(1)}, f32[256,256]{1,0:T(8,128)}, u32[]{:S(2)}) copy-start(f32[256,256]{1,0:T(8,128)} %fusion.85) | copy-start | bytes 786436
  419.3 39.9 %copy-start.24 = (f32[128,128]{0,1:T(8,128)}, f32[128,128]{0,1:T(8,128)S(1)}, u32[]{:S(2)}) copy-start(f32[128,128]{0,1:T(8,128)S(1)} %get-tuple-element.18) | copy-start | bytes 196612
  470.1 11.8 %collective-permute-start.4 = (f32[96,512]{1,0:T(8,128)S(1)}, f32[96,512]{1,0:T(8,128)S(1)}, u32[]{:S(2)}, u32[]{:S(2)}) collective-permute-start(f32[96,512]{1,0:T(8,128)S(1)} %fusion.243), channel_id=1, source_target_pairs={{0,48},{16,32},{32,16},{48,0},{64,112},{80,96},{96,80},{112,64},{1... | collective-permute-start | bytes 589832 | tf_op jit(solution)/shard_map/ppermute | solution.py:16
  472.7 10.3 %collective-permute-start.3 = (f32[96,512]{1,0:T(8,128)S(1)}, f32[96,512]{1,0:T(8,128)S(1)}, u32[]{:S(2)}, u32[]{:S(2)}) collective-permute-start(f32[96,512]{1,0:T(8,128)S(1)} %fusion.243), channel_id=1, source_target_pairs={{0,32},{16,48},{32,0},{48,16},{64,96},{80,112},{96,64},{112,80},{1... | collective-permute-start | bytes 589832 | tf_op jit(solution)/shard_map/ppermute | solution.py:16
  474.0 46.0 %copy-start.5 = (f32[256,128]{0,1:T(8,128)S(1)}, f32[256,128]{0,1:T(8,128)}, u32[]{:S(2)}) copy-start(f32[256,128]{0,1:T(8,128)} %copy-done.4) | copy-start | bytes 393220
  474.0 46.0 %copy-start.14 = (f32[128,128]{0,1:T(8,128)S(1)}, f32[128,128]{0,1:T(8,128)}, u32[]{:S(2)}) copy-start(f32[128,128]{0,1:T(8,128)} %copy-done.13) | copy-start | bytes 196612
  474.0 46.0 %copy-start.18 = (f32[128,128]{0,1:T(8,128)S(1)}, f32[128,128]{0,1:T(8,128)}, u32[]{:S(2)}) copy-start(f32[128,128]{0,1:T(8,128)} %copy-done.17) | copy-start | bytes 196612
  474.0 46.0 %copy-start.25 = (f32[128,128]{0,1:T(8,128)S(1)}, f32[128,128]{0,1:T(8,128)}, u32[]{:S(2)}) copy-start(f32[128,128]{0,1:T(8,128)} %copy-done.24) | copy-start | bytes 196612
  474.0 46.0 %copy-start.29 = (f32[128,128]{0,1:T(8,128)S(1)}, f32[128,128]{0,1:T(8,128)}, u32[]{:S(2)}) copy-start(f32[128,128]{0,1:T(8,128)} %copy-done.28) | copy-start | bytes 196612
  474.0 46.0 %copy-start.44 = (f32[128,128]{0,1:T(8,128)S(1)}, f32[128,128]{0,1:T(8,128)}, u32[]{:S(2)}) copy-start(f32[128,128]{0,1:T(8,128)} %get-tuple-element.16) | copy-start | bytes 196612
  474.8 51.6 %copy-start.10 = (f32[96,512]{1,0:T(8,128)S(1)}, f32[96,512]{1,0:T(8,128)}, u32[]{:S(2)}) copy-start(f32[96,512]{1,0:T(8,128)} %copy-done.8) | copy-start | bytes 589828
  515.5 4.5 collective-permute-start.5
  521.0 4.7 collective-permute-start.6
  573.5 49.7 %copy-start.3 = (f32[512,512]{0,1:T(8,128)}, f32[512,512]{0,1:T(8,128)S(1)}, u32[]{:S(2)}) copy-start(f32[512,512]{0,1:T(8,128)S(1)} %convolution_add_fusion) | copy-start | bytes 3145732
  623.3 74.5 %copy-start = (f32[512,1024]{1,0:T(8,128)S(1)}, f32[512,1024]{1,0:T(8,128)}, u32[]{:S(2)}) copy-start(f32[512,1024]{1,0:T(8,128)} %all-gather.8.cloned.1.call-done) | copy-start | bytes 6291460
  (34 other events, 510.8 us)
Sparse Core Ops, SparseCore 0:
  28.2 61.7 reduce-scatter.3
  92.2 47.9 all-gather.3
  308.1 39.0 all-gather.5
  526.5 40.1 all-gather.7
